TPU v7x, 512 devices: a whole 4x4x16 slice. The times are simulated.
512 devices in a mesh: team: 32 (over x, y, core), rep: 16 (over z).
Axes of the slice: x: 4, y: 4, z: 16, core: 2. Of those that a mesh axis runs over, the one named last changes fastest.
Arguments:
- features: bfloat16 [16384, 1024], P(('team', 'rep')), may hold values from -6 to 6
- degree: int32 [16384], P(('team', 'rep')), may hold values from 4 to 16
- blocks: bfloat16 [128, 16, 8, 128, 128], P('team', 'rep'), may hold values from -3 to 3
- block_cols: int32 [128, 16, 8], P('team', 'rep'), may hold values from 0 to 7, each once within a row
- block_count: int32 [128, 16], P('team', 'rep'), may hold values from 1 to 8, as said below
Outputs:
- hop1: bfloat16 [16384, 1024], P(('team', 'rep'))
- hop2: bfloat16 [16384, 1024], P(('team', 'rep'))
- hop3: bfloat16 [16384, 1024], P(('team', 'rep'))
Inputs may be any that keep to these rules, and one draw needn't show every extreme that they name: Each of the 8 entries of a row of block_cols names a different column block; only the first block_count entries are used. `block_count`: some block row of some replica uses all 8 of its blocks.
All inputs are finite; a program needn't handle non-finite values.
Results may differ from a plain program's by a relative error of at most 0.04.
Values may be sent and summed in bfloat16 or wider, within the bound.
No kernel may reach another device: no remote copies, remote signals or barrier semaphores. Data moves between devices by JAX's collectives and lax.ppermute only.
A program may use at most 64 MiB of HBM per device.

v0:
```python
import jax
import jax.numpy as jnp
from jax import lax
from jax.sharding import PartitionSpec as P

HOPS = 3


def on_device(features, degree, blocks, block_cols, block_count):
    width = features.shape[1]
    block_size = blocks.shape[-1]
    row_blocks = blocks.shape[0]
    col_blocks = blocks.shape[2]
    panel = row_blocks * block_size
    tiles = blocks[:, 0]
    columns_used = block_cols[:, 0]
    counts_used = block_count[:, 0]
    scale = lax.rsqrt(degree.astype(jnp.float32))[:, None]
    current = features
    results = []
    for hop in range(HOPS):
        sent = (scale * current.astype(jnp.float32)).astype(jnp.bfloat16)
        whole = lax.all_gather(sent, "team", axis=0, tiled=True)
        pieces = whole.reshape(col_blocks, block_size, width)

        def row_block(which, accum):

            def add_slot(slot, inner):
                tile = tiles[which, slot]
                piece = pieces[columns_used[which, slot]]
                return inner + jnp.dot(tile, piece, preferred_element_type=jnp.float32)

            block_rows = lax.fori_loop(
                0, counts_used[which], add_slot, jnp.zeros((block_size, width), jnp.float32)
            )
            return lax.dynamic_update_slice_in_dim(accum, block_rows, which * block_size, 0)

        partial_value = lax.fori_loop(
            0, row_blocks, row_block, jnp.zeros((panel, width), jnp.float32)
        )
        total = lax.psum_scatter(
            partial_value.astype(jnp.bfloat16), "rep", scatter_dimension=0, tiled=True
        ).astype(jnp.float32)
        current = (scale * (total + sent.astype(jnp.float32))).astype(jnp.bfloat16)
        results.append(current)
    return (results[0], results[1], results[2])


def solution(mesh):
    in_specs = (
        P(("team", "rep"), None),
        P(("team", "rep")),
        P("team", "rep", None, None, None),
        P("team", "rep", None),
        P("team", "rep"),
    )
    out_specs = (P(("team", "rep"), None), P(("team", "rep"), None), P(("team", "rep"), None))
    return jax.shard_map(
        on_device, mesh=mesh, in_specs=in_specs, out_specs=out_specs, check_vma=False
    )
```

profile of v0, /device:TPU:1, one launch (start us, length us, event | category | flops | bytes accessed | tf_op | source)
XLA Modules:
  0.0 816.9 jit_solution(12673961398546274017)
XLA Ops:
  9.5 67.1 %all-gather.4.cloned.1.call-done = bf16[1024,1024]{1,0:T(8,128)(2,1)} async-done(((bf16[32,1024]{1,0:T(8,128)(2,1)}), bf16[1024,1024]{1,0:T(8,128)(2,1)}) %all-gather.4.cloned.1.call-update) | async-done | bytes 2097168 | tf_op jit(solution)/shard_map/all_gather | solution.py:23
  76.7 74.1 %while.112 = (s32[]{:T(128)}, bf16[512,1024]{1,0:T(8,128)(2,1)S(1)}, s32[4]{0:T(128)}, bf16[4,8,128,128]{3,2,1,0:T(8,128)(2,1)}, s32[4,8]{1,0:T(4,128)}, /*index...) while((s32[]{:T(128)}, bf16[512,1024]{1,0:T(8,128)(2,1)S(1)}, ...), condition=%wide.region_3.0_spmd, body=%wide.region_0.0_spmd.sunk | while | flops 33685512 | bytes 2917356 | solution.py:38
  78.1 26.0 %while.117 = (s32[]{:T(128)}, f32[128,1024]{1,0:T(8,128)S(1)}, s32[]{:T(128)}, bf16[4,8,128,128]{3,2,1,0:T(8,128)(2,1)}, s32[]{:T(128)}, /*index=5*/s32[4,8]{1,0...) while((s32[]{:T(128)}, f32[128,1024]{1,0:T(8,128)S(1)}, s32[]{:T(128)}, ...), condition=%wide.region_2.0_spmd, body=%wide.region_1.0_spmd.sunk | while | flops 33685512 | bytes 1344197 | solution.py:33
  105.5 15.9 %while.117 = (s32[]{:T(128)}, f32[128,1024]{1,0:T(8,128)S(1)}, s32[]{:T(128)}, bf16[4,8,128,128]{3,2,1,0:T(8,128)(2,1)}, s32[]{:T(128)}, /*index=5*/s32[4,8]{1,0...) while((s32[]{:T(128)}, f32[128,1024]{1,0:T(8,128)S(1)}, s32[]{:T(128)}, ...), condition=%wide.region_2.0_spmd, body=%wide.region_1.0_spmd.sunk | while | flops 33685512 | bytes 1344197 | solution.py:33
  122.7 5.7 while.117
  129.8 20.9 %while.117 = (s32[]{:T(128)}, f32[128,1024]{1,0:T(8,128)S(1)}, s32[]{:T(128)}, bf16[4,8,128,128]{3,2,1,0:T(8,128)(2,1)}, s32[]{:T(128)}, /*index=5*/s32[4,8]{1,0...) while((s32[]{:T(128)}, f32[128,1024]{1,0:T(8,128)S(1)}, s32[]{:T(128)}, ...), condition=%wide.region_2.0_spmd, body=%wide.region_1.0_spmd.sunk | while | flops 33685512 | bytes 1344197 | solution.py:33
  151.9 136.4 %reduce-scatter.4.cloned.1.call-done = bf16[32,1024]{1,0:T(8,128)(2,1)} async-done(((bf16[512,1024]{1,0:T(8,128)(2,1)}), bf16[32,1024]{1,0:T(8,128)(2,1)}) %reduce-scatter.4.cloned.1.call-update) | async-done | bytes 65552 | tf_op jit(solution)/shard_map/reduce_scatter | solution.py:41
  288.2 1.6 multiply_convert_fusion.3
  289.9 69.7 %all-gather.6.cloned.1.call-done = bf16[1024,1024]{1,0:T(8,128)(2,1)} async-done(((bf16[32,1024]{1,0:T(8,128)(2,1)}), bf16[1024,1024]{1,0:T(8,128)(2,1)}) %all-gather.6.cloned.1.call-update) | async-done | bytes 2097168 | tf_op jit(solution)/shard_map/all_gather | solution.py:23
  359.8 62.5 %while.114 = (s32[]{:T(128)}, bf16[512,1024]{1,0:T(8,128)(2,1)S(1)}, s32[4]{0:T(128)S(1)}, bf16[4,8,128,128]{3,2,1,0:T(8,128)(2,1)}, s32[4,8]{1,0:T(4,128)S(1)},...) while((s32[]{:T(128)}, bf16[512,1024]{1,0:T(8,128)(2,1)S(1)}, ...), condition=%wide.region_8.0_spmd, body=%wide.region_5.0_spmd.sunk | while | flops 33685512 | bytes 2917364 | solution.py:38
  360.5 22.6 %while.118 = (s32[]{:T(128)}, f32[128,1024]{1,0:T(8,128)S(1)}, s32[]{:T(128)}, bf16[4,8,128,128]{3,2,1,0:T(8,128)(2,1)}, s32[]{:T(128)}, /*index=5*/s32[4,8]{1,0...) while((s32[]{:T(128)}, f32[128,1024]{1,0:T(8,128)S(1)}, s32[]{:T(128)}, ...), condition=%wide.region_7.0_spmd, body=%wide.region_6.0_spmd.sunk | while | flops 33685512 | bytes 1344197 | solution.py:33
  383.8 13.8 %while.118 = (s32[]{:T(128)}, f32[128,1024]{1,0:T(8,128)S(1)}, s32[]{:T(128)}, bf16[4,8,128,128]{3,2,1,0:T(8,128)(2,1)}, s32[]{:T(128)}, /*index=5*/s32[4,8]{1,0...) while((s32[]{:T(128)}, f32[128,1024]{1,0:T(8,128)S(1)}, s32[]{:T(128)}, ...), condition=%wide.region_7.0_spmd, body=%wide.region_6.0_spmd.sunk | while | flops 33685512 | bytes 1344197 | solution.py:33
  398.3 5.0 while.118
  404.1 18.2 %while.118 = (s32[]{:T(128)}, f32[128,1024]{1,0:T(8,128)S(1)}, s32[]{:T(128)}, bf16[4,8,128,128]{3,2,1,0:T(8,128)(2,1)}, s32[]{:T(128)}, /*index=5*/s32[4,8]{1,0...) while((s32[]{:T(128)}, f32[128,1024]{1,0:T(8,128)S(1)}, s32[]{:T(128)}, ...), condition=%wide.region_7.0_spmd, body=%wide.region_6.0_spmd.sunk | while | flops 33685512 | bytes 1344197 | solution.py:33
  423.4 125.1 %reduce-scatter.6.cloned.1.call-done = bf16[32,1024]{1,0:T(8,128)(2,1)} async-done(((bf16[512,1024]{1,0:T(8,128)(2,1)}), bf16[32,1024]{1,0:T(8,128)(2,1)}) %reduce-scatter.6.cloned.1.call-update) | async-done | bytes 65552 | tf_op jit(solution)/shard_map/reduce_scatter | solution.py:41
  548.5 1.6 multiply_convert_fusion.1
  550.2 69.4 %all-gather.8.cloned.1.call-done = bf16[1024,1024]{1,0:T(8,128)(2,1)} async-done(((bf16[32,1024]{1,0:T(8,128)(2,1)}), bf16[1024,1024]{1,0:T(8,128)(2,1)}) %all-gather.8.cloned.1.call-update) | async-done | bytes 2097168 | tf_op jit(solution)/shard_map/all_gather | solution.py:23
  619.7 62.5 %while.116 = (s32[]{:T(128)}, bf16[512,1024]{1,0:T(8,128)(2,1)S(1)}, s32[4]{0:T(128)S(1)}, bf16[4,8,128,128]{3,2,1,0:T(8,128)(2,1)}, s32[4,8]{1,0:T(4,128)S(1)},...) while((s32[]{:T(128)}, bf16[512,1024]{1,0:T(8,128)(2,1)S(1)}, ...), condition=%wide.region_13.0_spmd, body=%wide.region_10.0_spmd.sunk | while | flops 33685512 | bytes 2917356 | solution.py:38
  620.4 22.6 %while.119 = (s32[]{:T(128)}, f32[128,1024]{1,0:T(8,128)S(1)}, s32[]{:T(128)}, bf16[4,8,128,128]{3,2,1,0:T(8,128)(2,1)}, s32[]{:T(128)}, /*index=5*/s32[4,8]{1,0...) while((s32[]{:T(128)}, f32[128,1024]{1,0:T(8,128)S(1)}, s32[]{:T(128)}, ...), condition=%wide.region_12.0_spmd, body=%wide.region_11.0_spmd.sunk | while | flops 33685512 | bytes 1344197 | solution.py:33
  643.7 13.8 %while.119 = (s32[]{:T(128)}, f32[128,1024]{1,0:T(8,128)S(1)}, s32[]{:T(128)}, bf16[4,8,128,128]{3,2,1,0:T(8,128)(2,1)}, s32[]{:T(128)}, /*index=5*/s32[4,8]{1,0...) while((s32[]{:T(128)}, f32[128,1024]{1,0:T(8,128)S(1)}, s32[]{:T(128)}, ...), condition=%wide.region_12.0_spmd, body=%wide.region_11.0_spmd.sunk | while | flops 33685512 | bytes 1344197 | solution.py:33
  658.3 5.0 while.119
  664.0 18.2 %while.119 = (s32[]{:T(128)}, f32[128,1024]{1,0:T(8,128)S(1)}, s32[]{:T(128)}, bf16[4,8,128,128]{3,2,1,0:T(8,128)(2,1)}, s32[]{:T(128)}, /*index=5*/s32[4,8]{1,0...) while((s32[]{:T(128)}, f32[128,1024]{1,0:T(8,128)S(1)}, s32[]{:T(128)}, ...), condition=%wide.region_12.0_spmd, body=%wide.region_11.0_spmd.sunk | while | flops 33685512 | bytes 1344197 | solution.py:33
  683.3 125.2 %reduce-scatter.8.cloned.1.call-done = bf16[32,1024]{1,0:T(8,128)(2,1)} async-done(((bf16[512,1024]{1,0:T(8,128)(2,1)}), bf16[32,1024]{1,0:T(8,128)(2,1)}) %reduce-scatter.8.cloned.1.call-update) | async-done | bytes 65552 | tf_op jit(solution)/shard_map/reduce_scatter | solution.py:41
  808.5 1.6 multiply_convert_fusion
  (147 shorter events, 96.6 us)
Async XLA Ops:
  7.2 69.4 %all-gather.4.cloned.1.call-start = ((), (), s32[]{:S(2)}) async-start(), calls=%async_computation.3 | async-start | bytes 2162688 | tf_op jit(solution)/shard_map/all_gather | solution.py:23
  9.4 278.8 %reduce-scatter.4.cloned.1.call-start = ((), (), s32[]{:S(2)}) async-start(), calls=%async_computation.4 | async-start | bytes 1114112 | tf_op jit(solution)/shard_map/reduce_scatter | solution.py:41
  76.7 211.5 %copy-start.5 = (bf16[32,1024]{1,0:T(8,128)(2,1)S(1)}, bf16[32,1024]{1,0:T(8,128)(2,1)}, u32[]{:S(2)}) copy-start(bf16[32,1024]{1,0:T(8,128)(2,1)} %param.17) | copy-start | bytes 196612
  150.8 1.0 copy-start.1
  150.8 208.9 %copy-start.3 = (s32[4,8]{1,0:T(4,128)S(1)}, s32[4,8]{1,0:T(4,128)}, u32[]{:S(2)}) copy-start(s32[4,8]{1,0:T(4,128)} %get-tuple-element.1213) | copy-start | bytes 388
  150.8 208.9 %copy-start.7 = (s32[4]{0:T(128)S(1)}, s32[4]{0:T(128)}, u32[]{:S(2)}) copy-start(s32[4]{0:T(128)} %get-tuple-element.1240) | copy-start | bytes 52
  151.8 207.8 %all-gather.6.cloned.1.call-start = ((), (), s32[]{:S(2)}) async-start(), calls=%async_computation.5 | async-start | bytes 2162688 | tf_op jit(solution)/shard_map/all_gather | solution.py:23
  289.8 258.7 %copy-start.6 = (bf16[32,1024]{1,0:T(8,128)(2,1)}, bf16[32,1024]{1,0:T(8,128)(2,1)S(1)}, u32[]{:S(2)}) copy-start(bf16[32,1024]{1,0:T(8,128)(2,1)S(1)} %get-tuple-element.678) | copy-start | bytes 196612
  289.8 258.7 %reduce-scatter.6.cloned.1.call-start = ((), (), s32[]{:S(2)}) async-start(), calls=%async_computation.6 | async-start | bytes 1114112 | tf_op jit(solution)/shard_map/reduce_scatter | solution.py:41
  422.3 1.0 copy-start.2
  423.4 196.3 %all-gather.8.cloned.1.call-start = ((), (), s32[]{:S(2)}) async-start(), calls=%async_computation.7 | async-start | bytes 2162688 | tf_op jit(solution)/shard_map/all_gather | solution.py:23
  550.1 258.4 %copy-start.4 = (bf16[32,1024]{1,0:T(8,128)(2,1)}, bf16[32,1024]{1,0:T(8,128)(2,1)S(1)}, u32[]{:S(2)}) copy-start(bf16[32,1024]{1,0:T(8,128)(2,1)S(1)} %get-tuple-element.676) | copy-start | bytes 196612
  550.1 258.4 %reduce-scatter.8.cloned.1.call-start = ((), (), s32[]{:S(2)}) async-start(), calls=%async_computation.8 | async-start | bytes 1114112 | tf_op jit(solution)/shard_map/reduce_scatter | solution.py:41
  682.3 1.0 copy-start
Sparse Core Ops, SparseCore 0:
  11.7 64.8 all-gather.3
  152.0 136.2 reduce-scatter.3
  292.4 67.1 all-gather.5
  423.5 125.0 reduce-scatter.5
  552.1 67.4 all-gather.7
  683.4 125.0 reduce-scatter.7
where the time goes:
time: 832 us; the launch traced here: 817 us
  waiting for transfers between devices  593 us (71%)
  loops' own time  108 us (13%)
  matrix products  47.1 us (6%)
  local copies, waits for them, and re-layouts  47 us (6%)
  between operations  14.2 us (2%)
    reduce_scatter x3, waiting for transfers between devices, on_device(): lax.psum_scatter(partial_value.astype(jnp.bfloat16), 'rep', scatter_dimen...  387 us
    all_gather x3, waiting for transfers between devices, on_device(): whole = lax.all_gather(sent, 'team', axis=0, tiled=True)  206 us
    another operation x12, loops' own time, row_block(): lax.fori_loop(0, counts_used[which], add_slot, jnp.zeros((block_size, wid...  108 us
    dot_general x39, matrix products, add_slot(): return inner + jnp.dot(tile, piece, preferred_element_type=jnp.float32)  47.1 us
    dynamic_slice x39, local copies, waits for them, and re-layouts, add_slot(): piece = pieces[columns_used[which, slot]]  32.8 us
  transfers between devices with their start and end apart: 6, of which 6 were waited for; matrix products, arithmetic and copies ran while one was open for 0% of the time, Pallas kernels for 0%

commit v1 on v0

v1 whole, which is shorter than its diff:
```python
import jax
import jax.numpy as jnp
from jax import lax
from jax.experimental import pallas as pl
from jax.experimental.pallas import tpu as pltpu
from jax.sharding import Mesh, PartitionSpec as P

HOPS = 3
PLANE = ("x", "y")
FAR = ("zh", "zm")
POOL = ("c", "z0")
SIZES = {"x": 4, "y": 4, "c": 2, "zh": 4, "zm": 2, "z0": 2}
VMEM = pl.BlockSpec(memory_space=pltpu.VMEM)
SMEM = pl.BlockSpec(memory_space=pltpu.SMEM)


def exchange(x, axes):
    return lax.all_to_all(x, axes, 0, 0, tiled=True)


def swap(x, axis):
    return lax.ppermute(x, axis, [(0, 1), (1, 0)])


def dense_kernel(cols, counts, blocks, out):
    out[...] = jnp.zeros_like(out)
    row_blocks, slots, size, _ = blocks.shape
    for g in range(row_blocks):
        for t in range(slots):

            @pl.when(t < counts[g])
            def _():
                at = pl.multiple_of(cols[g, t] * size, size)
                out[g * size : (g + 1) * size, pl.ds(at, size)] = blocks[g, t]


def build_dense(blocks, cols, counts):
    g, t, size, _ = blocks.shape
    return pl.pallas_call(
        dense_kernel,
        out_shape=jax.ShapeDtypeStruct((g * size, t * size), blocks.dtype),
        in_specs=[SMEM, SMEM, VMEM],
        out_specs=VMEM,
        name="dense_panel",
    )(cols, counts, blocks)


def first_kernel(got, sent, copies, scale):
    pool, rows, width = got.shape
    wide = width - 128
    for q in range(pool):
        s = lax.rsqrt(got[q, :, wide:].astype(jnp.float32))
        s = jnp.concatenate([s] * (wide // 128), axis=1)
        scale[q * rows : (q + 1) * rows, :] = s
        value = (s * got[q, :, :wide].astype(jnp.float32)).astype(jnp.bfloat16)
        sent[q * rows : (q + 1) * rows, :] = value
        for k in range(copies.shape[0]):
            copies[k, q * rows : (q + 1) * rows, :] = value


def first(got, n_copies):
    pool, rows, width = got.shape
    wide = width - 128
    shape = (pool * rows, wide)
    return pl.pallas_call(
        first_kernel,
        out_shape=(
            jax.ShapeDtypeStruct(shape, jnp.bfloat16),
            jax.ShapeDtypeStruct((n_copies,) + shape, jnp.bfloat16),
            jax.ShapeDtypeStruct(shape, jnp.float32),
        ),
        in_specs=[VMEM],
        out_specs=(VMEM, VMEM, VMEM),
        name="first_scale",
    )(got)


def product_kernel(place, whole, a00, a01, a10, a11, out, columns):
    plane, pair, rows, _ = whole.shape
    far = out.shape[0]
    for j in range(plane):
        for z in range(pair):
            columns[z, j * rows : (j + 1) * rows, :] = whole[j, z]
    core, level = place[0], place[1]
    mine = columns[level]
    other = columns[1 - level]
    for near, (ours, theirs) in enumerate(((a00, a01), (a10, a11))):
        value = jnp.dot(ours[...], mine, preferred_element_type=jnp.float32)
        value += jnp.dot(theirs[...], other, preferred_element_type=jnp.float32)
        value = value.astype(jnp.bfloat16).reshape(far, pair, rows // 2, -1)
        target = core if near == 0 else 1 - core
        for z in range(pair):
            out[:, z, target] = value[:, z]


def product(place, whole, panels, far):
    plane, pair, rows, width = whole.shape
    return pl.pallas_call(
        product_kernel,
        out_shape=jax.ShapeDtypeStruct((far, pair, 2, rows // 2, width), jnp.bfloat16),
        in_specs=[SMEM] + [VMEM] * 5,
        out_specs=VMEM,
        scratch_shapes=[pltpu.VMEM((pair, plane * rows, width), jnp.bfloat16)],
        compiler_params=pltpu.CompilerParams(vmem_limit_bytes=40 << 20),
        name="panel_product",
    )(place, whole, *panels)


def update_kernel(parts, sent, scale, hop, new_sent, copies):
    total = parts[0].astype(jnp.float32)
    for k in range(1, parts.shape[0]):
        total += parts[k].astype(jnp.float32)
    s = scale[...]
    value = (s * (total + sent[...].astype(jnp.float32))).astype(jnp.bfloat16)
    hop[...] = value
    value = (s * value.astype(jnp.float32)).astype(jnp.bfloat16)
    new_sent[...] = value
    for k in range(copies.shape[0]):
        copies[k] = value


def update(parts, sent, scale, n_copies):
    shape = sent.shape
    return pl.pallas_call(
        update_kernel,
        out_shape=(
            jax.ShapeDtypeStruct(shape, jnp.bfloat16),
            jax.ShapeDtypeStruct(shape, jnp.bfloat16),
            jax.ShapeDtypeStruct((n_copies,) + shape, jnp.bfloat16),
        ),
        in_specs=[VMEM] * 3,
        out_specs=(VMEM,) * 3,
        name="update",
    )(parts, sent, scale)


def last_kernel(parts, sent, scale, hop):
    total = parts[0].astype(jnp.float32)
    for k in range(1, parts.shape[0]):
        total += parts[k].astype(jnp.float32)
    value = scale[...] * (total + sent[...].astype(jnp.float32))
    hop[...] = value.astype(jnp.bfloat16)


def last(parts, sent, scale):
    return pl.pallas_call(
        last_kernel,
        out_shape=jax.ShapeDtypeStruct(sent.shape, jnp.bfloat16),
        in_specs=[VMEM] * 3,
        out_specs=VMEM,
        name="last_update",
    )(parts, sent, scale)


def on_device(features, degree, blocks, block_cols, block_count):
    rows, full = features.shape
    pool = SIZES["c"] * SIZES["z0"]
    far = SIZES["zh"] * SIZES["zm"]
    plane = SIZES["x"] * SIZES["y"]
    width = full // pool
    place = jnp.stack([lax.axis_index("c"), lax.axis_index("z0")]).astype(jnp.int32)

    slices = features.reshape(rows, pool, width).transpose(1, 0, 2)
    counts = jnp.broadcast_to(degree.astype(jnp.bfloat16)[None, :, None], (pool, rows, 128))
    got = exchange(jnp.concatenate([slices, counts], axis=2), ("z0", "c"))
    sent, copies, scale = first(got, plane)

    a00 = build_dense(blocks[:, 0], block_cols[:, 0], block_count[:, 0])
    a01 = swap(a00, "z0")
    a10 = swap(a00, "c")
    a11 = swap(a01, "c")
    panels = (a00, a01, a10, a11)

    hops = []
    for hop in range(HOPS):
        whole = exchange(copies, PLANE).reshape(plane, 2, 2 * rows, width)
        partial_value = product(place, whole, panels, far)
        parts = exchange(partial_value.reshape(far, pool * rows, width), FAR)
        if hop < HOPS - 1:
            value, sent, copies = update(parts, sent, scale, plane)
        else:
            value = last(parts, sent, scale)
        hops.append(value.reshape(pool, rows, width))
    back = exchange(jnp.stack(hops, axis=1), ("z0", "c"))
    return tuple(
        back[:, k].transpose(1, 0, 2).reshape(rows, full) for k in range(HOPS)
    )


def solution(mesh):
    axes = tuple(SIZES)
    fine = Mesh(mesh.devices.reshape(tuple(SIZES.values())), axes)
    in_specs = (
        P(axes, None),
        P(axes),
        P(axes[:3], axes[3:], None, None, None),
        P(axes[:3], axes[3:], None),
        P(axes[:3], axes[3:]),
    )
    out_specs = (P(axes, None),) * 3
    return jax.shard_map(
        on_device, mesh=fine, in_specs=in_specs, out_specs=out_specs, check_vma=False
    )
```

time: 832 us -> 240 us (0.29); the launches traced: 817 us -> 239 us
  waiting for transfers between devices: 593 us -> 25.1 us
  blocking collectives: 0 us -> 161 us
  loops' own time: 108 us -> 0 us
  matrix products: 47.1 us -> 0 us
  local copies, waits for them, and re-layouts: 47 us -> 2.66 us
  starting transfers between devices: 0.24 us -> 29.1 us
  Pallas kernels: 0 us -> 19.1 us
  between operations: 14.2 us -> 0.78 us
    reduce_scatter x3 -> x0, waiting for transfers between devices: 387 us -> none  [on_device(): lax.psum_scatter(partial_value.astype(jnp.bfloat16), 'rep', scatter_dimen...]
    all_gather x3 -> x0, waiting for transfers between devices: 206 us -> none  [on_device(): whole = lax.all_gather(sent, 'team', axis=0, tiled=True)]
    all_to_all x0 -> x6, blocking collectives: none -> 161 us  [exchange(): return lax.all_to_all(x, axes, 0, 0, tiled=True)]
    another operation x15 -> x0, loops' own time: 108 us -> none  [the longest x12 108 us: row_block(): lax.fori_loop(0, counts_used[which], add_slot, jnp.zeros((block_size, wid...]
    dot_general x39 -> x0, matrix products: 47.1 us -> none  [add_slot(): return inner + jnp.dot(tile, piece, preferred_element_type=jnp.float32)]
    dynamic_slice x51 -> x0, local copies, waits for them, and re-layouts: 42.8 us -> none  [the longest x39 32.8 us: add_slot(): piece = pieces[columns_used[which, slot]]]
    pallas_call x0 -> x8, Pallas kernels: none -> 19.1 us  [the longest x3 8.02 us: product(): pl.pallas_call(product_kernel, out_shape=jax.ShapeDtypeStruct((far, pair,...]
    all_to_all x0 -> x2, waiting for transfers between devices: none -> 17 us  [exchange(): return lax.all_to_all(x, axes, 0, 0, tiled=True)]
  transfers between devices with their start and end apart: 6 -> 5, of which waited for: 6 -> 2; matrix products, arithmetic and copies ran while one was open for 0% -> 0% of each run, Pallas kernels for 0% -> 1%
where the time goes in v1:
time: 240 us; the launch traced here: 239 us
  blocking collectives  161 us (67%)
  starting transfers between devices  29.1 us (12%)
  waiting for transfers between devices  25.1 us (10%)
  Pallas kernels  19.1 us (8%)
  local copies, waits for them, and re-layouts  2.66 us (1%)
    all_to_all x6, blocking collectives, exchange(): return lax.all_to_all(x, axes, 0, 0, tiled=True)  161 us
    all_to_all x2, waiting for transfers between devices, exchange(): return lax.all_to_all(x, axes, 0, 0, tiled=True)  17 us
    all_to_all x2, starting transfers between devices, exchange(): return lax.all_to_all(x, axes, 0, 0, tiled=True)  14.7 us
    ppermute x3, starting transfers between devices, swap(): return lax.ppermute(x, axis, [(0, 1), (1, 0)])  14.4 us
    ppermute x3, waiting for transfers between devices, swap(): return lax.ppermute(x, axis, [(0, 1), (1, 0)])  8.13 us
    pallas_call x3, Pallas kernels, product(): pl.pallas_call(product_kernel, out_shape=jax.ShapeDtypeStruct((far, pair,...  8.02 us
  transfers between devices with their start and end apart: 5, of which 2 were waited for; matrix products, arithmetic and copies ran while one was open for 0% of the time, Pallas kernels for 1%

profile of v1, /device:TPU:1, one launch (start us, length us, event | category | flops | bytes accessed | tf_op | source)
XLA Modules:
  0.0 239.0 jit_solution(2409724159280810864)
XLA Ops:
  0.7 2.7 %dense_panel.1.a00 = bf16[512,1024]{1,0:T(8,128)(2,1)} custom-call(s32[4,8]{1,0:T(4,128)} %bitcast.59, s32[4]{0:T(128)} %bitcast.60, bf16[4,8,128,128]{3,2,1,0:T(8,128)(2,1)} %bitcast.50), custom_call_target="tpu_custom_call" | custom-call | tf_op jit(solution)/shard_map/dense_panel/pallas_call | solution.py:39
  3.3 4.3 %collective-permute-start = (bf16[512,1024]{1,0:T(8,128)(2,1)}, bf16[512,1024]{1,0:T(8,128)(2,1)S(1)}, u32[]{:S(2)}, u32[]{:S(2)}) collective-permute-start(bf16[512,1024]{1,0:T(8,128)(2,1)} %dense_panel.1.a00), channel_id=1, source_target_pairs={{0,1},{1,0},{2,3},{3,2},{4,5},{5,4},{6,7},{7,6},{8,9},{9,8},{10,11... | collective-permute-start | bytes 3145736 | tf_op jit(solution)/shard_map/ppermute | solution.py:22
  7.8 0.6 pad_maximum_fusion.1
  8.4 7.7 %all-to-all-start = ((bf16[4,32,384]{2,1,0:T(8,128)(2,1)}), bf16[4,32,384]{2,1,0:T(8,128)(2,1)S(1)}, u32[]{:S(2)}, u32[]{:S(2)}) async-start(bf16[4,32,384]{2,1,0:T(8,128)(2,1)} %pad_maximum_fusion.1), calls=%async_computation | async-start | bytes 196608 | tf_op jit(solution)/shard_map/all_to_all | solution.py:18
  16.2 1.9 collective-permute-start.1
  18.1 8.1 %collective-permute-done.a01 = bf16[512,1024]{1,0:T(8,128)(2,1)S(1)} collective-permute-done((bf16[512,1024]{1,0:T(8,128)(2,1)}, bf16[512,1024]{1,0:T(8,128)(2,1)S(1)}, u32[]{:S(2)}, u32[]{:S(2)}) %collective-permute-start) | collective-permute-done | bytes 1048608 | tf_op jit(solution)/shard_map/ppermute | solution.py:22
  26.2 8.2 %collective-permute-start.2 = (bf16[512,1024]{1,0:T(8,128)(2,1)S(1)}, bf16[512,1024]{1,0:T(8,128)(2,1)}, u32[]{:S(2)}, u32[]{:S(2)}) collective-permute-start(bf16[512,1024]{1,0:T(8,128)(2,1)S(1)} %collective-permute-done.a01), channel_id=1, source_target_pairs={{0,16},{16,0},{1,17},{17,1},{2,18},{18,2},{3,19},{19,3},{4,20},{20... | collective-permute-start | bytes 3145736 | tf_op jit(solution)/shard_map/ppermute | solution.py:22
  34.4 0.6 copy-done.1
  35.1 2.0 first_scale.1
  37.1 7.0 %all-to-all-start.1 = ((bf16[16,128,256]{2,1,0:T(8,128)(2,1)}), bf16[16,128,256]{2,1,0:T(8,128)(2,1)}, u32[]{:S(2)}, u32[]{:S(2)}) async-start(bf16[16,128,256]{2,1,0:T(8,128)(2,1)} %get-tuple-element.12), calls=%async_computation.1 | async-start | bytes 2097152 | tf_op jit(solution)/shard_map/all_to_all | solution.py:18
  44.2 16.9 %all-to-all-done.1 = bf16[16,128,256]{2,1,0:T(8,128)(2,1)} async-done(((bf16[16,128,256]{2,1,0:T(8,128)(2,1)}), bf16[16,128,256]{2,1,0:T(8,128)(2,1)}, u32[]{:S(2)}, u32[]{:S(2)}) %all-to-all-start.1) | async-done | bytes 1048608 | tf_op jit(solution)/shard_map/all_to_all | solution.py:18
  61.1 2.9 %panel_product.3 = bf16[8,2,2,32,256]{4,3,2,1,0:T(8,128)(2,1)S(1)} custom-call(s32[2]{0:T(128)S(1)} %pad_add_fusion.place, bf16[16,2,64,256]{3,2,1,0:T(8,128)(2,1)} %bitcast.3.whole, bf16[512,1024]{1,0:T(8,128)(2,1)S(1)} %copy-done, bf16[512,1024]{1,0:T(8,128)(2,1)S(1)} %collective-permute-done.a01, bf16[512,1024]{1,0:T(8,128)(2,1)S(1)} %collective-permute-done.1.a10, ...), custom_call_target="tpu_custom_call" | custom-call | tf_op jit(solution)/shard_map/panel_product/pallas_call | solution.py:98
  64.0 39.3 %all_to_all.40.parts = bf16[8,128,256]{2,1,0:T(8,128)(2,1)} all-to-all(bf16[8,128,256]{2,1,0:T(8,128)(2,1)S(1)} %bitcast.48), channel_id=1, replica_groups=mesh['x'=4,'y'=4,'c'=2,'zh'=4,'zm'=2,'z0'=2] {'zh','zm'}, dimensions={0} | all-to-all | bytes 1048576 | tf_op jit(solution)/shard_map/all_to_all | solution.py:18
  103.3 2.3 update.2
  105.6 15.4 %all_to_all.41 = bf16[16,128,256]{2,1,0:T(8,128)(2,1)S(1)} all-to-all(bf16[16,128,256]{2,1,0:T(8,128)(2,1)} %get-tuple-element.16), channel_id=1, replica_groups=mesh['x'=4,'y'=4,'c'=2,'zh'=4,'zm'=2,'z0'=2] {'x','y'}, dimensions={0} | all-to-all | bytes 2097152 | tf_op jit(solution)/shard_map/all_to_all | solution.py:18
  121.0 2.6 %panel_product.4 = bf16[8,2,2,32,256]{4,3,2,1,0:T(8,128)(2,1)S(1)} custom-call(s32[2]{0:T(128)S(1)} %pad_add_fusion.place, bf16[16,2,64,256]{3,2,1,0:T(8,128)(2,1)S(1)} %bitcast.46, bf16[512,1024]{1,0:T(8,128)(2,1)S(1)} %copy-done, bf16[512,1024]{1,0:T(8,128)(2,1)S(1)} %collective-permute-done.a01, bf16[512,1024]{1,0:T(8,128)(2,1)S(1)} %collective-permute-done.1.a10, ...), custom_call_target="tpu_custom_call" | custom-call | tf_op jit(solution)/shard_map/panel_product/pallas_call | solution.py:98
  123.5 36.3 %all_to_all.42.parts = bf16[8,128,256]{2,1,0:T(8,128)(2,1)} all-to-all(bf16[8,128,256]{2,1,0:T(8,128)(2,1)S(1)} %bitcast.49), channel_id=1, replica_groups=mesh['x'=4,'y'=4,'c'=2,'zh'=4,'zm'=2,'z0'=2] {'zh','zm'}, dimensions={0} | all-to-all | bytes 1048576 | tf_op jit(solution)/shard_map/all_to_all | solution.py:18
  159.8 2.3 update.3
  162.1 15.4 %all_to_all.43 = bf16[16,128,256]{2,1,0:T(8,128)(2,1)S(1)} all-to-all(bf16[16,128,256]{2,1,0:T(8,128)(2,1)} %get-tuple-element.19), channel_id=1, replica_groups=mesh['x'=4,'y'=4,'c'=2,'zh'=4,'zm'=2,'z0'=2] {'x','y'}, dimensions={0} | all-to-all | bytes 2097152 | tf_op jit(solution)/shard_map/all_to_all | solution.py:18
  177.5 2.6 %panel_product.5 = bf16[8,2,2,32,256]{4,3,2,1,0:T(8,128)(2,1)S(1)} custom-call(s32[2]{0:T(128)S(1)} %pad_add_fusion.place, bf16[16,2,64,256]{3,2,1,0:T(8,128)(2,1)S(1)} %bitcast.45, bf16[512,1024]{1,0:T(8,128)(2,1)S(1)} %copy-done, bf16[512,1024]{1,0:T(8,128)(2,1)S(1)} %collective-permute-done.a01, bf16[512,1024]{1,0:T(8,128)(2,1)S(1)} %collective-permute-done.1.a10, ...), custom_call_target="tpu_custom_call" | custom-call | tf_op jit(solution)/shard_map/panel_product/pallas_call | solution.py:98
  180.0 32.4 %all_to_all.44.parts = bf16[8,128,256]{2,1,0:T(8,128)(2,1)} all-to-all(bf16[8,128,256]{2,1,0:T(8,128)(2,1)S(1)} %bitcast.47), channel_id=1, replica_groups=mesh['x'=4,'y'=4,'c'=2,'zh'=4,'zm'=2,'z0'=2] {'zh','zm'}, dimensions={0} | all-to-all | bytes 1048576 | tf_op jit(solution)/shard_map/all_to_all | solution.py:18
  212.5 1.8 last_update.1
  214.3 0.9 pad_maximum_fusion
  215.2 21.9 %all_to_all.45 = bf16[4,3,32,256]{3,2,1,0:T(8,128)(2,1)S(1)} all-to-all(bf16[4,3,32,256]{3,2,1,0:T(8,128)(2,1)S(1)} %pad_maximum_fusion), channel_id=1, replica_groups=mesh['x'=4,'y'=4,'c'=2,'zh'=4,'zm'=2,'z0'=2] {'z0','c'}, dimensions={0} | all-to-all | bytes 393216 | tf_op jit(solution)/shard_map/all_to_all | solution.py:18
  (22 shorter events, 2.1 us)
Async XLA Ops:
  0.6 7.0 %copy-start.5 = (s32[32]{0:T(128)S(1)}, s32[32]{0:T(128)}, u32[]{:S(2)}) copy-start(s32[32]{0:T(128)} %param.6) | copy-start | bytes 388
  0.6 7.0 %copy-start.2 = (bf16[32,1024]{1,0:T(8,128)(2,1)S(1)}, bf16[32,1024]{1,0:T(8,128)(2,1)}, u32[]{:S(2)}) copy-start(bf16[32,1024]{1,0:T(8,128)(2,1)} %param.5) | copy-start | bytes 196612
  3.3 22.9 %collective-permute-start = (bf16[512,1024]{1,0:T(8,128)(2,1)}, bf16[512,1024]{1,0:T(8,128)(2,1)S(1)}, u32[]{:S(2)}, u32[]{:S(2)}) collective-permute-start(bf16[512,1024]{1,0:T(8,128)(2,1)} %dense_panel.1.a00), channel_id=1, source_target_pairs={{0,1},{1,0},{2,3},{3,2},{4,5},{5,4},{6,7},{7,6},{8,9},{9,8},{10,11... | collective-permute-start | bytes 3145736 | tf_op jit(solution)/shard_map/ppermute | solution.py:22
  8.4 26.0 %all-to-all-start = ((bf16[4,32,384]{2,1,0:T(8,128)(2,1)}), bf16[4,32,384]{2,1,0:T(8,128)(2,1)S(1)}, u32[]{:S(2)}, u32[]{:S(2)}) async-start(bf16[4,32,384]{2,1,0:T(8,128)(2,1)} %pad_maximum_fusion.1), calls=%async_computation | async-start | bytes 196608 | tf_op jit(solution)/shard_map/all_to_all | solution.py:18
  16.2 28.0 %collective-permute-start.1 = (bf16[512,1024]{1,0:T(8,128)(2,1)}, bf16[512,1024]{1,0:T(8,128)(2,1)S(1)}, u32[]{:S(2)}, u32[]{:S(2)}) collective-permute-start(bf16[512,1024]{1,0:T(8,128)(2,1)} %dense_panel.1.a00), channel_id=1, source_target_pairs={{0,16},{16,0},{1,17},{17,1},{2,18},{18,2},{3,19},{19,3},{4,20},{20... | collective-permute-start | bytes 3145736 | tf_op jit(solution)/shard_map/ppermute | solution.py:22
  26.2 34.9 %collective-permute-start.2 = (bf16[512,1024]{1,0:T(8,128)(2,1)S(1)}, bf16[512,1024]{1,0:T(8,128)(2,1)}, u32[]{:S(2)}, u32[]{:S(2)}) collective-permute-start(bf16[512,1024]{1,0:T(8,128)(2,1)S(1)} %collective-permute-done.a01), channel_id=1, source_target_pairs={{0,16},{16,0},{1,17},{17,1},{2,18},{18,2},{3,19},{19,3},{4,20},{20... | collective-permute-start | bytes 3145736 | tf_op jit(solution)/shard_map/ppermute | solution.py:22
  34.4 0.7 copy-start.1
  37.1 24.0 %copy-start = (bf16[512,1024]{1,0:T(8,128)(2,1)S(1)}, bf16[512,1024]{1,0:T(8,128)(2,1)}, u32[]{:S(2)}) copy-start(bf16[512,1024]{1,0:T(8,128)(2,1)} %dense_panel.1.a00) | copy-start | bytes 3145732
  37.1 24.0 %all-to-all-start.1 = ((bf16[16,128,256]{2,1,0:T(8,128)(2,1)}), bf16[16,128,256]{2,1,0:T(8,128)(2,1)}, u32[]{:S(2)}, u32[]{:S(2)}) async-start(bf16[16,128,256]{2,1,0:T(8,128)(2,1)} %get-tuple-element.12), calls=%async_computation.1 | async-start | bytes 2097152 | tf_op jit(solution)/shard_map/all_to_all | solution.py:18
  212.5 1.9 copy-start.3
  212.5 1.9 copy-start.4

commit v2 on v0

v2 whole, which is shorter than its diff:
```python
import jax
import jax.numpy as jnp
from jax import lax
from jax.experimental import pallas as pl
from jax.experimental.pallas import tpu as pltpu
from jax.sharding import Mesh, PartitionSpec as P

HOPS = 3
SIZES = {"x": 4, "y": 4, "c": 2, "zh": 4, "zl": 4}
PLANE = ("x", "y")
LINE = ("zh", "zl")
LENGTH = 16
WINDOW = 4
LANES = 128
VMEM = pl.BlockSpec(memory_space=pltpu.VMEM)
SMEM = pl.BlockSpec(memory_space=pltpu.SMEM)


def exchange(x, axes):
    return lax.all_to_all(x, axes, 0, 0, tiled=True)


def send(x, step):
    return lax.ppermute(x, LINE, [(i, (i + step) % LENGTH) for i in range(LENGTH)])


def swap_cores(x):
    return lax.ppermute(x, "c", [(0, 1), (1, 0)])


def struct(shape, dtype=jnp.bfloat16):
    return jax.ShapeDtypeStruct(shape, dtype)


def dense_kernel(cols, counts, blocks, out):
    out[...] = jnp.zeros_like(out)
    row_blocks, slots, size, _ = blocks.shape
    for g in range(row_blocks):
        for t in range(slots):

            @pl.when(t < counts[g])
            def _():
                at = pl.multiple_of(cols[g, t] * size, size)
                out[g * size : (g + 1) * size, pl.ds(at, size)] = blocks[g, t]


def build_dense(blocks, cols, counts):
    g, t, size, _ = blocks.shape
    return pl.pallas_call(
        dense_kernel,
        out_shape=struct((g * size, t * size)),
        in_specs=[SMEM, SMEM, VMEM],
        out_specs=VMEM,
        name="dense_panel",
    )(cols, counts, blocks)


def spread_kernel(place, features, degree, own, ahead, back, back2):
    width = features.shape[1] // WINDOW
    for step, out in ((0, own), (1, ahead), (-1, back), (-2, back2)):
        piece = lax.rem(place[1] + step + WINDOW, WINDOW)
        at = pl.multiple_of(piece * width, width)
        out[:, :width] = features[:, pl.ds(at, width)]
        out[:, width:] = degree[...]


def spread(place, features, degree):
    rows, full = features.shape
    shape = struct((rows, full // WINDOW + LANES))
    return pl.pallas_call(
        spread_kernel,
        out_shape=(shape,) * 4,
        in_specs=[SMEM, VMEM, VMEM],
        out_specs=(VMEM,) * 4,
        name="spread_rows",
    )(place, features, degree)


def first_kernel(*refs):
    sent, copies, scale = refs[WINDOW:]
    rows, width = refs[0].shape
    width -= LANES
    for w, got in enumerate(refs[:WINDOW]):
        at = slice(w * rows, (w + 1) * rows)
        s = lax.rsqrt(got[:, width:].astype(jnp.float32))
        s = jnp.concatenate([s] * (width // LANES), axis=1)
        value = (s * got[:, :width].astype(jnp.float32)).astype(jnp.bfloat16)
        scale[at, :] = s
        sent[at, :] = value
        for k in range(copies.shape[0]):
            copies[k, at, :] = value


def first(pieces, n_copies):
    rows, width = pieces[0].shape
    shape = (WINDOW * rows, width - LANES)
    return pl.pallas_call(
        first_kernel,
        out_shape=(struct(shape), struct((n_copies,) + shape), struct(shape, jnp.float32)),
        in_specs=[VMEM] * WINDOW,
        out_specs=(VMEM,) * 3,
        name="first_scale",
    )(*pieces)


def product_kernel(place, ours, theirs, p0, p1, p2, p3, out, columns):
    core, level = place[0], place[1]
    plane, rows, width = ours.shape
    rows //= WINDOW
    for j in range(plane):
        for w in range(WINDOW):
            columns[w, j, core] = ours[j, w * rows : (w + 1) * rows]
            columns[w, j, 1 - core] = theirs[j, w * rows : (w + 1) * rows]
    total = None
    for w, panel in enumerate((p0, p1, p2, p3)):
        value = jnp.dot(
            panel[...], columns[w].reshape(-1, width), preferred_element_type=jnp.float32
        )
        total = value if total is None else total + value
    total = total.astype(jnp.bfloat16).reshape(LENGTH, rows, width)
    for r in range(LENGTH):
        out[lax.rem(r + 1 + LENGTH - level, LENGTH)] = total[r]


def product(place, ours, theirs, panels):
    plane, rows, width = ours.shape
    rows //= WINDOW
    return pl.pallas_call(
        product_kernel,
        out_shape=struct((LENGTH, rows, width)),
        in_specs=[SMEM] + [VMEM] * 6,
        out_specs=VMEM,
        scratch_shapes=[pltpu.VMEM((WINDOW, plane, 2, rows, width), jnp.bfloat16)],
        compiler_params=pltpu.CompilerParams(vmem_limit_bytes=40 << 20),
        name="panel_product",
    )(place, ours, theirs, *panels)


def update_kernel(parts, sent, scale, hop, *more):
    total = parts[0].astype(jnp.float32)
    for k in range(1, parts.shape[0]):
        total += parts[k].astype(jnp.float32)
    s = scale[...]
    value = (s * (total + sent[...].astype(jnp.float32))).astype(jnp.bfloat16)
    hop[...] = value
    if more:
        new_sent, copies = more
        value = (s * value.astype(jnp.float32)).astype(jnp.bfloat16)
        new_sent[...] = value
        for k in range(copies.shape[0]):
            copies[k] = value


def update(parts, sent, scale, n_copies):
    shape = struct(sent.shape)
    out = (shape, shape, struct((n_copies,) + sent.shape)) if n_copies else (shape,)
    return pl.pallas_call(
        update_kernel,
        out_shape=out,
        in_specs=[VMEM] * 3,
        out_specs=(VMEM,) * len(out),
        name="update",
    )(parts, sent, scale)


def collect_kernel(place, own, ahead, back, back2, *outs):
    width = own.shape[2]
    for step, got in ((0, own), (1, ahead), (-1, back), (-2, back2)):
        piece = lax.rem(place[1] + step + WINDOW, WINDOW)
        at = pl.multiple_of(piece * width, width)
        for k, out in enumerate(outs):
            out[:, pl.ds(at, width)] = got[k]


def collect(place, pieces):
    hops, rows, width = pieces[0].shape
    return pl.pallas_call(
        collect_kernel,
        out_shape=(struct((rows, WINDOW * width)),) * hops,
        in_specs=[SMEM] + [VMEM] * 4,
        out_specs=(VMEM,) * hops,
        name="collect_rows",
    )(place, *pieces)


def on_device(features, degree, blocks, block_cols, block_count):
    rows = features.shape[0]
    plane = SIZES["x"] * SIZES["y"]
    place = jnp.stack([lax.axis_index("c"), lax.axis_index("zl")]).astype(jnp.int32)

    wide = jnp.broadcast_to(degree.astype(jnp.bfloat16)[:, None], (rows, LANES))
    own, ahead, back, back2 = spread(place, features, wide)
    pieces = (send(ahead, 1), own, send(back, -1), send(back2, -2))
    sent, copies, scale = first(pieces, plane)

    panel = build_dense(blocks[:, 0], block_cols[:, 0], block_count[:, 0])
    above = send(panel, -1)
    below = send(panel, 1)
    gate, _ = lax.optimization_barrier((above, copies))
    panels = (below, panel, above, send(gate, -1))

    hops = []
    for hop in range(HOPS):
        ours = exchange(copies, PLANE)
        theirs = swap_cores(ours)
        partial_value = product(place, ours, theirs, panels)
        parts = exchange(partial_value.reshape(SIZES["zh"], WINDOW * rows, -1), "zh")
        value, *more = update(parts, sent, scale, plane if hop < HOPS - 1 else 0)
        if more:
            sent, copies = more
        hops.append(value.reshape(WINDOW, rows, -1))
    hops = jnp.stack(hops, axis=1)
    return collect(place, (hops[1], send(hops[0], -1), send(hops[2], 1), send(hops[3], 2)))


def solution(mesh):
    axes = tuple(SIZES)
    fine = Mesh(mesh.devices.reshape(tuple(SIZES.values())), axes)
    in_specs = (
        P(axes, None),
        P(axes),
        P(axes[:3], axes[3:], None, None, None),
        P(axes[:3], axes[3:], None),
        P(axes[:3], axes[3:]),
    )
    out_specs = (P(axes, None),) * 3
    return jax.shard_map(
        on_device, mesh=fine, in_specs=in_specs, out_specs=out_specs, check_vma=False
    )
```

time: 832 us -> 247 us (0.30); the launches traced: 817 us -> 246 us
  waiting for transfers between devices: 593 us -> 53.6 us
  loops' own time: 108 us -> 0 us
  blocking collectives: 0 us -> 90.7 us
  starting transfers between devices: 0.24 us -> 76.5 us
  matrix products: 47.1 us -> 0 us
  local copies, waits for them, and re-layouts: 47 us -> 2.61 us
  Pallas kernels: 0 us -> 20.5 us
  between operations: 14.2 us -> 0.86 us
    reduce_scatter x3 -> x0, waiting for transfers between devices: 387 us -> none  [on_device(): lax.psum_scatter(partial_value.astype(jnp.bfloat16), 'rep', scatter_dimen...]
    all_gather x3 -> x0, waiting for transfers between devices: 206 us -> none  [on_device(): whole = lax.all_gather(sent, 'team', axis=0, tiled=True)]
    another operation x15 -> x0, loops' own time: 108 us -> none  [the longest x12 108 us: row_block(): lax.fori_loop(0, counts_used[which], add_slot, jnp.zeros((block_size, wid...]
    all_to_all x0 -> x5, blocking collectives: none -> 90.7 us  [exchange(): return lax.all_to_all(x, axes, 0, 0, tiled=True)]
    ppermute x0 -> x12, starting transfers between devices: none -> 69.4 us  [the longest x9 46.6 us: send(): lax.ppermute(x, LINE, [(i, (i + step) % LENGTH) for i in range(LENGTH)])]
    dot_general x39 -> x0, matrix products: 47.1 us -> none  [add_slot(): return inner + jnp.dot(tile, piece, preferred_element_type=jnp.float32)]
    dynamic_slice x51 -> x0, local copies, waits for them, and re-layouts: 42.8 us -> none  [the longest x39 32.8 us: add_slot(): piece = pieces[columns_used[which, slot]]]
    ppermute x0 -> x12, waiting for transfers between devices: none -> 40.4 us  [the longest x9 35.9 us: send(): lax.ppermute(x, LINE, [(i, (i + step) % LENGTH) for i in range(LENGTH)])]
  transfers between devices with their start and end apart: 6 -> 13, of which waited for: 6 -> 8; matrix products, arithmetic and copies ran while one was open for 0% -> 1% of each run, Pallas kernels for 0% -> 1%
where the time goes in v2:
time: 247 us; the launch traced here: 246 us
  blocking collectives  90.7 us (37%)
  starting transfers between devices  76.5 us (31%)
  waiting for transfers between devices  53.6 us (22%)
  Pallas kernels  20.5 us (8%)
  local copies, waits for them, and re-layouts  2.61 us (1%)
    all_to_all x5, blocking collectives, exchange(): return lax.all_to_all(x, axes, 0, 0, tiled=True)  90.7 us
    ppermute x9, starting transfers between devices, send(): lax.ppermute(x, LINE, [(i, (i + step) % LENGTH) for i in range(LENGTH)])  46.6 us
    ppermute x9, waiting for transfers between devices, send(): lax.ppermute(x, LINE, [(i, (i + step) % LENGTH) for i in range(LENGTH)])  35.9 us
    ppermute x3, starting transfers between devices, swap_cores(): return lax.ppermute(x, 'c', [(0, 1), (1, 0)])  22.8 us
    all_to_all x1, waiting for transfers between devices, exchange(): return lax.all_to_all(x, axes, 0, 0, tiled=True)  13.1 us
    all_to_all x1, starting transfers between devices, exchange(): return lax.all_to_all(x, axes, 0, 0, tiled=True)  7.05 us
    pallas_call x3, Pallas kernels, product(): pl.pallas_call(product_kernel, out_shape=struct((LENGTH, rows, width)), i...  6.86 us
    pallas_call x3, Pallas kernels, update(): pl.pallas_call(update_kernel, out_shape=out, in_specs=[VMEM] * 3, out_spe...  6.04 us
  transfers between devices with their start and end apart: 13, of which 8 were waited for; matrix products, arithmetic and copies ran while one was open for 1% of the time, Pallas kernels for 1%

profile of v2, /device:TPU:1, one launch (start us, length us, event | category | flops | bytes accessed | tf_op | source)
XLA Modules:
  0.0 246.1 jit_solution(7375122541985157433)
XLA Ops:
  0.6 2.6 %dense_panel.1.p1 = bf16[512,1024]{1,0:T(8,128)(2,1)} custom-call(s32[4,8]{1,0:T(4,128)} %bitcast.26, s32[4]{0:T(128)} %bitcast.27, bf16[4,8,128,128]{3,2,1,0:T(8,128)(2,1)} %bitcast.22), custom_call_target="tpu_custom_call" | custom-call | tf_op jit(solution)/shard_map/dense_panel/pallas_call | solution.py:49
  3.2 11.9 %collective-permute-start.5 = (bf16[512,1024]{1,0:T(8,128)(2,1)}, bf16[512,1024]{1,0:T(8,128)(2,1)S(1)}, u32[]{:S(2)}, u32[]{:S(2)}) collective-permute-start(bf16[512,1024]{1,0:T(8,128)(2,1)} %dense_panel.1.p1), channel_id=1, source_target_pairs={{0,15},{1,0},{2,1},{3,2},{4,3},{5,4},{6,5},{7,6},{8,7},{9,8},{10,9... | collective-permute-start | bytes 3145736 | tf_op jit(solution)/shard_map/ppermute | solution.py:24
  19.9 4.6 %collective-permute-start.1 = (bf16[32,384]{1,0:T(8,128)(2,1)}, bf16[32,384]{1,0:T(8,128)(2,1)S(1)}, u32[]{:S(2)}, u32[]{:S(2)}) collective-permute-start(bf16[32,384]{1,0:T(8,128)(2,1)} %get-tuple-element.19), channel_id=1, source_target_pairs={{0,15},{1,0},{2,1},{3,2},{4,3},{5,4},{6,5},{7,6},{8,7},{9,8},{10,9... | collective-permute-start | bytes 73736 | tf_op jit(solution)/shard_map/ppermute | solution.py:24
  26.4 11.7 %collective-permute-done.1.refs_2_ = bf16[32,384]{1,0:T(8,128)(2,1)S(1)} collective-permute-done((bf16[32,384]{1,0:T(8,128)(2,1)}, bf16[32,384]{1,0:T(8,128)(2,1)S(1)}, u32[]{:S(2)}, u32[]{:S(2)}) %collective-permute-start.1) | collective-permute-done | bytes 24608 | tf_op jit(solution)/shard_map/ppermute | solution.py:24
  41.2 7.1 %all-to-all-start = ((bf16[16,128,256]{2,1,0:T(8,128)(2,1)}), bf16[16,128,256]{2,1,0:T(8,128)(2,1)}, u32[]{:S(2)}, u32[]{:S(2)}) async-start(bf16[16,128,256]{2,1,0:T(8,128)(2,1)} %get-tuple-element.21), calls=%async_computation | async-start | bytes 2097152 | tf_op jit(solution)/shard_map/all_to_all | solution.py:20
  50.2 13.1 %all-to-all-done.ours = bf16[16,128,256]{2,1,0:T(8,128)(2,1)} async-done(((bf16[16,128,256]{2,1,0:T(8,128)(2,1)}), bf16[16,128,256]{2,1,0:T(8,128)(2,1)}, u32[]{:S(2)}, u32[]{:S(2)}) %all-to-all-start) | async-done | bytes 1048608 | tf_op jit(solution)/shard_map/all_to_all | solution.py:20
  63.3 5.0 %collective-permute-start.3 = (bf16[16,128,256]{2,1,0:T(8,128)(2,1)}, bf16[16,128,256]{2,1,0:T(8,128)(2,1)S(1)}, u32[]{:S(2)}, u32[]{:S(2)}) collective-permute-start(bf16[16,128,256]{2,1,0:T(8,128)(2,1)} %all-to-all-done.ours), channel_id=1, source_target_pairs={{0,16},{16,0},{1,17},{17,1},{2,18},{18,2},{3,19},{19,3},{4,20},{20... | collective-permute-start | bytes 3145736 | tf_op jit(solution)/shard_map/ppermute | solution.py:28
  68.3 4.8 %collective-permute-start.6 = (bf16[512,1024]{1,0:T(8,128)(2,1)S(1)}, bf16[512,1024]{1,0:T(8,128)(2,1)S(1)}, u32[]{:S(2)}, u32[]{:S(2)}) collective-permute-start(bf16[512,1024]{1,0:T(8,128)(2,1)S(1)} %collective-permute-done.5.p2), channel_id=1, source_target_pairs={{0,15},{1,0},{2,1},{3,2},{4,3},{5,4},{6,5},{7,6},{8,7},{9,8},{10,9... | collective-permute-start | bytes 3145736 | tf_op jit(solution)/shard_map/ppermute | solution.py:24
  74.5 21.2 %collective-permute-done.6.p3 = bf16[512,1024]{1,0:T(8,128)(2,1)S(1)} collective-permute-done((bf16[512,1024]{1,0:T(8,128)(2,1)S(1)}, bf16[512,1024]{1,0:T(8,128)(2,1)S(1)}, u32[]{:S(2)}, u32[]{:S(2)}) %collective-permute-start.6) | collective-permute-done | bytes 1048608 | tf_op jit(solution)/shard_map/ppermute | solution.py:24
  95.7 3.0 %panel_product.3 = bf16[16,32,256]{2,1,0:T(8,128)(2,1)S(1)} custom-call(s32[2]{0:T(128)S(1)} %copy-done.4, bf16[16,128,256]{2,1,0:T(8,128)(2,1)} %all-to-all-done.ours, bf16[16,128,256]{2,1,0:T(8,128)(2,1)S(1)} %collective-permute-done.3.theirs, bf16[512,1024]{1,0:T(8,128)(2,1)S(1)} %collective-permute-done.4.p0, bf16[512,1024]{1,0:T(8,128)(2,1)S(1)} %copy-done, ...), custom_call_target="tpu_custom_call" | custom-call | tf_op jit(solution)/shard_map/panel_product/pallas_call | solution.py:128
  98.7 20.3 %all_to_all.30.parts = bf16[4,128,256]{2,1,0:T(8,128)(2,1)} all-to-all(bf16[4,128,256]{2,1,0:T(8,128)(2,1)S(1)} %bitcast.20), channel_id=1, replica_groups=mesh['x'=4,'y'=4,'c'=2,'zh'=4,'zl'=4] {'zh'}, dimensions={0} | all-to-all | bytes 524288 | tf_op jit(solution)/shard_map/all_to_all | solution.py:20
  119.0 2.2 update.3
  121.2 15.5 %all_to_all.31.ours = bf16[16,128,256]{2,1,0:T(8,128)(2,1)S(1)} all-to-all(bf16[16,128,256]{2,1,0:T(8,128)(2,1)} %get-tuple-element.26), channel_id=1, replica_groups=mesh['x'=4,'y'=4,'c'=2,'zh'=4,'zl'=4] {'x','y'}, dimensions={0} | all-to-all | bytes 2097152 | tf_op jit(solution)/shard_map/all_to_all | solution.py:20
  136.7 9.3 %collective-permute-start.7 = (bf16[16,128,256]{2,1,0:T(8,128)(2,1)S(1)}, bf16[16,128,256]{2,1,0:T(8,128)(2,1)S(1)}, u32[]{:S(2)}, u32[]{:S(2)}) collective-permute-start(bf16[16,128,256]{2,1,0:T(8,128)(2,1)S(1)} %all_to_all.31.ours), channel_id=1, source_target_pairs={{0,16},{16,0},{1,17},{17,1},{2,18},{18,2},{3,19},{19,3},{4,20},{20... | collective-permute-start | bytes 3145736 | tf_op jit(solution)/shard_map/ppermute | solution.py:28
  145.9 2.3 collective-permute-done.7.theirs
  150.1 19.8 %all_to_all.32.parts = bf16[4,128,256]{2,1,0:T(8,128)(2,1)} all-to-all(bf16[4,128,256]{2,1,0:T(8,128)(2,1)S(1)} %bitcast.21), channel_id=1, replica_groups=mesh['x'=4,'y'=4,'c'=2,'zh'=4,'zl'=4] {'zh'}, dimensions={0} | all-to-all | bytes 524288 | tf_op jit(solution)/shard_map/all_to_all | solution.py:20
  169.9 2.2 update.4
  172.1 15.6 %all_to_all.33.ours = bf16[16,128,256]{2,1,0:T(8,128)(2,1)S(1)} all-to-all(bf16[16,128,256]{2,1,0:T(8,128)(2,1)} %get-tuple-element.29), channel_id=1, replica_groups=mesh['x'=4,'y'=4,'c'=2,'zh'=4,'zl'=4] {'x','y'}, dimensions={0} | all-to-all | bytes 2097152 | tf_op jit(solution)/shard_map/all_to_all | solution.py:20
  187.7 8.6 %collective-permute-start.8 = (bf16[16,128,256]{2,1,0:T(8,128)(2,1)S(1)}, bf16[16,128,256]{2,1,0:T(8,128)(2,1)S(1)}, u32[]{:S(2)}, u32[]{:S(2)}) collective-permute-start(bf16[16,128,256]{2,1,0:T(8,128)(2,1)S(1)} %all_to_all.33.ours), channel_id=1, source_target_pairs={{0,16},{16,0},{1,17},{17,1},{2,18},{18,2},{3,19},{19,3},{4,20},{20... | collective-permute-start | bytes 3145736 | tf_op jit(solution)/shard_map/ppermute | solution.py:28
  196.3 2.3 collective-permute-done.8.theirs
  200.5 19.5 %all_to_all.34.parts = bf16[4,128,256]{2,1,0:T(8,128)(2,1)} all-to-all(bf16[4,128,256]{2,1,0:T(8,128)(2,1)S(1)} %bitcast.19), channel_id=1, replica_groups=mesh['x'=4,'y'=4,'c'=2,'zh'=4,'zl'=4] {'zh'}, dimensions={0} | all-to-all | bytes 524288 | tf_op jit(solution)/shard_map/all_to_all | solution.py:20
  223.2 11.6 %collective-permute-start.11 = (bf16[3,32,256]{2,1,0:T(8,128)(2,1)S(1)}, bf16[3,32,256]{2,1,0:T(8,128)(2,1)S(1)}, u32[]{:S(2)}, u32[]{:S(2)}) collective-permute-start(bf16[3,32,256]{2,1,0:T(8,128)(2,1)S(1)} %get-tuple-element.31), channel_id=1, source_target_pairs={{0,2},{1,3},{2,4},{3,5},{4,6},{5,7},{6,8},{7,9},{8,10},{9,11},{10,... | collective-permute-start | bytes 147464 | tf_op jit(solution)/shard_map/ppermute | solution.py:24
  234.8 3.7 %collective-permute-start.10 = (bf16[3,32,256]{2,1,0:T(8,128)(2,1)S(1)}, bf16[3,32,256]{2,1,0:T(8,128)(2,1)S(1)}, u32[]{:S(2)}, u32[]{:S(2)}) collective-permute-start(bf16[3,32,256]{2,1,0:T(8,128)(2,1)S(1)} %get-tuple-element.32), channel_id=1, source_target_pairs={{0,1},{1,2},{2,3},{3,4},{4,5},{5,6},{6,7},{7,8},{8,9},{9,10},{10,1... | collective-permute-start | bytes 147464 | tf_op jit(solution)/shard_map/ppermute | solution.py:24
  238.5 4.3 %collective-permute-start.9 = (bf16[3,32,256]{2,1,0:T(8,128)(2,1)S(1)}, bf16[3,32,256]{2,1,0:T(8,128)(2,1)S(1)}, u32[]{:S(2)}, u32[]{:S(2)}) collective-permute-start(bf16[3,32,256]{2,1,0:T(8,128)(2,1)S(1)} %get-tuple-element.33), channel_id=1, source_target_pairs={{0,15},{1,0},{2,1},{3,2},{4,3},{5,4},{6,5},{7,6},{8,7},{9,8},{10,9... | collective-permute-start | bytes 147464 | tf_op jit(solution)/shard_map/ppermute | solution.py:24
  (50 shorter events, 23.4 us)
Async XLA Ops:
  3.2 65.1 %collective-permute-start.5 = (bf16[512,1024]{1,0:T(8,128)(2,1)}, bf16[512,1024]{1,0:T(8,128)(2,1)S(1)}, u32[]{:S(2)}, u32[]{:S(2)}) collective-permute-start(bf16[512,1024]{1,0:T(8,128)(2,1)} %dense_panel.1.p1), channel_id=1, source_target_pairs={{0,15},{1,0},{2,1},{3,2},{4,3},{5,4},{6,5},{7,6},{8,7},{9,8},{10,9... | collective-permute-start | bytes 3145736 | tf_op jit(solution)/shard_map/ppermute | solution.py:24
  15.1 0.7 copy-start.13
  18.0 8.4 %collective-permute-start = (bf16[32,384]{1,0:T(8,128)(2,1)}, bf16[32,384]{1,0:T(8,128)(2,1)S(1)}, u32[]{:S(2)}, u32[]{:S(2)}) collective-permute-start(bf16[32,384]{1,0:T(8,128)(2,1)} %get-tuple-element.17), channel_id=1, source_target_pairs={{0,1},{1,2},{2,3},{3,4},{4,5},{5,6},{6,7},{7,8},{8,9},{9,10},{10,1... | collective-permute-start | bytes 73736 | tf_op jit(solution)/shard_map/ppermute | solution.py:24
  19.9 18.2 %collective-permute-start.1 = (bf16[32,384]{1,0:T(8,128)(2,1)}, bf16[32,384]{1,0:T(8,128)(2,1)S(1)}, u32[]{:S(2)}, u32[]{:S(2)}) collective-permute-start(bf16[32,384]{1,0:T(8,128)(2,1)} %get-tuple-element.19), channel_id=1, source_target_pairs={{0,15},{1,0},{2,1},{3,2},{4,3},{5,4},{6,5},{7,6},{8,7},{9,8},{10,9... | collective-permute-start | bytes 73736 | tf_op jit(solution)/shard_map/ppermute | solution.py:24
  24.5 14.2 %collective-permute-start.2 = (bf16[32,384]{1,0:T(8,128)(2,1)}, bf16[32,384]{1,0:T(8,128)(2,1)S(1)}, u32[]{:S(2)}, u32[]{:S(2)}) collective-permute-start(bf16[32,384]{1,0:T(8,128)(2,1)} %get-tuple-element.20), channel_id=1, source_target_pairs={{0,14},{1,15},{2,0},{3,1},{4,2},{5,3},{6,4},{7,5},{8,6},{9,7},{10,... | collective-permute-start | bytes 73736 | tf_op jit(solution)/shard_map/ppermute | solution.py:24
  26.4 12.3 %copy-start.10 = (bf16[32,384]{1,0:T(8,128)(2,1)}, bf16[32,384]{1,0:T(8,128)(2,1)S(1)}, u32[]{:S(2)}) copy-start(bf16[32,384]{1,0:T(8,128)(2,1)S(1)} %collective-permute-done.refs_0_) | copy-start | bytes 73732
  41.2 7.1 %copy-start = (bf16[512,1024]{1,0:T(8,128)(2,1)S(1)}, bf16[512,1024]{1,0:T(8,128)(2,1)}, u32[]{:S(2)}) copy-start(bf16[512,1024]{1,0:T(8,128)(2,1)} %dense_panel.1.p1) | copy-start | bytes 3145732
  41.2 54.5 %copy-start.4 = (s32[2]{0:T(128)S(1)}, s32[2]{0:T(128)}, u32[]{:S(2)}) copy-start(s32[2]{0:T(128)} %pad_add_fusion.place) | copy-start | bytes 28
  41.2 22.1 %all-to-all-start = ((bf16[16,128,256]{2,1,0:T(8,128)(2,1)}), bf16[16,128,256]{2,1,0:T(8,128)(2,1)}, u32[]{:S(2)}, u32[]{:S(2)}) async-start(bf16[16,128,256]{2,1,0:T(8,128)(2,1)} %get-tuple-element.21), calls=%async_computation | async-start | bytes 2097152 | tf_op jit(solution)/shard_map/all_to_all | solution.py:20
  48.3 26.2 %collective-permute-start.4 = (bf16[512,1024]{1,0:T(8,128)(2,1)S(1)}, bf16[512,1024]{1,0:T(8,128)(2,1)S(1)}, u32[]{:S(2)}, u32[]{:S(2)}) collective-permute-start(bf16[512,1024]{1,0:T(8,128)(2,1)S(1)} %copy-done), channel_id=1, source_target_pairs={{0,1},{1,2},{2,3},{3,4},{4,5},{5,6},{6,7},{7,8},{8,9},{9,10},{10,1... | collective-permute-start | bytes 3145736 | tf_op jit(solution)/shard_map/ppermute | solution.py:24
  63.3 11.1 %collective-permute-start.3 = (bf16[16,128,256]{2,1,0:T(8,128)(2,1)}, bf16[16,128,256]{2,1,0:T(8,128)(2,1)S(1)}, u32[]{:S(2)}, u32[]{:S(2)}) collective-permute-start(bf16[16,128,256]{2,1,0:T(8,128)(2,1)} %all-to-all-done.ours), channel_id=1, source_target_pairs={{0,16},{16,0},{1,17},{17,1},{2,18},{18,2},{3,19},{19,3},{4,20},{20... | collective-permute-start | bytes 3145736 | tf_op jit(solution)/shard_map/ppermute | solution.py:28
  68.3 27.3 %collective-permute-start.6 = (bf16[512,1024]{1,0:T(8,128)(2,1)S(1)}, bf16[512,1024]{1,0:T(8,128)(2,1)S(1)}, u32[]{:S(2)}, u32[]{:S(2)}) collective-permute-start(bf16[512,1024]{1,0:T(8,128)(2,1)S(1)} %collective-permute-done.5.p2), channel_id=1, source_target_pairs={{0,15},{1,0},{2,1},{3,2},{4,3},{5,4},{6,5},{7,6},{8,7},{9,8},{10,9... | collective-permute-start | bytes 3145736 | tf_op jit(solution)/shard_map/ppermute | solution.py:24
  95.7 3.0 %copy-start.1 = (bf16[512,1024]{1,0:T(8,128)(2,1)}, bf16[512,1024]{1,0:T(8,128)(2,1)S(1)}, u32[]{:S(2)}) copy-start(bf16[512,1024]{1,0:T(8,128)(2,1)S(1)} %collective-permute-done.6.p3) | copy-start | bytes 3145732
  121.2 27.0 %copy-start.2 = (bf16[512,1024]{1,0:T(8,128)(2,1)S(1)}, bf16[512,1024]{1,0:T(8,128)(2,1)}, u32[]{:S(2)}) copy-start(bf16[512,1024]{1,0:T(8,128)(2,1)} %copy-done.1) | copy-start | bytes 3145732
  136.7 11.5 %collective-permute-start.7 = (bf16[16,128,256]{2,1,0:T(8,128)(2,1)S(1)}, bf16[16,128,256]{2,1,0:T(8,128)(2,1)S(1)}, u32[]{:S(2)}, u32[]{:S(2)}) collective-permute-start(bf16[16,128,256]{2,1,0:T(8,128)(2,1)S(1)} %all_to_all.31.ours), channel_id=1, source_target_pairs={{0,16},{16,0},{1,17},{17,1},{2,18},{18,2},{3,19},{19,3},{4,20},{20... | collective-permute-start | bytes 3145736 | tf_op jit(solution)/shard_map/ppermute | solution.py:28
  172.1 26.5 %copy-start.3 = (bf16[512,1024]{1,0:T(8,128)(2,1)S(1)}, bf16[512,1024]{1,0:T(8,128)(2,1)}, u32[]{:S(2)}) copy-start(bf16[512,1024]{1,0:T(8,128)(2,1)} %copy-done.1) | copy-start | bytes 3145732
  187.7 10.9 %collective-permute-start.8 = (bf16[16,128,256]{2,1,0:T(8,128)(2,1)S(1)}, bf16[16,128,256]{2,1,0:T(8,128)(2,1)S(1)}, u32[]{:S(2)}, u32[]{:S(2)}) collective-permute-start(bf16[16,128,256]{2,1,0:T(8,128)(2,1)S(1)} %all_to_all.33.ours), channel_id=1, source_target_pairs={{0,16},{16,0},{1,17},{17,1},{2,18},{18,2},{3,19},{19,3},{4,20},{20... | collective-permute-start | bytes 3145736 | tf_op jit(solution)/shard_map/ppermute | solution.py:28
  220.0 1.7 copy-start.5
  220.0 1.7 copy-start.6
  223.2 19.6 %collective-permute-start.11 = (bf16[3,32,256]{2,1,0:T(8,128)(2,1)S(1)}, bf16[3,32,256]{2,1,0:T(8,128)(2,1)S(1)}, u32[]{:S(2)}, u32[]{:S(2)}) collective-permute-start(bf16[3,32,256]{2,1,0:T(8,128)(2,1)S(1)} %get-tuple-element.31), channel_id=1, source_target_pairs={{0,2},{1,3},{2,4},{3,5},{4,6},{5,7},{6,8},{7,9},{8,10},{9,11},{10,... | collective-permute-start | bytes 147464 | tf_op jit(solution)/shard_map/ppermute | solution.py:24
  234.8 8.0 %collective-permute-start.10 = (bf16[3,32,256]{2,1,0:T(8,128)(2,1)S(1)}, bf16[3,32,256]{2,1,0:T(8,128)(2,1)S(1)}, u32[]{:S(2)}, u32[]{:S(2)}) collective-permute-start(bf16[3,32,256]{2,1,0:T(8,128)(2,1)S(1)} %get-tuple-element.32), channel_id=1, source_target_pairs={{0,1},{1,2},{2,3},{3,4},{4,5},{5,6},{6,7},{7,8},{8,9},{9,10},{10,1... | collective-permute-start | bytes 147464 | tf_op jit(solution)/shard_map/ppermute | solution.py:24
  238.5 5.5 %collective-permute-start.9 = (bf16[3,32,256]{2,1,0:T(8,128)(2,1)S(1)}, bf16[3,32,256]{2,1,0:T(8,128)(2,1)S(1)}, u32[]{:S(2)}, u32[]{:S(2)}) collective-permute-start(bf16[3,32,256]{2,1,0:T(8,128)(2,1)S(1)} %get-tuple-element.33), channel_id=1, source_target_pairs={{0,15},{1,0},{2,1},{3,2},{4,3},{5,4},{6,5},{7,6},{8,7},{9,8},{10,9... | collective-permute-start | bytes 147464 | tf_op jit(solution)/shard_map/ppermute | solution.py:24
  242.8 1.1 copy-start.7
  242.8 1.1 copy-start.8
  (3 other events, 1.8 us)

commit v3 on v0

v3 whole, which is shorter than its diff:
```python
import jax
import jax.numpy as jnp
from jax import lax
from jax.experimental import pallas as pl
from jax.experimental.pallas import tpu as pltpu
from jax.sharding import Mesh, PartitionSpec as P

HOPS = 3
SIZES = {"x": 4, "y": 4, "c": 2, "zh": 4, "zl": 4}
PLANE = ("x", "y")
LINE = ("zh", "zl")
LENGTH = 16
WINDOW = 4
CORES = 2
LANES = 128
VMEM = pl.BlockSpec(memory_space=pltpu.VMEM)
SMEM = pl.BlockSpec(memory_space=pltpu.SMEM)


def exchange(x, axes):
    return lax.all_to_all(x, axes, 0, 0, tiled=True)


def send(x, step):
    return lax.ppermute(x, LINE, [(i, (i + step) % LENGTH) for i in range(LENGTH)])


def swap_cores(x):
    return lax.ppermute(x, "c", [(0, 1), (1, 0)])


def after(x, *others):
    return lax.optimization_barrier((x,) + others)[0]


def dense_kernel(cols, counts, blocks, out):
    out[...] = jnp.zeros_like(out)
    row_blocks, slots, size, _ = blocks.shape
    for g in range(row_blocks):
        for t in range(slots):

            @pl.when(t < counts[g])
            def _():
                at = pl.multiple_of(cols[g, t] * size, size)
                out[g * size : (g + 1) * size, pl.ds(at, size)] = blocks[g, t]


def build_dense(blocks, cols, counts):
    g, t, size, _ = blocks.shape
    return pl.pallas_call(
        dense_kernel,
        out_shape=jax.ShapeDtypeStruct((g * size, t * size), blocks.dtype),
        in_specs=[SMEM, SMEM, VMEM],
        out_specs=VMEM,
        name="dense_panel",
    )(cols, counts, blocks)


def product_kernel(place, whole, *refs):
    panels, (out, columns) = refs[: 2 * WINDOW], refs[2 * WINDOW :]
    core, level = place[0], place[1]
    plane, window, rows, width = whole.shape
    for j in range(plane):
        for w in range(window):
            columns[w, j] = whole[j, w]
    for near in range(CORES):
        total = None
        for w in range(window):
            value = jnp.dot(
                panels[near * window + w][...],
                columns[w].reshape(-1, width),
                preferred_element_type=jnp.float32,
            )
            total = value if total is None else total + value
        total = total.astype(jnp.bfloat16).reshape(LENGTH, rows // CORES, width)
        target = core if near == 0 else 1 - core
        for r in range(LENGTH):
            out[lax.rem(r + 1 + LENGTH - level, LENGTH), target] = total[r]


def product(place, whole, panels):
    plane, window, rows, width = whole.shape
    return pl.pallas_call(
        product_kernel,
        out_shape=jax.ShapeDtypeStruct((LENGTH, CORES, rows // CORES, width), jnp.bfloat16),
        in_specs=[SMEM] + [VMEM] * (1 + len(panels)),
        out_specs=VMEM,
        scratch_shapes=[pltpu.VMEM((window, plane, rows, width), jnp.bfloat16)],
        compiler_params=pltpu.CompilerParams(vmem_limit_bytes=40 << 20),
        name="panel_product",
    )(place, whole, *panels)


def on_device(features, degree, blocks, block_cols, block_count):
    f32, bf16 = jnp.float32, jnp.bfloat16
    rows, full = features.shape
    width = full // (CORES * WINDOW)
    plane = SIZES["x"] * SIZES["y"]
    pooled = WINDOW * CORES * rows
    level = lax.axis_index("zl")
    place = jnp.stack([lax.axis_index("c"), level]).astype(jnp.int32)

    panel = build_dense(blocks[:, 0], block_cols[:, 0], block_count[:, 0])
    above = send(panel, -1)
    below = send(panel, 1)

    half = full // CORES
    counts = jnp.broadcast_to(degree.astype(bf16)[:, None], (rows, LANES))
    halves = [jnp.concatenate([features[:, :half], counts], axis=1)]
    halves += [jnp.concatenate([features[:, half:], counts], axis=1)]
    got = exchange(jnp.stack(halves), "c")

    def piece(step):
        at = ((level + step) & (WINDOW - 1)) * width
        part = lax.dynamic_slice_in_dim(got, at, width, axis=2)
        return jnp.concatenate([part, got[:, :, half:]], axis=2)

    window = jnp.stack([send(piece(1), 1), piece(0), send(piece(-1), -1), send(piece(-2), -2)])
    window = window.reshape(pooled, width + LANES)
    scale = lax.rsqrt(window[:, width : width + 1].astype(f32))
    sent = (scale * window[:, :width].astype(f32)).astype(bf16)

    copies = jnp.broadcast_to(sent[None], (plane,) + sent.shape)
    two_above = send(after(above, below, copies), -1)
    whole = exchange(copies, PLANE)
    mine = (below, panel, above, two_above)
    early = tuple(swap_cores(p) for p in (after(below, copies), panel, after(above, copies)))
    panels = mine + early + (swap_cores(after(two_above, whole)),)

    hops = []
    for hop in range(HOPS):
        if hop:
            copies = jnp.broadcast_to(sent[None], (plane,) + sent.shape)
            whole = exchange(copies, PLANE)
        partial_value = product(
            place, whole.reshape(plane, WINDOW, CORES * rows, width), panels
        )
        parts = exchange(partial_value.reshape(SIZES["zh"], pooled, width), "zh")
        total = jnp.sum(parts.astype(f32), axis=0)
        value = (scale * (total + sent.astype(f32))).astype(bf16)
        sent = (scale * value.astype(f32)).astype(bf16)
        hops.append(value.reshape(WINDOW, CORES, rows, width))

    both = jnp.stack(hops, axis=2)
    arrived = (both[1], send(both[0], -1), send(both[3], 2), send(both[2], 1))
    turned = jnp.zeros((WINDOW,) + both.shape[1:], bf16)
    for step, part in enumerate(arrived):
        turned = lax.dynamic_update_index_in_dim(turned, part, (level + step) & (WINDOW - 1), 0)
    back = exchange(turned.transpose(1, 0, 2, 3, 4), "c")
    return tuple(
        jnp.concatenate([back[c, q, k] for c in range(CORES) for q in range(WINDOW)], axis=1)
        for k in range(HOPS)
    )


def solution(mesh):
    axes = tuple(SIZES)
    fine = Mesh(mesh.devices.reshape(tuple(SIZES.values())), axes)
    in_specs = (
        P(axes, None),
        P(axes),
        P(axes[:3], axes[3:], None, None, None),
        P(axes[:3], axes[3:], None),
        P(axes[:3], axes[3:]),
    )
    out_specs = (P(axes, None),) * 3
    return jax.shard_map(
        on_device, mesh=fine, in_specs=in_specs, out_specs=out_specs, check_vma=False
    )
```

time: 832 us -> 228 us (0.27); the launches traced: 817 us -> 226 us
  waiting for transfers between devices: 593 us -> 33.6 us
  loops' own time: 108 us -> 0 us
  blocking collectives: 0 us -> 86.1 us
  starting transfers between devices: 0.24 us -> 77.4 us
  matrix products: 47.1 us -> 0 us
  local copies, waits for them, and re-layouts: 47 us -> 8.37 us
  Pallas kernels: 0 us -> 18.4 us
  between operations: 14.2 us -> 1 us
    reduce_scatter x3 -> x0, waiting for transfers between devices: 387 us -> none  [on_device(): lax.psum_scatter(partial_value.astype(jnp.bfloat16), 'rep', scatter_dimen...]
    all_gather x3 -> x0, waiting for transfers between devices: 206 us -> none  [on_device(): whole = lax.all_gather(sent, 'team', axis=0, tiled=True)]
    another operation x15 -> x0, loops' own time: 108 us -> none  [the longest x12 108 us: row_block(): lax.fori_loop(0, counts_used[which], add_slot, jnp.zeros((block_size, wid...]
    all_to_all x0 -> x5, blocking collectives: none -> 86.1 us  [exchange(): return lax.all_to_all(x, axes, 0, 0, tiled=True)]
    ppermute x0 -> x13, starting transfers between devices: none -> 63 us  [the longest x9 49 us: send(): lax.ppermute(x, LINE, [(i, (i + step) % LENGTH) for i in range(LENGTH)])]
    dot_general x39 -> x0, matrix products: 47.1 us -> none  [add_slot(): return inner + jnp.dot(tile, piece, preferred_element_type=jnp.float32)]
    dynamic_slice x51 -> x1, local copies, waits for them, and re-layouts: 42.8 us -> 0.02 us  [piece(): part = lax.dynamic_slice_in_dim(got, at, width, axis=2)]
    all_to_all x0 -> x3, waiting for transfers between devices: none -> 19.9 us  [exchange(): return lax.all_to_all(x, axes, 0, 0, tiled=True)]
  transfers between devices with their start and end apart: 6 -> 16, of which waited for: 6 -> 9; matrix products, arithmetic and copies ran while one was open for 0% -> 1% of each run, Pallas kernels for 0% -> 0%
where the time goes in v3:
time: 228 us; the launch traced here: 226 us
  blocking collectives  86.1 us (38%)
  starting transfers between devices  77.4 us (34%)
  waiting for transfers between devices  33.6 us (15%)
  Pallas kernels  18.4 us (8%)
  local copies, waits for them, and re-layouts  8.37 us (4%)
    all_to_all x5, blocking collectives, exchange(): return lax.all_to_all(x, axes, 0, 0, tiled=True)  86.1 us
    ppermute x9, starting transfers between devices, send(): lax.ppermute(x, LINE, [(i, (i + step) % LENGTH) for i in range(LENGTH)])  49 us
    all_to_all x3, waiting for transfers between devices, exchange(): return lax.all_to_all(x, axes, 0, 0, tiled=True)  19.9 us
    pallas_call x3, Pallas kernels, product(): pl.pallas_call(product_kernel, out_shape=jax.ShapeDtypeStruct((LENGTH, CO...  15.8 us
    all_to_all x3, starting transfers between devices, exchange(): return lax.all_to_all(x, axes, 0, 0, tiled=True)  14.5 us
    ppermute x4, starting transfers between devices, swap_cores(): return lax.ppermute(x, 'c', [(0, 1), (1, 0)])  13.9 us
    ppermute x9, waiting for transfers between devices, send(): lax.ppermute(x, LINE, [(i, (i + step) % LENGTH) for i in range(LENGTH)])  11.2 us
    unnamed x22, local copies, waits for them, and re-layouts  5.86 us
  transfers between devices with their start and end apart: 16, of which 9 were waited for; matrix products, arithmetic and copies ran while one was open for 1% of the time, Pallas kernels for 0%

profile of v3, /device:TPU:1, one launch (start us, length us, event | category | flops | bytes accessed | tf_op | source)
XLA Modules:
  0.0 226.3 jit_solution(486598205238289406)
XLA Ops:
  0.6 2.6 %dense_panel.1.refs_1_ = bf16[512,1024]{1,0:T(8,128)(2,1)} custom-call(s32[4,8]{1,0:T(4,128)} %bitcast.161, s32[4]{0:T(128)} %bitcast.162, bf16[4,8,128,128]{3,2,1,0:T(8,128)(2,1)} %bitcast.146), custom_call_target="tpu_custom_call" | custom-call | tf_op jit(solution)/shard_map/dense_panel/pallas_call | solution.py:50
  3.2 4.6 %collective-permute-start.3 = (bf16[512,1024]{1,0:T(8,128)(2,1)}, bf16[512,1024]{1,0:T(8,128)(2,1)S(1)}, u32[]{:S(2)}, u32[]{:S(2)}) collective-permute-start(bf16[512,1024]{1,0:T(8,128)(2,1)} %dense_panel.1.refs_1_), channel_id=1, source_target_pairs={{0,1},{1,2},{2,3},{3,4},{4,5},{5,6},{6,7},{7,8},{8,9},{9,10},{10,1... | collective-permute-start | bytes 3145736 | tf_op jit(solution)/shard_map/ppermute | solution.py:25
  7.8 9.5 %collective-permute-start.4 = (bf16[512,1024]{1,0:T(8,128)(2,1)}, bf16[512,1024]{1,0:T(8,128)(2,1)S(1)}, u32[]{:S(2)}, u32[]{:S(2)}) collective-permute-start(bf16[512,1024]{1,0:T(8,128)(2,1)} %dense_panel.1.refs_1_), channel_id=1, source_target_pairs={{0,15},{1,0},{2,1},{3,2},{4,3},{5,4},{6,5},{7,6},{8,7},{9,8},{10,9... | collective-permute-start | bytes 3145736 | tf_op jit(solution)/shard_map/ppermute | solution.py:25
  18.1 4.2 %all-to-all-start = ((bf16[2,32,640]{2,1,0:T(8,128)(2,1)}), bf16[2,32,640]{2,1,0:T(8,128)(2,1)S(1)}, u32[]{:S(2)}, u32[]{:S(2)}) async-start(bf16[2,32,640]{2,1,0:T(8,128)(2,1)} %pad_maximum_fusion.2), calls=%async_computation | async-start | bytes 163840 | tf_op jit(solution)/shard_map/all_to_all | solution.py:21
  25.4 4.6 %collective-permute-start.1 = (bf16[2,32,256]{2,1,0:T(8,128)(2,1)S(1)}, bf16[2,32,256]{2,1,0:T(8,128)(2,1)S(1)}, u32[]{:S(2)}, u32[]{:S(2)}) collective-permute-start(bf16[2,32,256]{2,1,0:T(8,128)(2,1)S(1)} %get-tuple-element.51), channel_id=1, source_target_pairs={{0,15},{1,0},{2,1},{3,2},{4,3},{5,4},{6,5},{7,6},{8,7},{9,8},{10,9... | collective-permute-start | bytes 98312 | tf_op jit(solution)/shard_map/ppermute | solution.py:25
  29.9 2.9 %collective-permute-start.2 = (bf16[2,32,256]{2,1,0:T(8,128)(2,1)S(1)}, bf16[2,32,256]{2,1,0:T(8,128)(2,1)S(1)}, u32[]{:S(2)}, u32[]{:S(2)}) collective-permute-start(bf16[2,32,256]{2,1,0:T(8,128)(2,1)S(1)} %get-tuple-element.52), channel_id=1, source_target_pairs={{0,14},{1,15},{2,0},{3,1},{4,2},{5,3},{6,4},{7,5},{8,6},{9,7},{10,... | collective-permute-start | bytes 98312 | tf_op jit(solution)/shard_map/ppermute | solution.py:25
  32.8 6.4 %collective-permute-done = bf16[2,32,256]{2,1,0:T(8,128)(2,1)S(1)} collective-permute-done((bf16[2,32,256]{2,1,0:T(8,128)(2,1)S(1)}, bf16[2,32,256]{2,1,0:T(8,128)(2,1)S(1)}, u32[]{:S(2)}, u32[]{:S(2)}) %collective-permute-start) | collective-permute-done | bytes 32800 | tf_op jit(solution)/shard_map/ppermute | solution.py:25
  42.9 4.7 %collective-permute-start.5 = (bf16[512,1024]{1,0:T(8,128)(2,1)S(1)}, bf16[512,1024]{1,0:T(8,128)(2,1)}, u32[]{:S(2)}, u32[]{:S(2)}) collective-permute-start(bf16[512,1024]{1,0:T(8,128)(2,1)S(1)} %collective-permute-done.4.refs_2_), channel_id=1, source_target_pairs={{0,15},{1,0},{2,1},{3,2},{4,3},{5,4},{6,5},{7,6},{8,7},{9,8},{10,9... | collective-permute-start | bytes 3145736 | tf_op jit(solution)/shard_map/ppermute | solution.py:25
  47.7 6.8 %all-to-all-start.1 = ((bf16[16,256,128]{2,1,0:T(8,128)(2,1)}), bf16[16,256,128]{2,1,0:T(8,128)(2,1)}, u32[]{:S(2)}, u32[]{:S(2)}) async-start(bf16[16,256,128]{2,1,0:T(8,128)(2,1)} %broadcast_in_dim.40), calls=%async_computation.1 | async-start | bytes 2097152 | tf_op jit(solution)/shard_map/all_to_all | solution.py:21
  54.5 4.3 %collective-permute-start.7 = (bf16[512,1024]{1,0:T(8,128)(2,1)S(1)}, bf16[512,1024]{1,0:T(8,128)(2,1)}, u32[]{:S(2)}, u32[]{:S(2)}) collective-permute-start(bf16[512,1024]{1,0:T(8,128)(2,1)S(1)} %copy-done), channel_id=1, source_target_pairs={{0,16},{16,0},{1,17},{17,1},{2,18},{18,2},{3,19},{19,3},{4,20},{20... | collective-permute-start | bytes 3145736 | tf_op jit(solution)/shard_map/ppermute | solution.py:29
  63.2 6.1 %all-to-all-done.1 = bf16[16,256,128]{2,1,0:T(8,128)(2,1)} async-done(((bf16[16,256,128]{2,1,0:T(8,128)(2,1)}), bf16[16,256,128]{2,1,0:T(8,128)(2,1)}, u32[]{:S(2)}, u32[]{:S(2)}) %all-to-all-start.1) | async-done | bytes 1048608 | tf_op jit(solution)/shard_map/all_to_all | solution.py:21
  69.3 5.3 %collective-permute-start.9 = (bf16[512,1024]{1,0:T(8,128)(2,1)}, bf16[512,1024]{1,0:T(8,128)(2,1)}, u32[]{:S(2)}, u32[]{:S(2)}) collective-permute-start(bf16[512,1024]{1,0:T(8,128)(2,1)} %collective-permute-done.5.refs_3_), channel_id=1, source_target_pairs={{0,16},{16,0},{1,17},{17,1},{2,18},{18,2},{3,19},{19,3},{4,20},{20... | collective-permute-start | bytes 3145736 | tf_op jit(solution)/shard_map/ppermute | solution.py:29
  77.2 5.2 %panel_product.3 = bf16[16,2,32,128]{3,2,1,0:T(8,128)(2,1)S(1)} custom-call(s32[2]{0:T(128)S(1)} %pad_add_fusion.place, bf16[16,4,64,128]{3,2,1,0:T(8,128)(2,1)} %bitcast.10.whole, bf16[512,1024]{1,0:T(8,128)(2,1)S(1)} %collective-permute-done.3.refs_0_, bf16[512,1024]{1,0:T(8,128)(2,1)S(1)} %copy-done, ...), custom_call_target="tpu_custom_call" | custom-call | tf_op jit(solution)/shard_map/panel_product/pallas_call | solution.py:83
  82.4 23.3 %all_to_all.40 = bf16[4,256,128]{2,1,0:T(8,128)(2,1)S(1)} all-to-all(bf16[4,256,128]{2,1,0:T(8,128)(2,1)S(1)} %bitcast.144), channel_id=1, replica_groups=mesh['x'=4,'y'=4,'c'=2,'zh'=4,'zl'=4] {'zh'}, dimensions={0} | all-to-all | bytes 524288 | tf_op jit(solution)/shard_map/all_to_all | solution.py:21
  106.1 15.1 %all_to_all.41 = bf16[16,256,128]{2,1,0:T(8,128)(2,1)S(1)} all-to-all(bf16[16,256,128]{2,1,0:T(8,128)(2,1)S(1)} %broadcast_in_dim.41), channel_id=1, replica_groups=mesh['x'=4,'y'=4,'c'=2,'zh'=4,'zl'=4] {'x','y'}, dimensions={0} | all-to-all | bytes 2097152 | tf_op jit(solution)/shard_map/all_to_all | solution.py:21
  121.2 4.9 %panel_product.4 = bf16[16,2,32,128]{3,2,1,0:T(8,128)(2,1)S(1)} custom-call(s32[2]{0:T(128)S(1)} %pad_add_fusion.place, bf16[16,4,64,128]{3,2,1,0:T(8,128)(2,1)S(1)} %bitcast.143, bf16[512,1024]{1,0:T(8,128)(2,1)S(1)} %collective-permute-done.3.refs_0_, bf16[512,1024]{1,0:T(8,128)(2,1)S(1)} %copy-done, bf16[512,1024]{1,0:T(8,128)(2,1)S(1)} %collective-permute-done.4.refs_2_, ...), custom_call_target="tpu_custom_call" | custom-call | tf_op jit(solution)/shard_map/panel_product/pallas_call | solution.py:83
  126.1 20.6 %all_to_all.42 = bf16[4,256,128]{2,1,0:T(8,128)(2,1)S(1)} all-to-all(bf16[4,256,128]{2,1,0:T(8,128)(2,1)S(1)} %bitcast.145), channel_id=1, replica_groups=mesh['x'=4,'y'=4,'c'=2,'zh'=4,'zl'=4] {'zh'}, dimensions={0} | all-to-all | bytes 524288 | tf_op jit(solution)/shard_map/all_to_all | solution.py:21
  147.1 15.6 %all_to_all.43 = bf16[16,256,128]{2,1,0:T(8,128)(2,1)S(1)} all-to-all(bf16[16,256,128]{2,1,0:T(8,128)(2,1)S(1)} %broadcast_in_dim.42), channel_id=1, replica_groups=mesh['x'=4,'y'=4,'c'=2,'zh'=4,'zl'=4] {'x','y'}, dimensions={0} | all-to-all | bytes 2097152 | tf_op jit(solution)/shard_map/all_to_all | solution.py:21
  162.7 5.7 %panel_product.5 = bf16[16,2,32,128]{3,2,1,0:T(8,128)(2,1)} custom-call(s32[2]{0:T(128)S(1)} %pad_add_fusion.place, bf16[16,4,64,128]{3,2,1,0:T(8,128)(2,1)S(1)} %bitcast.142, bf16[512,1024]{1,0:T(8,128)(2,1)S(1)} %collective-permute-done.3.refs_0_, bf16[512,1024]{1,0:T(8,128)(2,1)S(1)} %copy-done, bf16[512,1024]{1,0:T(8,128)(2,1)S(1)} %collective-permute-done.4.refs_2_, ...), custom_call_target="tpu_custom_call" | custom-call | tf_op jit(solution)/shard_map/panel_product/pallas_call | solution.py:83
  168.4 3.4 %all-to-all-start.6 = ((bf16[4,256,128]{2,1,0:T(8,128)(2,1)}), bf16[4,256,128]{2,1,0:T(8,128)(2,1)S(1)}, u32[]{:S(2)}, u32[]{:S(2)}) async-start(bf16[4,256,128]{2,1,0:T(8,128)(2,1)} %bitcast.20), calls=%async_computation.6 | async-start | bytes 524288 | tf_op jit(solution)/shard_map/all_to_all | solution.py:21
  171.8 12.8 %all-to-all-done.6 = bf16[4,256,128]{2,1,0:T(8,128)(2,1)S(1)} async-done(((bf16[4,256,128]{2,1,0:T(8,128)(2,1)}), bf16[4,256,128]{2,1,0:T(8,128)(2,1)S(1)}, u32[]{:S(2)}, u32[]{:S(2)}) %all-to-all-start.6) | async-done | bytes 262176 | tf_op jit(solution)/shard_map/all_to_all | solution.py:21
  184.8 15.0 %collective-permute-start.10 = (bf16[2,3,32,128]{3,2,1,0:T(8,128)(2,1)S(1)}, bf16[2,3,32,128]{3,2,1,0:T(8,128)(2,1)S(1)}, u32[]{:S(2)}, u32[]{:S(2)}) collective-permute-start(bf16[2,3,32,128]{3,2,1,0:T(8,128)(2,1)S(1)} %get-tuple-element.41), channel_id=1, source_target_pairs={{0,15},{1,0},{2,1},{3,2},{4,3},{5,4},{6,5},{7,6},{8,7},{9,8},{10,9... | collective-permute-start | bytes 147464 | tf_op jit(solution)/shard_map/ppermute | solution.py:25
  202.3 3.4 %collective-permute-start.12 = (bf16[2,3,32,128]{3,2,1,0:T(8,128)(2,1)S(1)}, bf16[2,3,32,128]{3,2,1,0:T(8,128)(2,1)S(1)}, u32[]{:S(2)}, u32[]{:S(2)}) collective-permute-start(bf16[2,3,32,128]{3,2,1,0:T(8,128)(2,1)S(1)} %get-tuple-element.39), channel_id=1, source_target_pairs={{0,1},{1,2},{2,3},{3,4},{4,5},{5,6},{6,7},{7,8},{8,9},{9,10},{10,1... | collective-permute-start | bytes 147464 | tf_op jit(solution)/shard_map/ppermute | solution.py:25
  208.3 11.5 %all_to_all.44 = bf16[2,4,3,32,128]{4,3,2,1,0:T(8,128)(2,1)S(1)} all-to-all(bf16[2,4,3,32,128]{4,3,2,1,0:T(8,128)(2,1)S(1)} %bitcast.150), channel_id=1, replica_groups=mesh['x'=4,'y'=4,'c'=2,'zh'=4,'zl'=4] {'c'}, dimensions={0} | all-to-all | bytes 393216 | tf_op jit(solution)/shard_map/all_to_all | solution.py:21
  (67 shorter events, 26.9 us)
Async XLA Ops:
  0.6 16.7 %copy-start.2 = (bf16[32,1024]{1,0:T(8,128)(2,1)S(1)}, bf16[32,1024]{1,0:T(8,128)(2,1)}, u32[]{:S(2)}) copy-start(bf16[32,1024]{1,0:T(8,128)(2,1)} %param.5) | copy-start | bytes 196612
  3.2 14.1 %copy-start.6 = (s32[32]{0:T(128)S(1)}, s32[32]{0:T(128)}, u32[]{:S(2)}) copy-start(s32[32]{0:T(128)} %param.6) | copy-start | bytes 388
  3.2 38.5 %collective-permute-start.3 = (bf16[512,1024]{1,0:T(8,128)(2,1)}, bf16[512,1024]{1,0:T(8,128)(2,1)S(1)}, u32[]{:S(2)}, u32[]{:S(2)}) collective-permute-start(bf16[512,1024]{1,0:T(8,128)(2,1)} %dense_panel.1.refs_1_), channel_id=1, source_target_pairs={{0,1},{1,2},{2,3},{3,4},{4,5},{5,6},{6,7},{7,8},{8,9},{9,10},{10,1... | collective-permute-start | bytes 3145736 | tf_op jit(solution)/shard_map/ppermute | solution.py:25
  7.8 33.9 %collective-permute-start.4 = (bf16[512,1024]{1,0:T(8,128)(2,1)}, bf16[512,1024]{1,0:T(8,128)(2,1)S(1)}, u32[]{:S(2)}, u32[]{:S(2)}) collective-permute-start(bf16[512,1024]{1,0:T(8,128)(2,1)} %dense_panel.1.refs_1_), channel_id=1, source_target_pairs={{0,15},{1,0},{2,1},{3,2},{4,3},{5,4},{6,5},{7,6},{8,7},{9,8},{10,9... | collective-permute-start | bytes 3145736 | tf_op jit(solution)/shard_map/ppermute | solution.py:25
  18.1 5.3 %all-to-all-start = ((bf16[2,32,640]{2,1,0:T(8,128)(2,1)}), bf16[2,32,640]{2,1,0:T(8,128)(2,1)S(1)}, u32[]{:S(2)}, u32[]{:S(2)}) async-start(bf16[2,32,640]{2,1,0:T(8,128)(2,1)} %pad_maximum_fusion.2), calls=%async_computation | async-start | bytes 163840 | tf_op jit(solution)/shard_map/all_to_all | solution.py:21
  23.4 15.8 %collective-permute-start = (bf16[2,32,256]{2,1,0:T(8,128)(2,1)S(1)}, bf16[2,32,256]{2,1,0:T(8,128)(2,1)S(1)}, u32[]{:S(2)}, u32[]{:S(2)}) collective-permute-start(bf16[2,32,256]{2,1,0:T(8,128)(2,1)S(1)} %get-tuple-element.49), channel_id=1, source_target_pairs={{0,1},{1,2},{2,3},{3,4},{4,5},{5,6},{6,7},{7,8},{8,9},{9,10},{10,1... | collective-permute-start | bytes 98312 | tf_op jit(solution)/shard_map/ppermute | solution.py:25
  25.4 15.4 %collective-permute-start.1 = (bf16[2,32,256]{2,1,0:T(8,128)(2,1)S(1)}, bf16[2,32,256]{2,1,0:T(8,128)(2,1)S(1)}, u32[]{:S(2)}, u32[]{:S(2)}) collective-permute-start(bf16[2,32,256]{2,1,0:T(8,128)(2,1)S(1)} %get-tuple-element.51), channel_id=1, source_target_pairs={{0,15},{1,0},{2,1},{3,2},{4,3},{5,4},{6,5},{7,6},{8,7},{9,8},{10,9... | collective-permute-start | bytes 98312 | tf_op jit(solution)/shard_map/ppermute | solution.py:25
  29.9 11.5 %collective-permute-start.2 = (bf16[2,32,256]{2,1,0:T(8,128)(2,1)S(1)}, bf16[2,32,256]{2,1,0:T(8,128)(2,1)S(1)}, u32[]{:S(2)}, u32[]{:S(2)}) collective-permute-start(bf16[2,32,256]{2,1,0:T(8,128)(2,1)S(1)} %get-tuple-element.52), channel_id=1, source_target_pairs={{0,14},{1,15},{2,0},{3,1},{4,2},{5,3},{6,4},{7,5},{8,6},{9,7},{10,... | collective-permute-start | bytes 98312 | tf_op jit(solution)/shard_map/ppermute | solution.py:25
  42.9 11.6 %copy-start = (bf16[512,1024]{1,0:T(8,128)(2,1)S(1)}, bf16[512,1024]{1,0:T(8,128)(2,1)}, u32[]{:S(2)}) copy-start(bf16[512,1024]{1,0:T(8,128)(2,1)} %dense_panel.1.refs_1_) | copy-start | bytes 3145732
  42.9 26.3 %collective-permute-start.5 = (bf16[512,1024]{1,0:T(8,128)(2,1)S(1)}, bf16[512,1024]{1,0:T(8,128)(2,1)}, u32[]{:S(2)}, u32[]{:S(2)}) collective-permute-start(bf16[512,1024]{1,0:T(8,128)(2,1)S(1)} %collective-permute-done.4.refs_2_), channel_id=1, source_target_pairs={{0,15},{1,0},{2,1},{3,2},{4,3},{5,4},{6,5},{7,6},{8,7},{9,8},{10,9... | collective-permute-start | bytes 3145736 | tf_op jit(solution)/shard_map/ppermute | solution.py:25
  47.7 21.6 %all-to-all-start.1 = ((bf16[16,256,128]{2,1,0:T(8,128)(2,1)}), bf16[16,256,128]{2,1,0:T(8,128)(2,1)}, u32[]{:S(2)}, u32[]{:S(2)}) async-start(bf16[16,256,128]{2,1,0:T(8,128)(2,1)} %broadcast_in_dim.40), calls=%async_computation.1 | async-start | bytes 2097152 | tf_op jit(solution)/shard_map/all_to_all | solution.py:21
  54.5 20.1 %collective-permute-start.7 = (bf16[512,1024]{1,0:T(8,128)(2,1)S(1)}, bf16[512,1024]{1,0:T(8,128)(2,1)}, u32[]{:S(2)}, u32[]{:S(2)}) collective-permute-start(bf16[512,1024]{1,0:T(8,128)(2,1)S(1)} %copy-done), channel_id=1, source_target_pairs={{0,16},{16,0},{1,17},{17,1},{2,18},{18,2},{3,19},{19,3},{4,20},{20... | collective-permute-start | bytes 3145736 | tf_op jit(solution)/shard_map/ppermute | solution.py:29
  58.9 15.8 %collective-permute-start.6 = (bf16[512,1024]{1,0:T(8,128)(2,1)S(1)}, bf16[512,1024]{1,0:T(8,128)(2,1)}, u32[]{:S(2)}, u32[]{:S(2)}) collective-permute-start(bf16[512,1024]{1,0:T(8,128)(2,1)S(1)} %collective-permute-done.3.refs_0_), channel_id=1, source_target_pairs={{0,16},{16,0},{1,17},{17,1},{2,18},{18,2},{3,19},{19,3},{4,20},{20... | collective-permute-start | bytes 3145736 | tf_op jit(solution)/shard_map/ppermute | solution.py:29
  60.8 13.9 %collective-permute-start.8 = (bf16[512,1024]{1,0:T(8,128)(2,1)S(1)}, bf16[512,1024]{1,0:T(8,128)(2,1)}, u32[]{:S(2)}, u32[]{:S(2)}) collective-permute-start(bf16[512,1024]{1,0:T(8,128)(2,1)S(1)} %collective-permute-done.4.refs_2_), channel_id=1, source_target_pairs={{0,16},{16,0},{1,17},{17,1},{2,18},{18,2},{3,19},{19,3},{4,20},{20... | collective-permute-start | bytes 3145736 | tf_op jit(solution)/shard_map/ppermute | solution.py:29
  69.3 7.9 %collective-permute-start.9 = (bf16[512,1024]{1,0:T(8,128)(2,1)}, bf16[512,1024]{1,0:T(8,128)(2,1)}, u32[]{:S(2)}, u32[]{:S(2)}) collective-permute-start(bf16[512,1024]{1,0:T(8,128)(2,1)} %collective-permute-done.5.refs_3_), channel_id=1, source_target_pairs={{0,16},{16,0},{1,17},{17,1},{2,18},{18,2},{3,19},{19,3},{4,20},{20... | collective-permute-start | bytes 3145736 | tf_op jit(solution)/shard_map/ppermute | solution.py:29
  168.4 16.2 %all-to-all-start.6 = ((bf16[4,256,128]{2,1,0:T(8,128)(2,1)}), bf16[4,256,128]{2,1,0:T(8,128)(2,1)S(1)}, u32[]{:S(2)}, u32[]{:S(2)}) async-start(bf16[4,256,128]{2,1,0:T(8,128)(2,1)} %bitcast.20), calls=%async_computation.6 | async-start | bytes 524288 | tf_op jit(solution)/shard_map/all_to_all | solution.py:21
  184.8 20.9 %collective-permute-start.10 = (bf16[2,3,32,128]{3,2,1,0:T(8,128)(2,1)S(1)}, bf16[2,3,32,128]{3,2,1,0:T(8,128)(2,1)S(1)}, u32[]{:S(2)}, u32[]{:S(2)}) collective-permute-start(bf16[2,3,32,128]{3,2,1,0:T(8,128)(2,1)S(1)} %get-tuple-element.41), channel_id=1, source_target_pairs={{0,15},{1,0},{2,1},{3,2},{4,3},{5,4},{6,5},{7,6},{8,7},{9,8},{10,9... | collective-permute-start | bytes 147464 | tf_op jit(solution)/shard_map/ppermute | solution.py:25
  199.8 6.9 %collective-permute-start.11 = (bf16[2,3,32,128]{3,2,1,0:T(8,128)(2,1)S(1)}, bf16[2,3,32,128]{3,2,1,0:T(8,128)(2,1)S(1)}, u32[]{:S(2)}, u32[]{:S(2)}) collective-permute-start(bf16[2,3,32,128]{3,2,1,0:T(8,128)(2,1)S(1)} %get-tuple-element.40), channel_id=1, source_target_pairs={{0,2},{1,3},{2,4},{3,5},{4,6},{5,7},{6,8},{7,9},{8,10},{9,11},{10,... | collective-permute-start | bytes 147464 | tf_op jit(solution)/shard_map/ppermute | solution.py:25
  202.3 6.0 %collective-permute-start.12 = (bf16[2,3,32,128]{3,2,1,0:T(8,128)(2,1)S(1)}, bf16[2,3,32,128]{3,2,1,0:T(8,128)(2,1)S(1)}, u32[]{:S(2)}, u32[]{:S(2)}) collective-permute-start(bf16[2,3,32,128]{3,2,1,0:T(8,128)(2,1)S(1)} %get-tuple-element.39), channel_id=1, source_target_pairs={{0,1},{1,2},{2,3},{3,4},{4,5},{5,6},{6,7},{7,8},{8,9},{9,10},{10,1... | collective-permute-start | bytes 147464 | tf_op jit(solution)/shard_map/ppermute | solution.py:25
  219.8 0.7 copy-start.1
  225.7 0.6 copy-start.3
  225.7 0.6 copy-start.4
  225.7 0.7 copy-start.5

commit v4 on v3

v4 whole, which is shorter than its diff:
```python
import jax
import jax.numpy as jnp
from jax import lax
from jax.experimental import pallas as pl
from jax.experimental.pallas import tpu as pltpu
from jax.sharding import Mesh, PartitionSpec as P

HOPS = 3
SIZES = {"x": 4, "y": 4, "c": 2, "zhalf": 2, "zquad": 4, "zodd": 2}
PLANE = ("x", "y")
LINE = ("zhalf", "zquad", "zodd")
POOL = ("zodd", "c")
PAIRS = 8
GROUPS = [
    [2 * k + (s if k < PAIRS // 2 else 1 - s) for k in range(PAIRS)] for s in range(2)
]
LANES = 128
VMEM = pl.BlockSpec(memory_space=pltpu.VMEM)
SMEM = pl.BlockSpec(memory_space=pltpu.SMEM)


def exchange(x, axes, groups=None):
    return lax.all_to_all(x, axes, 0, 0, tiled=True, axis_index_groups=groups)


def swap(x, axis):
    return lax.ppermute(x, axis, [(0, 1), (1, 0)])


def after(x, *others):
    return lax.optimization_barrier((x,) + others)[0]


def dense_kernel(cols, counts, blocks, out):
    out[...] = jnp.zeros_like(out)
    row_blocks, slots, size, _ = blocks.shape
    for g in range(row_blocks):
        for t in range(slots):

            @pl.when(t < counts[g])
            def _():
                at = pl.multiple_of(cols[g, t] * size, size)
                out[g * size : (g + 1) * size, pl.ds(at, size)] = blocks[g, t]


def build_dense(blocks, cols, counts):
    g, t, size, _ = blocks.shape
    return pl.pallas_call(
        dense_kernel,
        out_shape=jax.ShapeDtypeStruct((g * size, t * size), blocks.dtype),
        in_specs=[SMEM, SMEM, VMEM],
        out_specs=VMEM,
        compiler_params=pltpu.CompilerParams(vmem_limit_bytes=8 << 20),
        name="dense_panel",
    )(cols, counts, blocks)


def product_kernel(place, whole, a00, a01, a10, a11, out, columns):
    core, level = place[0], place[1]
    plane, pair, rows, width = whole.shape
    for j in range(plane):
        for z in range(pair):
            columns[z, j] = whole[j, z]
    for near, (ours, theirs) in enumerate(((a00, a01), (a10, a11))):
        value = jnp.dot(
            ours[...], columns[level].reshape(-1, width), preferred_element_type=jnp.float32
        )
        value += jnp.dot(
            theirs[...], columns[1 - level].reshape(-1, width), preferred_element_type=jnp.float32
        )
        value = value.astype(jnp.bfloat16).reshape(PAIRS, pair, rows // 2, width)
        target = core if near == 0 else 1 - core
        for z in range(pair):
            out[:, z, target] = value[:, z]


def product(place, whole, panels):
    plane, pair, rows, width = whole.shape
    return pl.pallas_call(
        product_kernel,
        out_shape=jax.ShapeDtypeStruct((PAIRS, pair, 2, rows // 2, width), jnp.bfloat16),
        in_specs=[SMEM] + [VMEM] * 5,
        out_specs=VMEM,
        scratch_shapes=[pltpu.VMEM((pair, plane, rows, width), jnp.bfloat16)],
        compiler_params=pltpu.CompilerParams(vmem_limit_bytes=14 << 20),
        name="panel_product",
    )(place, whole, *panels)


def on_device(features, degree, blocks, block_cols, block_count):
    f32, bf16 = jnp.float32, jnp.bfloat16
    rows, full = features.shape
    width = full // 4
    pooled = 4 * rows
    plane = SIZES["x"] * SIZES["y"]
    place = jnp.stack([lax.axis_index("c"), lax.axis_index("zodd")]).astype(jnp.int32)
    crossed = lax.axis_index("zhalf") == 1

    counts = jnp.broadcast_to(degree.astype(bf16)[:, None], (rows, LANES))
    slices = jnp.stack(
        [
            jnp.concatenate([features[:, q * width : (q + 1) * width], counts], axis=1)
            for q in range(4)
        ]
    )
    slices = jnp.where(crossed, jnp.roll(slices, 2, axis=0), slices)
    got = exchange(slices, POOL).reshape(pooled, width + LANES)
    scale = lax.rsqrt(got[:, width : width + 1].astype(f32))
    sent = (scale * got[:, :width].astype(f32)).astype(bf16)
    copies = jnp.broadcast_to(sent[None], (plane,) + sent.shape)
    whole = exchange(copies, PLANE)

    blocks, block_cols = lax.optimization_barrier((blocks, block_cols, slices))[:2]
    a00 = build_dense(blocks[:, 0], block_cols[:, 0], block_count[:, 0])
    a01 = swap(a00, "zodd")
    a10 = swap(a00, "c")
    a11 = swap(after(a01, whole), "c")
    panels = (a00, a01, a10, a11)

    hops = []
    for hop in range(HOPS):
        if hop:
            copies = jnp.broadcast_to(sent[None], (plane,) + sent.shape)
            whole = exchange(copies, PLANE)
        partial_value = product(place, whole.reshape(plane, 2, 2 * rows, width), panels)
        parts = exchange(partial_value.reshape(PAIRS, pooled, width), LINE, GROUPS)
        total = jnp.sum(parts.astype(f32), axis=0)
        value = (scale * (total + sent.astype(f32))).astype(bf16)
        sent = (scale * value.astype(f32)).astype(bf16)
        hops.append(value.reshape(4, rows, width))
    back = exchange(jnp.stack(hops, axis=1), POOL)
    back = jnp.where(crossed, jnp.roll(back, 2, axis=0), back)
    return tuple(
        back[:, k].transpose(1, 0, 2).reshape(rows, full) for k in range(HOPS)
    )


def solution(mesh):
    axes = tuple(SIZES)
    fine = Mesh(mesh.devices.reshape(tuple(SIZES.values())), axes)
    in_specs = (
        P(axes, None),
        P(axes),
        P(axes[:3], axes[3:], None, None, None),
        P(axes[:3], axes[3:], None),
        P(axes[:3], axes[3:]),
    )
    out_specs = (P(axes, None),) * 3
    return jax.shard_map(
        on_device, mesh=fine, in_specs=in_specs, out_specs=out_specs, check_vma=False
    )
```

time: 228 us -> 218 us (0.956)
  blocking collectives: 86.1 us -> 158 us
  starting transfers between devices: 77.4 us -> 23.3 us
  waiting for transfers between devices: 33.6 us -> 17.4 us
  Pallas kernels: 18.4 us -> 8.96 us
    all_to_all x5 -> x6, blocking collectives: 86.1 us -> 158 us  [exchange(): return lax.all_to_all(x, axes, 0, 0, tiled=True, axis_index_groups=groups)]
    ppermute x13 -> x3, starting transfers between devices: 63 us -> 8.86 us  [swap(): return lax.ppermute(x, axis, [(0, 1), (1, 0)])]
    all_to_all x3 -> x2, waiting for transfers between devices: 19.9 us -> 0.01 us  [exchange(): return lax.all_to_all(x, axes, 0, 0, tiled=True, axis_index_groups=groups)]
    pallas_call x3, Pallas kernels: 15.8 us -> 8.02 us  [product(): pl.pallas_call(product_kernel, out_shape=jax.ShapeDtypeStruct((PAIRS, pai...]
    ppermute x13 -> x3, waiting for transfers between devices: 13.7 us -> 17.4 us  [swap(): return lax.ppermute(x, axis, [(0, 1), (1, 0)])]
    unnamed x22 -> x9, local copies, waits for them, and re-layouts: 5.86 us -> 2.57 us
    all_to_all x3 -> x2, starting transfers between devices: 14.5 us -> 14.5 us  [exchange(): return lax.all_to_all(x, axes, 0, 0, tiled=True, axis_index_groups=groups)]
  transfers between devices with their start and end apart: 16 -> 5, of which waited for: 9 -> 2; matrix products, arithmetic and copies ran while one was open for 1% -> 1% of each run, Pallas kernels for 0% -> 0%
where the time goes in v4:
time: 218 us; the launch traced here: 217 us
  blocking collectives  158 us (72%)
  starting transfers between devices  23.3 us (11%)
  waiting for transfers between devices  17.4 us (8%)
  Pallas kernels  8.96 us (4%)
  local copies, waits for them, and re-layouts  6.66 us (3%)
    all_to_all x6, blocking collectives, exchange(): return lax.all_to_all(x, axes, 0, 0, tiled=True, axis_index_groups=groups)  158 us
    ppermute x3, waiting for transfers between devices, swap(): return lax.ppermute(x, axis, [(0, 1), (1, 0)])  17.4 us
    all_to_all x2, starting transfers between devices, exchange(): return lax.all_to_all(x, axes, 0, 0, tiled=True, axis_index_groups=groups)  14.5 us
    ppermute x3, starting transfers between devices, swap(): return lax.ppermute(x, axis, [(0, 1), (1, 0)])  8.86 us
    pallas_call x3, Pallas kernels, product(): pl.pallas_call(product_kernel, out_shape=jax.ShapeDtypeStruct((PAIRS, pai...  8.02 us
  transfers between devices with their start and end apart: 5, of which 2 were waited for; matrix products, arithmetic and copies ran while one was open for 1% of the time, Pallas kernels for 0%

profile of v4, /device:TPU:1, one launch (start us, length us, event | category | flops | bytes accessed | tf_op | source)
XLA Modules:
  0.0 216.9 jit_solution(177567350093161818)
XLA Ops:
  0.6 0.6 copy-done.3
  1.3 0.8 fusion.5
  2.2 0.7 maximum_select_fusion.1
  2.8 10.1 %all-to-all-start = ((bf16[4,32,384]{2,1,0:T(8,128)(2,1)}), bf16[4,32,384]{2,1,0:T(8,128)(2,1)S(1)}, u32[]{:S(2)}, u32[]{:S(2)}) async-start(bf16[4,32,384]{2,1,0:T(8,128)(2,1)} %maximum_select_fusion.1), calls=%async_computation | async-start | bytes 196608 | tf_op jit(solution)/shard_map/all_to_all | solution.py:23
  13.0 0.7 copy-done.1
  13.7 1.2 copy-done
  14.9 0.9 dense_panel.1.a00
  15.8 3.3 %collective-permute-start = (bf16[512,1024]{1,0:T(8,128)(2,1)S(1)}, bf16[512,1024]{1,0:T(8,128)(2,1)S(1)}, u32[]{:S(2)}, u32[]{:S(2)}) collective-permute-start(bf16[512,1024]{1,0:T(8,128)(2,1)S(1)} %dense_panel.1.a00), channel_id=1, source_target_pairs={{0,1},{1,0},{2,3},{3,2},{4,5},{5,4},{6,7},{7,6},{8,9},{9,8},{10,11... | collective-permute-start | bytes 3145736 | tf_op jit(solution)/shard_map/ppermute | solution.py:27
  19.4 1.1 broadcast_in_dim.9
  20.5 4.3 %all-to-all-start.1 = ((bf16[16,128,256]{2,1,0:T(8,128)(2,1)}), bf16[16,128,256]{2,1,0:T(8,128)(2,1)}, u32[]{:S(2)}, u32[]{:S(2)}) async-start(bf16[16,128,256]{2,1,0:T(8,128)(2,1)} %broadcast_in_dim.9), calls=%async_computation.1 | async-start | bytes 2097152 | tf_op jit(solution)/shard_map/all_to_all | solution.py:23
  24.8 2.6 %collective-permute-start.1 = (bf16[512,1024]{1,0:T(8,128)(2,1)S(1)}, bf16[512,1024]{1,0:T(8,128)(2,1)S(1)}, u32[]{:S(2)}, u32[]{:S(2)}) collective-permute-start(bf16[512,1024]{1,0:T(8,128)(2,1)S(1)} %dense_panel.1.a00), channel_id=1, source_target_pairs={{0,16},{16,0},{1,17},{17,1},{2,18},{18,2},{3,19},{19,3},{4,20},{20... | collective-permute-start | bytes 3145736 | tf_op jit(solution)/shard_map/ppermute | solution.py:27
  27.4 15.1 %collective-permute-done.a01 = bf16[512,1024]{1,0:T(8,128)(2,1)S(1)} collective-permute-done((bf16[512,1024]{1,0:T(8,128)(2,1)S(1)}, bf16[512,1024]{1,0:T(8,128)(2,1)S(1)}, u32[]{:S(2)}, u32[]{:S(2)}) %collective-permute-start) | collective-permute-done | bytes 1048608 | tf_op jit(solution)/shard_map/ppermute | solution.py:27
  42.5 3.0 %collective-permute-start.2 = (bf16[512,1024]{1,0:T(8,128)(2,1)S(1)}, bf16[512,1024]{1,0:T(8,128)(2,1)}, u32[]{:S(2)}, u32[]{:S(2)}) collective-permute-start(bf16[512,1024]{1,0:T(8,128)(2,1)S(1)} %collective-permute-done.a01), channel_id=1, source_target_pairs={{0,16},{16,0},{1,17},{17,1},{2,18},{18,2},{3,19},{19,3},{4,20},{20... | collective-permute-start | bytes 3145736 | tf_op jit(solution)/shard_map/ppermute | solution.py:27
  45.6 2.3 %collective-permute-done.2.a11 = bf16[512,1024]{1,0:T(8,128)(2,1)} collective-permute-done((bf16[512,1024]{1,0:T(8,128)(2,1)S(1)}, bf16[512,1024]{1,0:T(8,128)(2,1)}, u32[]{:S(2)}, u32[]{:S(2)}) %collective-permute-start.2) | collective-permute-done | bytes 1048608 | tf_op jit(solution)/shard_map/ppermute | solution.py:27
  47.9 2.9 %panel_product.3 = bf16[8,2,2,32,256]{4,3,2,1,0:T(8,128)(2,1)S(1)} custom-call(s32[2]{0:T(128)S(1)} %pad_add_fusion.place, bf16[16,2,64,256]{3,2,1,0:T(8,128)(2,1)} %bitcast.7.whole, bf16[512,1024]{1,0:T(8,128)(2,1)S(1)} %dense_panel.1.a00, bf16[512,1024]{1,0:T(8,128)(2,1)S(1)} %collective-permute-done.a01, ...), custom_call_target="tpu_custom_call" | custom-call | tf_op jit(solution)/shard_map/panel_product/pallas_call | solution.py:79
  50.8 32.9 %all_to_all.40 = bf16[8,128,256]{2,1,0:T(8,128)(2,1)S(1)} all-to-all(bf16[8,128,256]{2,1,0:T(8,128)(2,1)S(1)} %bitcast.44), channel_id=1, replica_groups={{0,2,4,6,9,11,13,15},{1,3,5,7,8,10,12,14},{16,18,20,22,25,27,29,31},{17..., dimensions={0} | all-to-all | bytes 1048576 | tf_op jit(solution)/shard_map/all_to_all | solution.py:23
  83.9 31.3 %all_to_all.41 = bf16[16,128,256]{2,1,0:T(8,128)(2,1)S(1)} all-to-all(bf16[16,128,256]{2,1,0:T(8,128)(2,1)S(1)} %broadcast_in_dim.10), channel_id=1, replica_groups=mesh['x'=4,'y'=4,'c'=2,'zhalf'=2,'zquad'=4,'zodd'=2] {'x','y'}, dimensions={0} | all-to-all | bytes 2097152 | tf_op jit(solution)/shard_map/all_to_all | solution.py:23
  115.2 2.6 %panel_product.4 = bf16[8,2,2,32,256]{4,3,2,1,0:T(8,128)(2,1)S(1)} custom-call(s32[2]{0:T(128)S(1)} %pad_add_fusion.place, bf16[16,2,64,256]{3,2,1,0:T(8,128)(2,1)S(1)} %bitcast.42, bf16[512,1024]{1,0:T(8,128)(2,1)S(1)} %dense_panel.1.a00, bf16[512,1024]{1,0:T(8,128)(2,1)S(1)} %collective-permute-done.a01, bf16[512,1024]{1,0:T(8,128)(2,1)S(1)} %collective-permute-done.1.a10, ...), custom_call_target="tpu_custom_call" | custom-call | tf_op jit(solution)/shard_map/panel_product/pallas_call | solution.py:79
  117.8 31.2 %all_to_all.42 = bf16[8,128,256]{2,1,0:T(8,128)(2,1)S(1)} all-to-all(bf16[8,128,256]{2,1,0:T(8,128)(2,1)S(1)} %bitcast.45), channel_id=1, replica_groups={{0,2,4,6,9,11,13,15},{1,3,5,7,8,10,12,14},{16,18,20,22,25,27,29,31},{17..., dimensions={0} | all-to-all | bytes 1048576 | tf_op jit(solution)/shard_map/all_to_all | solution.py:23
  149.3 17.8 %all_to_all.43 = bf16[16,128,256]{2,1,0:T(8,128)(2,1)S(1)} all-to-all(bf16[16,128,256]{2,1,0:T(8,128)(2,1)S(1)} %broadcast_in_dim.11), channel_id=1, replica_groups=mesh['x'=4,'y'=4,'c'=2,'zhalf'=2,'zquad'=4,'zodd'=2] {'x','y'}, dimensions={0} | all-to-all | bytes 2097152 | tf_op jit(solution)/shard_map/all_to_all | solution.py:23
  167.0 2.6 %panel_product.5 = bf16[8,2,2,32,256]{4,3,2,1,0:T(8,128)(2,1)S(1)} custom-call(s32[2]{0:T(128)S(1)} %pad_add_fusion.place, bf16[16,2,64,256]{3,2,1,0:T(8,128)(2,1)S(1)} %bitcast.41, bf16[512,1024]{1,0:T(8,128)(2,1)S(1)} %dense_panel.1.a00, bf16[512,1024]{1,0:T(8,128)(2,1)S(1)} %collective-permute-done.a01, bf16[512,1024]{1,0:T(8,128)(2,1)S(1)} %collective-permute-done.1.a10, ...), custom_call_target="tpu_custom_call" | custom-call | tf_op jit(solution)/shard_map/panel_product/pallas_call | solution.py:79
  169.6 34.5 %all_to_all.44 = bf16[8,128,256]{2,1,0:T(8,128)(2,1)S(1)} all-to-all(bf16[8,128,256]{2,1,0:T(8,128)(2,1)S(1)} %bitcast.43), channel_id=1, replica_groups={{0,2,4,6,9,11,13,15},{1,3,5,7,8,10,12,14},{16,18,20,22,25,27,29,31},{17..., dimensions={0} | all-to-all | bytes 1048576 | tf_op jit(solution)/shard_map/all_to_all | solution.py:23
  204.3 10.6 %all_to_all.45 = bf16[4,3,32,256]{3,2,1,0:T(8,128)(2,1)S(1)} all-to-all(bf16[4,3,32,256]{3,2,1,0:T(8,128)(2,1)S(1)} %copy.12), channel_id=1, replica_groups=mesh['x'=4,'y'=4,'c'=2,'zhalf'=2,'zquad'=4,'zodd'=2] {'zodd','c'}, dimensions={0} | all-to-all | bytes 393216 | tf_op jit(solution)/shard_map/all_to_all | solution.py:23
  215.0 0.6 copy.18
  (29 shorter events, 2.4 us)
Async XLA Ops:
  0.6 0.7 copy-start.3
  2.8 16.3 %all-to-all-start = ((bf16[4,32,384]{2,1,0:T(8,128)(2,1)}), bf16[4,32,384]{2,1,0:T(8,128)(2,1)S(1)}, u32[]{:S(2)}, u32[]{:S(2)}) async-start(bf16[4,32,384]{2,1,0:T(8,128)(2,1)} %maximum_select_fusion.1), calls=%async_computation | async-start | bytes 196608 | tf_op jit(solution)/shard_map/all_to_all | solution.py:23
  13.0 0.7 copy-start.1
  13.0 0.7 copy-start.2
  13.7 1.2 copy-start
  15.8 26.7 %collective-permute-start = (bf16[512,1024]{1,0:T(8,128)(2,1)S(1)}, bf16[512,1024]{1,0:T(8,128)(2,1)S(1)}, u32[]{:S(2)}, u32[]{:S(2)}) collective-permute-start(bf16[512,1024]{1,0:T(8,128)(2,1)S(1)} %dense_panel.1.a00), channel_id=1, source_target_pairs={{0,1},{1,0},{2,3},{3,2},{4,5},{5,4},{6,7},{7,6},{8,9},{9,8},{10,11... | collective-permute-start | bytes 3145736 | tf_op jit(solution)/shard_map/ppermute | solution.py:27
  20.5 22.0 %all-to-all-start.1 = ((bf16[16,128,256]{2,1,0:T(8,128)(2,1)}), bf16[16,128,256]{2,1,0:T(8,128)(2,1)}, u32[]{:S(2)}, u32[]{:S(2)}) async-start(bf16[16,128,256]{2,1,0:T(8,128)(2,1)} %broadcast_in_dim.9), calls=%async_computation.1 | async-start | bytes 2097152 | tf_op jit(solution)/shard_map/all_to_all | solution.py:23
  24.8 20.7 %collective-permute-start.1 = (bf16[512,1024]{1,0:T(8,128)(2,1)S(1)}, bf16[512,1024]{1,0:T(8,128)(2,1)S(1)}, u32[]{:S(2)}, u32[]{:S(2)}) collective-permute-start(bf16[512,1024]{1,0:T(8,128)(2,1)S(1)} %dense_panel.1.a00), channel_id=1, source_target_pairs={{0,16},{16,0},{1,17},{17,1},{2,18},{18,2},{3,19},{19,3},{4,20},{20... | collective-permute-start | bytes 3145736 | tf_op jit(solution)/shard_map/ppermute | solution.py:27
  42.5 5.4 %collective-permute-start.2 = (bf16[512,1024]{1,0:T(8,128)(2,1)S(1)}, bf16[512,1024]{1,0:T(8,128)(2,1)}, u32[]{:S(2)}, u32[]{:S(2)}) collective-permute-start(bf16[512,1024]{1,0:T(8,128)(2,1)S(1)} %collective-permute-done.a01), channel_id=1, source_target_pairs={{0,16},{16,0},{1,17},{17,1},{2,18},{18,2},{3,19},{19,3},{4,20},{20... | collective-permute-start | bytes 3145736 | tf_op jit(solution)/shard_map/ppermute | solution.py:27

commit v5 on v4

--- a/solution.py
+++ b/solution.py
@@ -6,15 +6,33 @@
 from jax.sharding import Mesh, PartitionSpec as P
 
 HOPS = 3
-SIZES = {"x": 4, "y": 4, "c": 2, "zhalf": 2, "zquad": 4, "zodd": 2}
+SIZES = {"x": 4, "y": 4, "c": 2, "z": 16}
 PLANE = ("x", "y")
-LINE = ("zhalf", "zquad", "zodd")
-POOL = ("zodd", "c")
-PAIRS = 8
-GROUPS = [
-    [2 * k + (s if k < PAIRS // 2 else 1 - s) for k in range(PAIRS)] for s in range(2)
+LENGTH = 16
+TILES = LENGTH // 2
+STEP = 4
+TILE_GROUPS = [
+    [core * LENGTH + 2 * k + level for level in range(2) for core in range(2)] for k in range(TILES)
 ]
+NEIGHBOURS = [(z, (z + 1 if z % 2 else z - 1) % LENGTH) for z in range(LENGTH)]
+SUM_GROUPS = [
+    [(STEP * k + first + (side if k < STEP // 2 else 1 - side)) % LENGTH for k in range(STEP)]
+    for first in (1, 3)
+    for side in range(2)
+]
+
+
+def tile_places():
+    group_of = {z: group for group in SUM_GROUPS for z in group}
+    return [
+        [[z // 2 for z in group_of[me] + group_of[other]].index(k) for k in range(TILES)]
+        for me, other in NEIGHBOURS
+    ]
+
+
 LANES = 128
+CORES = [(0, 1), (1, 0)]
+LEVELS = [(z, z ^ 1) for z in range(LENGTH)]
 VMEM = pl.BlockSpec(memory_space=pltpu.VMEM)
 SMEM = pl.BlockSpec(memory_space=pltpu.SMEM)
 
@@ -23,8 +41,8 @@
     return lax.all_to_all(x, axes, 0, 0, tiled=True, axis_index_groups=groups)
 
 
-def swap(x, axis):
-    return lax.ppermute(x, axis, [(0, 1), (1, 0)])
+def swap(x, axis, pairs):
+    return lax.ppermute(x, axis, pairs)
 
 
 def after(x, *others):
@@ -55,7 +73,7 @@
     )(cols, counts, blocks)
 
 
-def product_kernel(place, whole, a00, a01, a10, a11, out, columns):
+def product_kernel(place, whole, a00, a01, a10, a11, stay, go, columns, tiles):
     core, level = place[0], place[1]
     plane, pair, rows, width = whole.shape
     for j in range(plane):
@@ -68,20 +86,28 @@
         value += jnp.dot(
             theirs[...], columns[1 - level].reshape(-1, width), preferred_element_type=jnp.float32
         )
-        value = value.astype(jnp.bfloat16).reshape(PAIRS, pair, rows // 2, width)
+        value = value.astype(jnp.bfloat16).reshape(TILES, pair, rows // 2, width)
         target = core if near == 0 else 1 - core
-        for z in range(pair):
-            out[:, z, target] = value[:, z]
+        for k in range(TILES):
+            for z in range(pair):
+                tiles[place[2 + k], z, target] = value[k, z]
+    stay[...] = tiles[:STEP]
+    go[...] = tiles[STEP:]
 
 
 def product(place, whole, panels):
     plane, pair, rows, width = whole.shape
+    part = (pair, 2, rows // 2, width)
+    half = jax.ShapeDtypeStruct((STEP,) + part, jnp.bfloat16)
     return pl.pallas_call(
         product_kernel,
-        out_shape=jax.ShapeDtypeStruct((PAIRS, pair, 2, rows // 2, width), jnp.bfloat16),
+        out_shape=(half, half),
         in_specs=[SMEM] + [VMEM] * 5,
-        out_specs=VMEM,
-        scratch_shapes=[pltpu.VMEM((pair, plane, rows, width), jnp.bfloat16)],
+        out_specs=(VMEM, VMEM),
+        scratch_shapes=[
+            pltpu.VMEM((pair, plane, rows, width), jnp.bfloat16),
+            pltpu.VMEM((TILES,) + part, jnp.bfloat16),
+        ],
         compiler_params=pltpu.CompilerParams(vmem_limit_bytes=14 << 20),
         name="panel_product",
     )(place, whole, *panels)
@@ -93,8 +119,10 @@
     width = full // 4
     pooled = 4 * rows
     plane = SIZES["x"] * SIZES["y"]
-    place = jnp.stack([lax.axis_index("c"), lax.axis_index("zodd")]).astype(jnp.int32)
-    crossed = lax.axis_index("zhalf") == 1
+    z = lax.axis_index("z")
+    here = jnp.stack([lax.axis_index("c"), z & 1]).astype(jnp.int32)
+    place = jnp.concatenate([here, jnp.asarray(tile_places(), jnp.int32)[z]])
+    crossed = (z & 2) != 0
 
     counts = jnp.broadcast_to(degree.astype(bf16)[:, None], (rows, LANES))
     slices = jnp.stack(
@@ -104,7 +132,7 @@
         ]
     )
     slices = jnp.where(crossed, jnp.roll(slices, 2, axis=0), slices)
-    got = exchange(slices, POOL).reshape(pooled, width + LANES)
+    got = exchange(slices, ("c", "z"), TILE_GROUPS).reshape(pooled, width + LANES)
     scale = lax.rsqrt(got[:, width : width + 1].astype(f32))
     sent = (scale * got[:, :width].astype(f32)).astype(bf16)
     copies = jnp.broadcast_to(sent[None], (plane,) + sent.shape)
@@ -112,9 +140,9 @@
 
     blocks, block_cols = lax.optimization_barrier((blocks, block_cols, slices))[:2]
     a00 = build_dense(blocks[:, 0], block_cols[:, 0], block_count[:, 0])
-    a01 = swap(a00, "zodd")
-    a10 = swap(a00, "c")
-    a11 = swap(after(a01, whole), "c")
+    a01 = swap(a00, "z", LEVELS)
+    a10 = swap(a00, "c", CORES)
+    a11 = swap(after(a01, whole), "c", CORES)
     panels = (a00, a01, a10, a11)
 
     hops = []
@@ -122,13 +150,15 @@
         if hop:
             copies = jnp.broadcast_to(sent[None], (plane,) + sent.shape)
             whole = exchange(copies, PLANE)
-        partial_value = product(place, whole.reshape(plane, 2, 2 * rows, width), panels)
-        parts = exchange(partial_value.reshape(PAIRS, pooled, width), LINE, GROUPS)
+        stay, go = product(place, whole.reshape(plane, 2, 2 * rows, width), panels)
+        come = swap(go, "z", NEIGHBOURS)
+        both = (stay.astype(f32) + come.astype(f32)).astype(bf16)
+        parts = exchange(both.reshape(STEP, pooled, width), "z", SUM_GROUPS)
         total = jnp.sum(parts.astype(f32), axis=0)
         value = (scale * (total + sent.astype(f32))).astype(bf16)
         sent = (scale * value.astype(f32)).astype(bf16)
         hops.append(value.reshape(4, rows, width))
-    back = exchange(jnp.stack(hops, axis=1), POOL)
+    back = exchange(jnp.stack(hops, axis=1), ("c", "z"), TILE_GROUPS)
     back = jnp.where(crossed, jnp.roll(back, 2, axis=0), back)
     return tuple(
         back[:, k].transpose(1, 0, 2).reshape(rows, full) for k in range(HOPS)

time: 218 us -> 206 us (0.945)
  blocking collectives: 158 us -> 99.3 us
  starting transfers between devices: 23.3 us -> 56.7 us
  waiting for transfers between devices: 17.4 us -> 30.6 us
    all_to_all x6, blocking collectives: 158 us -> 99.3 us  [exchange(): return lax.all_to_all(x, axes, 0, 0, tiled=True, axis_index_groups=groups)]
    ppermute x3 -> x6, starting transfers between devices: 8.86 us -> 42.2 us  [swap(): return lax.ppermute(x, axis, pairs)]
    ppermute x3 -> x6, waiting for transfers between devices: 17.4 us -> 30.6 us  [swap(): return lax.ppermute(x, axis, pairs)]
  transfers between devices with their start and end apart: 5 -> 8, of which waited for: 2 -> 5; matrix products, arithmetic and copies ran while one was open for 1% -> 1% of each run, Pallas kernels for 0% -> 0%
where the time goes in v5:
time: 206 us; the launch traced here: 205 us
  blocking collectives  99.3 us (48%)
  starting transfers between devices  56.7 us (28%)
  waiting for transfers between devices  30.6 us (15%)
  Pallas kernels  9.07 us (4%)
  local copies, waits for them, and re-layouts  7.34 us (4%)
    all_to_all x6, blocking collectives, exchange(): return lax.all_to_all(x, axes, 0, 0, tiled=True, axis_index_groups=groups)  99.3 us
    ppermute x6, starting transfers between devices, swap(): return lax.ppermute(x, axis, pairs)  42.2 us
    ppermute x6, waiting for transfers between devices, swap(): return lax.ppermute(x, axis, pairs)  30.6 us
    all_to_all x2, starting transfers between devices, exchange(): return lax.all_to_all(x, axes, 0, 0, tiled=True, axis_index_groups=groups)  14.5 us
    pallas_call x3, Pallas kernels, product(): pl.pallas_call(product_kernel, out_shape=(half, half), in_specs=[SMEM] +...  8.13 us
  transfers between devices with their start and end apart: 8, of which 5 were waited for; matrix products, arithmetic and copies ran while one was open for 1% of the time, Pallas kernels for 0%

profile of v5, /device:TPU:1, one launch (start us, length us, event | category | flops | bytes accessed | tf_op | source)
XLA Modules:
  0.0 205.5 jit_solution(6604660024346036985)
XLA Ops:
  2.8 10.1 %all-to-all-start = ((bf16[4,32,384]{2,1,0:T(8,128)(2,1)}), bf16[4,32,384]{2,1,0:T(8,128)(2,1)S(1)}, u32[]{:S(2)}, u32[]{:S(2)}) async-start(bf16[4,32,384]{2,1,0:T(8,128)(2,1)} %maximum_select_fusion.1), calls=%async_computation | async-start | bytes 196608 | tf_op jit(solution)/shard_map/all_to_all | solution.py:41
  13.7 1.2 copy-done
  15.8 3.3 %collective-permute-start = (bf16[512,1024]{1,0:T(8,128)(2,1)S(1)}, bf16[512,1024]{1,0:T(8,128)(2,1)S(1)}, u32[]{:S(2)}, u32[]{:S(2)}) collective-permute-start(bf16[512,1024]{1,0:T(8,128)(2,1)S(1)} %dense_panel.1.a00), channel_id=1, source_target_pairs={{0,1},{1,0},{2,3},{3,2},{4,5},{5,4},{6,7},{7,6},{8,9},{9,8},{10,11... | collective-permute-start | bytes 3145736 | tf_op jit(solution)/shard_map/ppermute | solution.py:45
  19.4 1.1 broadcast_in_dim.9
  20.5 4.3 %all-to-all-start.1 = ((bf16[16,128,256]{2,1,0:T(8,128)(2,1)}), bf16[16,128,256]{2,1,0:T(8,128)(2,1)}, u32[]{:S(2)}, u32[]{:S(2)}) async-start(bf16[16,128,256]{2,1,0:T(8,128)(2,1)} %broadcast_in_dim.9), calls=%async_computation.1 | async-start | bytes 2097152 | tf_op jit(solution)/shard_map/all_to_all | solution.py:41
  24.8 2.5 %collective-permute-start.1 = (bf16[512,1024]{1,0:T(8,128)(2,1)S(1)}, bf16[512,1024]{1,0:T(8,128)(2,1)S(1)}, u32[]{:S(2)}, u32[]{:S(2)}) collective-permute-start(bf16[512,1024]{1,0:T(8,128)(2,1)S(1)} %dense_panel.1.a00), channel_id=1, source_target_pairs={{0,16},{16,0},{1,17},{17,1},{2,18},{18,2},{3,19},{19,3},{4,20},{20... | collective-permute-start | bytes 3145736 | tf_op jit(solution)/shard_map/ppermute | solution.py:45
  27.4 15.1 %collective-permute-done.a01 = bf16[512,1024]{1,0:T(8,128)(2,1)S(1)} collective-permute-done((bf16[512,1024]{1,0:T(8,128)(2,1)S(1)}, bf16[512,1024]{1,0:T(8,128)(2,1)S(1)}, u32[]{:S(2)}, u32[]{:S(2)}) %collective-permute-start) | collective-permute-done | bytes 1048608 | tf_op jit(solution)/shard_map/ppermute | solution.py:45
  42.5 3.0 %collective-permute-start.2 = (bf16[512,1024]{1,0:T(8,128)(2,1)S(1)}, bf16[512,1024]{1,0:T(8,128)(2,1)}, u32[]{:S(2)}, u32[]{:S(2)}) collective-permute-start(bf16[512,1024]{1,0:T(8,128)(2,1)S(1)} %collective-permute-done.a01), channel_id=1, source_target_pairs={{0,16},{16,0},{1,17},{17,1},{2,18},{18,2},{3,19},{19,3},{4,20},{20... | collective-permute-start | bytes 3145736 | tf_op jit(solution)/shard_map/ppermute | solution.py:45
  46.3 1.6 collective-permute-done.2.a11
  47.9 2.9 %panel_product.3 = (bf16[4,2,2,32,256]{4,3,2,1,0:T(8,128)(2,1)S(1)}, bf16[4,2,2,32,256]{4,3,2,1,0:T(8,128)(2,1)S(1)}) custom-call(s32[10]{0:T(128)S(1)} %pad_add_fusion.place, bf16[16,2,64,256]{3,2,1,0:T(8,128)(2,1)} %bitcast.8.whole, bf16[512,1024]{1,0:T(8,128)(2,1)S(1)} %dense_panel.1.a00, bf16[512,1024]{1,0:T(8,128)(2,1)S(1)} %collective-permute-done.a01, ...), custom_call_target="tpu_custom_call" | custom-call | tf_op jit(solution)/shard_map/panel_product/pallas_call | solution.py:102
  50.8 7.6 %collective-permute-start.3 = (bf16[4,2,2,32,256]{4,3,2,1,0:T(8,128)(2,1)S(1)}, bf16[4,2,2,32,256]{4,3,2,1,0:T(8,128)(2,1)S(1)}, u32[]{:S(2)}, u32[]{:S(2)}) collective-permute-start(bf16[4,2,2,32,256]{4,3,2,1,0:T(8,128)(2,1)S(1)} %get-tuple-element.16), channel_id=1, source_target_pairs={{0,15},{1,2},{2,1},{3,4},{4,3},{5,6},{6,5},{7,8},{8,7},{9,10},{10,... | collective-permute-start | bytes 786440 | tf_op jit(solution)/shard_map/ppermute | solution.py:45
  58.4 6.4 %collective-permute-done.3 = bf16[4,2,2,32,256]{4,3,2,1,0:T(8,128)(2,1)S(1)} collective-permute-done((bf16[4,2,2,32,256]{4,3,2,1,0:T(8,128)(2,1)S(1)}, bf16[4,2,2,32,256]{4,3,2,1,0:T(8,128)(2,1)S(1)}, u32[]{:S(2)}, u32[]{:S(2)}) %collective-permute-start.3) | collective-permute-done | bytes 262176 | tf_op jit(solution)/shard_map/ppermute | solution.py:45
  64.9 16.9 %all_to_all.40 = bf16[4,128,256]{2,1,0:T(8,128)(2,1)S(1)} all-to-all(bf16[4,128,256]{2,1,0:T(8,128)(2,1)S(1)} %bitcast.48), channel_id=1, replica_groups={{1,5,10,14},{2,6,9,13},{3,7,12,0},{4,8,11,15},{17,21,26,30},{18,22,25,2..., dimensions={0} | all-to-all | bytes 524288 | tf_op jit(solution)/shard_map/all_to_all | solution.py:41
  82.1 15.0 %all_to_all.41 = bf16[16,128,256]{2,1,0:T(8,128)(2,1)S(1)} all-to-all(bf16[16,128,256]{2,1,0:T(8,128)(2,1)S(1)} %broadcast_in_dim.10), channel_id=1, replica_groups=mesh['x'=4,'y'=4,'c'=2,'z'=16] {'x','y'}, dimensions={0} | all-to-all | bytes 2097152 | tf_op jit(solution)/shard_map/all_to_all | solution.py:41
  97.0 2.6 %panel_product.4 = (bf16[4,2,2,32,256]{4,3,2,1,0:T(8,128)(2,1)S(1)}, bf16[4,2,2,32,256]{4,3,2,1,0:T(8,128)(2,1)S(1)}) custom-call(s32[10]{0:T(128)S(1)} %pad_add_fusion.place, bf16[16,2,64,256]{3,2,1,0:T(8,128)(2,1)S(1)} %bitcast.44, bf16[512,1024]{1,0:T(8,128)(2,1)S(1)} %dense_panel.1.a00, bf16[512,1024]{1,0:T(8,128)(2,1)S(1)} %collective-permute-done.a01, ...), custom_call_target="tpu_custom_call" | custom-call | tf_op jit(solution)/shard_map/panel_product/pallas_call | solution.py:102
  99.6 15.3 %collective-permute-start.4 = (bf16[4,2,2,32,256]{4,3,2,1,0:T(8,128)(2,1)S(1)}, bf16[4,2,2,32,256]{4,3,2,1,0:T(8,128)(2,1)S(1)}, u32[]{:S(2)}, u32[]{:S(2)}) collective-permute-start(bf16[4,2,2,32,256]{4,3,2,1,0:T(8,128)(2,1)S(1)} %get-tuple-element.18), channel_id=1, source_target_pairs={{0,15},{1,2},{2,1},{3,4},{4,3},{5,6},{6,5},{7,8},{8,7},{9,10},{10,... | collective-permute-start | bytes 786440 | tf_op jit(solution)/shard_map/ppermute | solution.py:45
  114.9 3.7 %collective-permute-done.4 = bf16[4,2,2,32,256]{4,3,2,1,0:T(8,128)(2,1)S(1)} collective-permute-done((bf16[4,2,2,32,256]{4,3,2,1,0:T(8,128)(2,1)S(1)}, bf16[4,2,2,32,256]{4,3,2,1,0:T(8,128)(2,1)S(1)}, u32[]{:S(2)}, u32[]{:S(2)}) %collective-permute-start.4) | collective-permute-done | bytes 262176 | tf_op jit(solution)/shard_map/ppermute | solution.py:45
  118.8 14.8 %all_to_all.42 = bf16[4,128,256]{2,1,0:T(8,128)(2,1)S(1)} all-to-all(bf16[4,128,256]{2,1,0:T(8,128)(2,1)S(1)} %bitcast.49), channel_id=1, replica_groups={{1,5,10,14},{2,6,9,13},{3,7,12,0},{4,8,11,15},{17,21,26,30},{18,22,25,2..., dimensions={0} | all-to-all | bytes 524288 | tf_op jit(solution)/shard_map/all_to_all | solution.py:41
  133.9 15.4 %all_to_all.43 = bf16[16,128,256]{2,1,0:T(8,128)(2,1)S(1)} all-to-all(bf16[16,128,256]{2,1,0:T(8,128)(2,1)S(1)} %broadcast_in_dim.11), channel_id=1, replica_groups=mesh['x'=4,'y'=4,'c'=2,'z'=16] {'x','y'}, dimensions={0} | all-to-all | bytes 2097152 | tf_op jit(solution)/shard_map/all_to_all | solution.py:41
  149.3 2.6 %panel_product.5 = (bf16[4,2,2,32,256]{4,3,2,1,0:T(8,128)(2,1)S(1)}, bf16[4,2,2,32,256]{4,3,2,1,0:T(8,128)(2,1)S(1)}) custom-call(s32[10]{0:T(128)S(1)} %pad_add_fusion.place, bf16[16,2,64,256]{3,2,1,0:T(8,128)(2,1)S(1)} %bitcast.43, bf16[512,1024]{1,0:T(8,128)(2,1)S(1)} %dense_panel.1.a00, bf16[512,1024]{1,0:T(8,128)(2,1)S(1)} %collective-permute-done.a01, ...), custom_call_target="tpu_custom_call" | custom-call | tf_op jit(solution)/shard_map/panel_product/pallas_call | solution.py:102
  151.9 10.5 %collective-permute-start.5 = (bf16[4,2,2,32,256]{4,3,2,1,0:T(8,128)(2,1)S(1)}, bf16[4,2,2,32,256]{4,3,2,1,0:T(8,128)(2,1)S(1)}, u32[]{:S(2)}, u32[]{:S(2)}) collective-permute-start(bf16[4,2,2,32,256]{4,3,2,1,0:T(8,128)(2,1)S(1)} %get-tuple-element.20), channel_id=1, source_target_pairs={{0,15},{1,2},{2,1},{3,4},{4,3},{5,6},{6,5},{7,8},{8,7},{9,10},{10,... | collective-permute-start | bytes 786440 | tf_op jit(solution)/shard_map/ppermute | solution.py:45
  162.4 3.7 %collective-permute-done.5 = bf16[4,2,2,32,256]{4,3,2,1,0:T(8,128)(2,1)S(1)} collective-permute-done((bf16[4,2,2,32,256]{4,3,2,1,0:T(8,128)(2,1)S(1)}, bf16[4,2,2,32,256]{4,3,2,1,0:T(8,128)(2,1)S(1)}, u32[]{:S(2)}, u32[]{:S(2)}) %collective-permute-start.5) | collective-permute-done | bytes 262176 | tf_op jit(solution)/shard_map/ppermute | solution.py:45
  166.2 16.2 %all_to_all.44 = bf16[4,128,256]{2,1,0:T(8,128)(2,1)S(1)} all-to-all(bf16[4,128,256]{2,1,0:T(8,128)(2,1)S(1)} %bitcast.50), channel_id=1, replica_groups={{1,5,10,14},{2,6,9,13},{3,7,12,0},{4,8,11,15},{17,21,26,30},{18,22,25,2..., dimensions={0} | all-to-all | bytes 524288 | tf_op jit(solution)/shard_map/all_to_all | solution.py:41
  182.6 20.9 %all_to_all.45 = bf16[4,3,32,256]{3,2,1,0:T(8,128)(2,1)S(1)} all-to-all(bf16[4,3,32,256]{3,2,1,0:T(8,128)(2,1)S(1)} %copy.13), channel_id=1, replica_groups={{0,16,1,17},{2,18,3,19},{4,20,5,21},{6,22,7,23},{8,24,9,25},{10,26,11,2..., dimensions={0} | all-to-all | bytes 393216 | tf_op jit(solution)/shard_map/all_to_all | solution.py:41
  (39 shorter events, 7.6 us)
Async XLA Ops:
  0.6 0.7 copy-start.3
  2.8 16.4 %all-to-all-start = ((bf16[4,32,384]{2,1,0:T(8,128)(2,1)}), bf16[4,32,384]{2,1,0:T(8,128)(2,1)S(1)}, u32[]{:S(2)}, u32[]{:S(2)}) async-start(bf16[4,32,384]{2,1,0:T(8,128)(2,1)} %maximum_select_fusion.1), calls=%async_computation | async-start | bytes 196608 | tf_op jit(solution)/shard_map/all_to_all | solution.py:41
  13.0 0.7 copy-start.1
  13.0 0.7 copy-start.2
  13.7 1.2 copy-start
  15.8 26.7 %collective-permute-start = (bf16[512,1024]{1,0:T(8,128)(2,1)S(1)}, bf16[512,1024]{1,0:T(8,128)(2,1)S(1)}, u32[]{:S(2)}, u32[]{:S(2)}) collective-permute-start(bf16[512,1024]{1,0:T(8,128)(2,1)S(1)} %dense_panel.1.a00), channel_id=1, source_target_pairs={{0,1},{1,0},{2,3},{3,2},{4,5},{5,4},{6,7},{7,6},{8,9},{9,8},{10,11... | collective-permute-start | bytes 3145736 | tf_op jit(solution)/shard_map/ppermute | solution.py:45
  20.5 22.0 %all-to-all-start.1 = ((bf16[16,128,256]{2,1,0:T(8,128)(2,1)}), bf16[16,128,256]{2,1,0:T(8,128)(2,1)}, u32[]{:S(2)}, u32[]{:S(2)}) async-start(bf16[16,128,256]{2,1,0:T(8,128)(2,1)} %broadcast_in_dim.9), calls=%async_computation.1 | async-start | bytes 2097152 | tf_op jit(solution)/shard_map/all_to_all | solution.py:41
  24.8 21.4 %collective-permute-start.1 = (bf16[512,1024]{1,0:T(8,128)(2,1)S(1)}, bf16[512,1024]{1,0:T(8,128)(2,1)S(1)}, u32[]{:S(2)}, u32[]{:S(2)}) collective-permute-start(bf16[512,1024]{1,0:T(8,128)(2,1)S(1)} %dense_panel.1.a00), channel_id=1, source_target_pairs={{0,16},{16,0},{1,17},{17,1},{2,18},{18,2},{3,19},{19,3},{4,20},{20... | collective-permute-start | bytes 3145736 | tf_op jit(solution)/shard_map/ppermute | solution.py:45
  42.5 5.4 %collective-permute-start.2 = (bf16[512,1024]{1,0:T(8,128)(2,1)S(1)}, bf16[512,1024]{1,0:T(8,128)(2,1)}, u32[]{:S(2)}, u32[]{:S(2)}) collective-permute-start(bf16[512,1024]{1,0:T(8,128)(2,1)S(1)} %collective-permute-done.a01), channel_id=1, source_target_pairs={{0,16},{16,0},{1,17},{17,1},{2,18},{18,2},{3,19},{19,3},{4,20},{20... | collective-permute-start | bytes 3145736 | tf_op jit(solution)/shard_map/ppermute | solution.py:45
  50.8 14.0 %collective-permute-start.3 = (bf16[4,2,2,32,256]{4,3,2,1,0:T(8,128)(2,1)S(1)}, bf16[4,2,2,32,256]{4,3,2,1,0:T(8,128)(2,1)S(1)}, u32[]{:S(2)}, u32[]{:S(2)}) collective-permute-start(bf16[4,2,2,32,256]{4,3,2,1,0:T(8,128)(2,1)S(1)} %get-tuple-element.16), channel_id=1, source_target_pairs={{0,15},{1,2},{2,1},{3,4},{4,3},{5,6},{6,5},{7,8},{8,7},{9,10},{10,... | collective-permute-start | bytes 786440 | tf_op jit(solution)/shard_map/ppermute | solution.py:45
  99.6 19.1 %collective-permute-start.4 = (bf16[4,2,2,32,256]{4,3,2,1,0:T(8,128)(2,1)S(1)}, bf16[4,2,2,32,256]{4,3,2,1,0:T(8,128)(2,1)S(1)}, u32[]{:S(2)}, u32[]{:S(2)}) collective-permute-start(bf16[4,2,2,32,256]{4,3,2,1,0:T(8,128)(2,1)S(1)} %get-tuple-element.18), channel_id=1, source_target_pairs={{0,15},{1,2},{2,1},{3,4},{4,3},{5,6},{6,5},{7,8},{8,7},{9,10},{10,... | collective-permute-start | bytes 786440 | tf_op jit(solution)/shard_map/ppermute | solution.py:45
  151.9 14.2 %collective-permute-start.5 = (bf16[4,2,2,32,256]{4,3,2,1,0:T(8,128)(2,1)S(1)}, bf16[4,2,2,32,256]{4,3,2,1,0:T(8,128)(2,1)S(1)}, u32[]{:S(2)}, u32[]{:S(2)}) collective-permute-start(bf16[4,2,2,32,256]{4,3,2,1,0:T(8,128)(2,1)S(1)} %get-tuple-element.20), channel_id=1, source_target_pairs={{0,15},{1,2},{2,1},{3,4},{4,3},{5,6},{6,5},{7,8},{8,7},{9,10},{10,... | collective-permute-start | bytes 786440 | tf_op jit(solution)/shard_map/ppermute | solution.py:45

commit v6 on v5

--- a/solution.py
+++ b/solution.py
@@ -22,12 +22,9 @@
 ]
 
 
-def tile_places():
+def tile_order():
     group_of = {z: group for group in SUM_GROUPS for z in group}
-    return [
-        [[z // 2 for z in group_of[me] + group_of[other]].index(k) for k in range(TILES)]
-        for me, other in NEIGHBOURS
-    ]
+    return [[z // 2 for z in group_of[me] + group_of[other]] for me, other in NEIGHBOURS]
 
 
 LANES = 128
@@ -73,44 +70,61 @@
     )(cols, counts, blocks)
 
 
-def product_kernel(place, whole, a00, a01, a10, a11, stay, go, columns, tiles):
+def product_kernel(begin, place, whole, a00, a01, a10, a11, out, columns):
     core, level = place[0], place[1]
     plane, pair, rows, width = whole.shape
+    tile = pair * rows // 2
     for j in range(plane):
         for z in range(pair):
             columns[z, j] = whole[j, z]
+    starts = [pl.multiple_of(place[2 + begin + p] * tile, tile) for p in range(STEP)]
     for near, (ours, theirs) in enumerate(((a00, a01), (a10, a11))):
-        value = jnp.dot(
-            ours[...], columns[level].reshape(-1, width), preferred_element_type=jnp.float32
-        )
-        value += jnp.dot(
-            theirs[...], columns[1 - level].reshape(-1, width), preferred_element_type=jnp.float32
-        )
-        value = value.astype(jnp.bfloat16).reshape(TILES, pair, rows // 2, width)
+        value = None
+        for panel, at in ((ours, level), (theirs, 1 - level)):
+            left = jnp.concatenate([panel[pl.ds(start, tile), :] for start in starts])
+            right = columns[at].reshape(-1, width)
+            part = jnp.dot(left, right, preferred_element_type=jnp.float32)
+            value = part if value is None else value + part
+        value = value.astype(jnp.bfloat16).reshape(STEP, pair, rows // 2, width)
         target = core if near == 0 else 1 - core
-        for k in range(TILES):
-            for z in range(pair):
-                tiles[place[2 + k], z, target] = value[k, z]
-    stay[...] = tiles[:STEP]
-    go[...] = tiles[STEP:]
+        for z in range(pair):
+            out[:, z, target] = value[:, z]
 
 
-def product(place, whole, panels):
+def product(begin, place, whole, panels):
     plane, pair, rows, width = whole.shape
-    part = (pair, 2, rows // 2, width)
-    half = jax.ShapeDtypeStruct((STEP,) + part, jnp.bfloat16)
+
+    def body(*refs):
+        product_kernel(begin, *refs)
+
     return pl.pallas_call(
-        product_kernel,
-        out_shape=(half, half),
+        body,
+        out_shape=jax.ShapeDtypeStruct((STEP, pair, 2, rows // 2, width), jnp.bfloat16),
         in_specs=[SMEM] + [VMEM] * 5,
-        out_specs=(VMEM, VMEM),
-        scratch_shapes=[
-            pltpu.VMEM((pair, plane, rows, width), jnp.bfloat16),
-            pltpu.VMEM((TILES,) + part, jnp.bfloat16),
-        ],
+        out_specs=VMEM,
+        scratch_shapes=[pltpu.VMEM((pair, plane, rows, width), jnp.bfloat16)],
         compiler_params=pltpu.CompilerParams(vmem_limit_bytes=14 << 20),
-        name="panel_product",
+        name="go_product" if begin else "stay_product",
     )(place, whole, *panels)
+
+
+def collect_kernel(crossed, back, *outs):
+    _, _, _, width = back.shape
+    for q in range(4):
+        for k, out in enumerate(outs):
+            out[:, q * width : (q + 1) * width] = back[q ^ 2 * crossed[0], k]
+
+
+def collect(crossed, back):
+    _, hops, rows, width = back.shape
+    return pl.pallas_call(
+        collect_kernel,
+        out_shape=(jax.ShapeDtypeStruct((rows, 4 * width), back.dtype),) * hops,
+        in_specs=[SMEM, VMEM],
+        out_specs=(VMEM,) * hops,
+        compiler_params=pltpu.CompilerParams(vmem_limit_bytes=8 << 20),
+        name="collect_rows",
+    )(crossed, back)
 
 
 def on_device(features, degree, blocks, block_cols, block_count):
@@ -121,7 +135,7 @@
     plane = SIZES["x"] * SIZES["y"]
     z = lax.axis_index("z")
     here = jnp.stack([lax.axis_index("c"), z & 1]).astype(jnp.int32)
-    place = jnp.concatenate([here, jnp.asarray(tile_places(), jnp.int32)[z]])
+    place = jnp.concatenate([here, jnp.asarray(tile_order(), jnp.int32)[z]])
     crossed = (z & 2) != 0
 
     counts = jnp.broadcast_to(degree.astype(bf16)[:, None], (rows, LANES))
@@ -150,8 +164,9 @@
         if hop:
             copies = jnp.broadcast_to(sent[None], (plane,) + sent.shape)
             whole = exchange(copies, PLANE)
-        stay, go = product(place, whole.reshape(plane, 2, 2 * rows, width), panels)
-        come = swap(go, "z", NEIGHBOURS)
+        whole = whole.reshape(plane, 2, 2 * rows, width)
+        come = swap(product(STEP, place, whole, panels), "z", NEIGHBOURS)
+        stay = product(0, place, whole, panels)
         both = (stay.astype(f32) + come.astype(f32)).astype(bf16)
         parts = exchange(both.reshape(STEP, pooled, width), "z", SUM_GROUPS)
         total = jnp.sum(parts.astype(f32), axis=0)
@@ -159,10 +174,7 @@
         sent = (scale * value.astype(f32)).astype(bf16)
         hops.append(value.reshape(4, rows, width))
     back = exchange(jnp.stack(hops, axis=1), ("c", "z"), TILE_GROUPS)
-    back = jnp.where(crossed, jnp.roll(back, 2, axis=0), back)
-    return tuple(
-        back[:, k].transpose(1, 0, 2).reshape(rows, full) for k in range(HOPS)
-    )
+    return collect(((z & 2) >> 1).astype(jnp.int32)[None], back)
 
 
 def solution(mesh):

time: 206 us -> 204 us (level)
  blocking collectives: 99.3 us -> 74.6 us
  starting transfers between devices: 56.7 us -> 76.2 us
  Pallas kernels: 9.07 us -> 14.4 us
  waiting for transfers between devices: 30.6 us -> 28.3 us
    all_to_all x6 -> x5, blocking collectives: 99.3 us -> 74.6 us  [exchange(): return lax.all_to_all(x, axes, 0, 0, tiled=True, axis_index_groups=groups)]
    all_to_all x2 -> x3, starting transfers between devices: 14.5 us -> 31.7 us  [exchange(): return lax.all_to_all(x, axes, 0, 0, tiled=True, axis_index_groups=groups)]
    ppermute x6, waiting for transfers between devices: 30.6 us -> 24.2 us  [swap(): return lax.ppermute(x, axis, pairs)]
    pallas_call x3 -> x7, Pallas kernels: 8.13 us -> 13.4 us  [the longest x6 12.7 us: product(): pl.pallas_call(body, out_shape=jax.ShapeDtypeStruct((STEP, pair, 2, rows...]
    all_to_all x2 -> x3, waiting for transfers between devices: 0.01 us -> 4.13 us  [exchange(): return lax.all_to_all(x, axes, 0, 0, tiled=True, axis_index_groups=groups)]
    ppermute x6, starting transfers between devices: 42.2 us -> 44.5 us  [swap(): return lax.ppermute(x, axis, pairs)]
  transfers between devices with their start and end apart: 8 -> 9, of which waited for: 5 -> 6; matrix products, arithmetic and copies ran while one was open for 1% -> 1% of each run, Pallas kernels for 0% -> 4%
where the time goes in v6:
time: 204 us; the launch traced here: 202 us
  starting transfers between devices  76.2 us (37%)
  blocking collectives  74.6 us (37%)
  waiting for transfers between devices  28.3 us (14%)
  Pallas kernels  14.4 us (7%)
  local copies, waits for them, and re-layouts  5.45 us (3%)
  other arithmetic  2.21 us (1%)
    all_to_all x5, blocking collectives, exchange(): return lax.all_to_all(x, axes, 0, 0, tiled=True, axis_index_groups=groups)  74.6 us
    ppermute x6, starting transfers between devices, swap(): return lax.ppermute(x, axis, pairs)  44.5 us
    all_to_all x3, starting transfers between devices, exchange(): return lax.all_to_all(x, axes, 0, 0, tiled=True, axis_index_groups=groups)  31.7 us
    ppermute x6, waiting for transfers between devices, swap(): return lax.ppermute(x, axis, pairs)  24.2 us
    pallas_call x6, Pallas kernels, product(): pl.pallas_call(body, out_shape=jax.ShapeDtypeStruct((STEP, pair, 2, rows...  12.7 us
    all_to_all x3, waiting for transfers between devices, exchange(): return lax.all_to_all(x, axes, 0, 0, tiled=True, axis_index_groups=groups)  4.13 us
  transfers between devices with their start and end apart: 9, of which 6 were waited for; matrix products, arithmetic and copies ran while one was open for 1% of the time, Pallas kernels for 4%

profile of v6, /device:TPU:1, one launch (start us, length us, event | category | flops | bytes accessed | tf_op | source)
XLA Modules:
  0.0 202.1 jit_solution(1315625304895791396)
XLA Ops:
  2.8 10.1 %all-to-all-start = ((bf16[4,32,384]{2,1,0:T(8,128)(2,1)}), bf16[4,32,384]{2,1,0:T(8,128)(2,1)S(1)}, u32[]{:S(2)}, u32[]{:S(2)}) async-start(bf16[4,32,384]{2,1,0:T(8,128)(2,1)} %maximum_select_fusion), calls=%async_computation | async-start | bytes 196608 | tf_op jit(solution)/shard_map/all_to_all | solution.py:38
  15.9 3.3 %collective-permute-start = (bf16[512,1024]{1,0:T(8,128)(2,1)S(1)}, bf16[512,1024]{1,0:T(8,128)(2,1)S(1)}, u32[]{:S(2)}, u32[]{:S(2)}) collective-permute-start(bf16[512,1024]{1,0:T(8,128)(2,1)S(1)} %dense_panel.1.refs_2_), channel_id=1, source_target_pairs={{0,1},{1,0},{2,3},{3,2},{4,5},{5,4},{6,7},{7,6},{8,9},{9,8},{10,11... | collective-permute-start | bytes 3145736 | tf_op jit(solution)/shard_map/ppermute | solution.py:42
  20.5 4.3 %all-to-all-start.1 = ((bf16[16,128,256]{2,1,0:T(8,128)(2,1)}), bf16[16,128,256]{2,1,0:T(8,128)(2,1)}, u32[]{:S(2)}, u32[]{:S(2)}) async-start(bf16[16,128,256]{2,1,0:T(8,128)(2,1)} %broadcast_in_dim.12), calls=%async_computation.1 | async-start | bytes 2097152 | tf_op jit(solution)/shard_map/all_to_all | solution.py:38
  24.8 2.6 %collective-permute-start.1 = (bf16[512,1024]{1,0:T(8,128)(2,1)S(1)}, bf16[512,1024]{1,0:T(8,128)(2,1)S(1)}, u32[]{:S(2)}, u32[]{:S(2)}) collective-permute-start(bf16[512,1024]{1,0:T(8,128)(2,1)S(1)} %dense_panel.1.refs_2_), channel_id=1, source_target_pairs={{0,16},{16,0},{1,17},{17,1},{2,18},{18,2},{3,19},{19,3},{4,20},{20... | collective-permute-start | bytes 3145736 | tf_op jit(solution)/shard_map/ppermute | solution.py:42
  27.4 15.1 %collective-permute-done.refs_3_ = bf16[512,1024]{1,0:T(8,128)(2,1)S(1)} collective-permute-done((bf16[512,1024]{1,0:T(8,128)(2,1)S(1)}, bf16[512,1024]{1,0:T(8,128)(2,1)S(1)}, u32[]{:S(2)}, u32[]{:S(2)}) %collective-permute-start) | collective-permute-done | bytes 1048608 | tf_op jit(solution)/shard_map/ppermute | solution.py:42
  42.5 2.9 %collective-permute-start.2 = (bf16[512,1024]{1,0:T(8,128)(2,1)S(1)}, bf16[512,1024]{1,0:T(8,128)(2,1)}, u32[]{:S(2)}, u32[]{:S(2)}) collective-permute-start(bf16[512,1024]{1,0:T(8,128)(2,1)S(1)} %collective-permute-done.refs_3_), channel_id=1, source_target_pairs={{0,16},{16,0},{1,17},{17,1},{2,18},{18,2},{3,19},{19,3},{4,20},{20... | collective-permute-start | bytes 3145736 | tf_op jit(solution)/shard_map/ppermute | solution.py:42
  47.9 2.3 %go_product.3 = bf16[4,2,2,32,256]{4,3,2,1,0:T(8,128)(2,1)S(1)} custom-call(s32[10]{0:T(128)S(1)} %pad_add_fusion.refs_0_, bf16[16,2,64,256]{3,2,1,0:T(8,128)(2,1)} %bitcast.10.refs_1_, bf16[512,1024]{1,0:T(8,128)(2,1)S(1)} %dense_panel.1.refs_2_, bf16[512,1024]{1,0:T(8,128)(2,1)S(1)} %collective-permute-done.refs_3_, ...), custom_call_target="tpu_custom_call" | custom-call | tf_op jit(solution)/shard_map/go_product/pallas_call | solution.py:100
  50.2 7.6 %collective-permute-start.3 = (bf16[4,2,2,32,256]{4,3,2,1,0:T(8,128)(2,1)S(1)}, bf16[4,2,2,32,256]{4,3,2,1,0:T(8,128)(2,1)S(1)}, u32[]{:S(2)}, u32[]{:S(2)}) collective-permute-start(bf16[4,2,2,32,256]{4,3,2,1,0:T(8,128)(2,1)S(1)} %go_product.3), channel_id=1, source_target_pairs={{0,15},{1,2},{2,1},{3,4},{4,3},{5,6},{6,5},{7,8},{8,7},{9,10},{10,... | collective-permute-start | bytes 786440 | tf_op jit(solution)/shard_map/ppermute | solution.py:42
  57.9 2.3 %stay_product.3 = bf16[4,2,2,32,256]{4,3,2,1,0:T(8,128)(2,1)S(1)} custom-call(s32[10]{0:T(128)S(1)} %pad_add_fusion.refs_0_, bf16[16,2,64,256]{3,2,1,0:T(8,128)(2,1)} %bitcast.10.refs_1_, bf16[512,1024]{1,0:T(8,128)(2,1)S(1)} %dense_panel.1.refs_2_, bf16[512,1024]{1,0:T(8,128)(2,1)S(1)} %collective-permute-done.refs_3_, ...), custom_call_target="tpu_custom_call" | custom-call | tf_op jit(solution)/shard_map/stay_product/pallas_call | solution.py:100
  60.2 4.0 %collective-permute-done.3 = bf16[4,2,2,32,256]{4,3,2,1,0:T(8,128)(2,1)S(1)} collective-permute-done((bf16[4,2,2,32,256]{4,3,2,1,0:T(8,128)(2,1)S(1)}, bf16[4,2,2,32,256]{4,3,2,1,0:T(8,128)(2,1)S(1)}, u32[]{:S(2)}, u32[]{:S(2)}) %collective-permute-start.3) | collective-permute-done | bytes 262176 | tf_op jit(solution)/shard_map/ppermute | solution.py:42
  64.3 16.8 %all_to_all.40 = bf16[4,128,256]{2,1,0:T(8,128)(2,1)S(1)} all-to-all(bf16[4,128,256]{2,1,0:T(8,128)(2,1)S(1)} %bitcast.34), channel_id=1, replica_groups={{1,5,10,14},{2,6,9,13},{3,7,12,0},{4,8,11,15},{17,21,26,30},{18,22,25,2..., dimensions={0} | all-to-all | bytes 524288 | tf_op jit(solution)/shard_map/all_to_all | solution.py:38
  81.4 15.0 %all_to_all.41 = bf16[16,128,256]{2,1,0:T(8,128)(2,1)S(1)} all-to-all(bf16[16,128,256]{2,1,0:T(8,128)(2,1)S(1)} %broadcast_in_dim.13), channel_id=1, replica_groups=mesh['x'=4,'y'=4,'c'=2,'z'=16] {'x','y'}, dimensions={0} | all-to-all | bytes 2097152 | tf_op jit(solution)/shard_map/all_to_all | solution.py:38
  96.4 2.0 go_product.4
  98.4 15.3 %collective-permute-start.4 = (bf16[4,2,2,32,256]{4,3,2,1,0:T(8,128)(2,1)S(1)}, bf16[4,2,2,32,256]{4,3,2,1,0:T(8,128)(2,1)S(1)}, u32[]{:S(2)}, u32[]{:S(2)}) collective-permute-start(bf16[4,2,2,32,256]{4,3,2,1,0:T(8,128)(2,1)S(1)} %go_product.4), channel_id=1, source_target_pairs={{0,15},{1,2},{2,1},{3,4},{4,3},{5,6},{6,5},{7,8},{8,7},{9,10},{10,... | collective-permute-start | bytes 786440 | tf_op jit(solution)/shard_map/ppermute | solution.py:42
  113.8 2.0 %stay_product.4 = bf16[4,2,2,32,256]{4,3,2,1,0:T(8,128)(2,1)S(1)} custom-call(s32[10]{0:T(128)S(1)} %pad_add_fusion.refs_0_, bf16[16,2,64,256]{3,2,1,0:T(8,128)(2,1)S(1)} %bitcast.30, bf16[512,1024]{1,0:T(8,128)(2,1)S(1)} %dense_panel.1.refs_2_, bf16[512,1024]{1,0:T(8,128)(2,1)S(1)} %collective-permute-done.refs_3_, ...), custom_call_target="tpu_custom_call" | custom-call | tf_op jit(solution)/shard_map/stay_product/pallas_call | solution.py:100
  117.6 15.0 %all_to_all.42 = bf16[4,128,256]{2,1,0:T(8,128)(2,1)S(1)} all-to-all(bf16[4,128,256]{2,1,0:T(8,128)(2,1)S(1)} %bitcast.35), channel_id=1, replica_groups={{1,5,10,14},{2,6,9,13},{3,7,12,0},{4,8,11,15},{17,21,26,30},{18,22,25,2..., dimensions={0} | all-to-all | bytes 524288 | tf_op jit(solution)/shard_map/all_to_all | solution.py:38
  132.8 15.6 %all_to_all.43 = bf16[16,128,256]{2,1,0:T(8,128)(2,1)S(1)} all-to-all(bf16[16,128,256]{2,1,0:T(8,128)(2,1)S(1)} %broadcast_in_dim.14), channel_id=1, replica_groups=mesh['x'=4,'y'=4,'c'=2,'z'=16] {'x','y'}, dimensions={0} | all-to-all | bytes 2097152 | tf_op jit(solution)/shard_map/all_to_all | solution.py:38
  148.4 2.0 go_product.5
  150.4 12.7 %collective-permute-start.5 = (bf16[4,2,2,32,256]{4,3,2,1,0:T(8,128)(2,1)S(1)}, bf16[4,2,2,32,256]{4,3,2,1,0:T(8,128)(2,1)S(1)}, u32[]{:S(2)}, u32[]{:S(2)}) collective-permute-start(bf16[4,2,2,32,256]{4,3,2,1,0:T(8,128)(2,1)S(1)} %go_product.5), channel_id=1, source_target_pairs={{0,15},{1,2},{2,1},{3,4},{4,3},{5,6},{6,5},{7,8},{8,7},{9,10},{10,... | collective-permute-start | bytes 786440 | tf_op jit(solution)/shard_map/ppermute | solution.py:42
  163.2 2.0 stay_product.5
  165.2 1.7 collective-permute-done.5
  167.0 12.2 %all_to_all.44 = bf16[4,128,256]{2,1,0:T(8,128)(2,1)S(1)} all-to-all(bf16[4,128,256]{2,1,0:T(8,128)(2,1)S(1)} %bitcast.36), channel_id=1, replica_groups={{1,5,10,14},{2,6,9,13},{3,7,12,0},{4,8,11,15},{17,21,26,30},{18,22,25,2..., dimensions={0} | all-to-all | bytes 524288 | tf_op jit(solution)/shard_map/all_to_all | solution.py:38
  180.0 17.2 %all-to-all-start.7 = ((bf16[4,3,32,256]{3,2,1,0:T(8,128)(2,1)}), bf16[4,3,32,256]{3,2,1,0:T(8,128)(2,1)S(1)}, u32[]{:S(2)}, u32[]{:S(2)}) async-start(bf16[4,3,32,256]{3,2,1,0:T(8,128)(2,1)} %pad_maximum_fusion), calls=%async_computation.7 | async-start | bytes 393216 | tf_op jit(solution)/shard_map/all_to_all | solution.py:38
  197.3 4.1 %all-to-all-done.7.back = bf16[4,3,32,256]{3,2,1,0:T(8,128)(2,1)S(1)} async-done(((bf16[4,3,32,256]{3,2,1,0:T(8,128)(2,1)}), bf16[4,3,32,256]{3,2,1,0:T(8,128)(2,1)S(1)}, u32[]{:S(2)}, u32[]{:S(2)}) %all-to-all-start.7) | async-done | bytes 196640 | tf_op jit(solution)/shard_map/all_to_all | solution.py:38
  (38 shorter events, 12.7 us)
Async XLA Ops:
  0.6 0.7 copy-start.3
  2.8 16.3 %all-to-all-start = ((bf16[4,32,384]{2,1,0:T(8,128)(2,1)}), bf16[4,32,384]{2,1,0:T(8,128)(2,1)S(1)}, u32[]{:S(2)}, u32[]{:S(2)}) async-start(bf16[4,32,384]{2,1,0:T(8,128)(2,1)} %maximum_select_fusion), calls=%async_computation | async-start | bytes 196608 | tf_op jit(solution)/shard_map/all_to_all | solution.py:38
  13.0 0.7 copy-start.1
  13.0 0.7 copy-start.2
  13.7 1.2 copy-start
  15.9 26.7 %collective-permute-start = (bf16[512,1024]{1,0:T(8,128)(2,1)S(1)}, bf16[512,1024]{1,0:T(8,128)(2,1)S(1)}, u32[]{:S(2)}, u32[]{:S(2)}) collective-permute-start(bf16[512,1024]{1,0:T(8,128)(2,1)S(1)} %dense_panel.1.refs_2_), channel_id=1, source_target_pairs={{0,1},{1,0},{2,3},{3,2},{4,5},{5,4},{6,7},{7,6},{8,9},{9,8},{10,11... | collective-permute-start | bytes 3145736 | tf_op jit(solution)/shard_map/ppermute | solution.py:42
  20.5 22.1 %all-to-all-start.1 = ((bf16[16,128,256]{2,1,0:T(8,128)(2,1)}), bf16[16,128,256]{2,1,0:T(8,128)(2,1)}, u32[]{:S(2)}, u32[]{:S(2)}) async-start(bf16[16,128,256]{2,1,0:T(8,128)(2,1)} %broadcast_in_dim.12), calls=%async_computation.1 | async-start | bytes 2097152 | tf_op jit(solution)/shard_map/all_to_all | solution.py:38
  24.8 21.4 %collective-permute-start.1 = (bf16[512,1024]{1,0:T(8,128)(2,1)S(1)}, bf16[512,1024]{1,0:T(8,128)(2,1)S(1)}, u32[]{:S(2)}, u32[]{:S(2)}) collective-permute-start(bf16[512,1024]{1,0:T(8,128)(2,1)S(1)} %dense_panel.1.refs_2_), channel_id=1, source_target_pairs={{0,16},{16,0},{1,17},{17,1},{2,18},{18,2},{3,19},{19,3},{4,20},{20... | collective-permute-start | bytes 3145736 | tf_op jit(solution)/shard_map/ppermute | solution.py:42
  42.5 5.3 %collective-permute-start.2 = (bf16[512,1024]{1,0:T(8,128)(2,1)S(1)}, bf16[512,1024]{1,0:T(8,128)(2,1)}, u32[]{:S(2)}, u32[]{:S(2)}) collective-permute-start(bf16[512,1024]{1,0:T(8,128)(2,1)S(1)} %collective-permute-done.refs_3_), channel_id=1, source_target_pairs={{0,16},{16,0},{1,17},{17,1},{2,18},{18,2},{3,19},{19,3},{4,20},{20... | collective-permute-start | bytes 3145736 | tf_op jit(solution)/shard_map/ppermute | solution.py:42
  50.2 14.0 %collective-permute-start.3 = (bf16[4,2,2,32,256]{4,3,2,1,0:T(8,128)(2,1)S(1)}, bf16[4,2,2,32,256]{4,3,2,1,0:T(8,128)(2,1)S(1)}, u32[]{:S(2)}, u32[]{:S(2)}) collective-permute-start(bf16[4,2,2,32,256]{4,3,2,1,0:T(8,128)(2,1)S(1)} %go_product.3), channel_id=1, source_target_pairs={{0,15},{1,2},{2,1},{3,4},{4,3},{5,6},{6,5},{7,8},{8,7},{9,10},{10,... | collective-permute-start | bytes 786440 | tf_op jit(solution)/shard_map/ppermute | solution.py:42
  98.4 19.1 %collective-permute-start.4 = (bf16[4,2,2,32,256]{4,3,2,1,0:T(8,128)(2,1)S(1)}, bf16[4,2,2,32,256]{4,3,2,1,0:T(8,128)(2,1)S(1)}, u32[]{:S(2)}, u32[]{:S(2)}) collective-permute-start(bf16[4,2,2,32,256]{4,3,2,1,0:T(8,128)(2,1)S(1)} %go_product.4), channel_id=1, source_target_pairs={{0,15},{1,2},{2,1},{3,4},{4,3},{5,6},{6,5},{7,8},{8,7},{9,10},{10,... | collective-permute-start | bytes 786440 | tf_op jit(solution)/shard_map/ppermute | solution.py:42
  150.4 16.5 %collective-permute-start.5 = (bf16[4,2,2,32,256]{4,3,2,1,0:T(8,128)(2,1)S(1)}, bf16[4,2,2,32,256]{4,3,2,1,0:T(8,128)(2,1)S(1)}, u32[]{:S(2)}, u32[]{:S(2)}) collective-permute-start(bf16[4,2,2,32,256]{4,3,2,1,0:T(8,128)(2,1)S(1)} %go_product.5), channel_id=1, source_target_pairs={{0,15},{1,2},{2,1},{3,4},{4,3},{5,6},{6,5},{7,8},{8,7},{9,10},{10,... | collective-permute-start | bytes 786440 | tf_op jit(solution)/shard_map/ppermute | solution.py:42
  180.0 21.4 %all-to-all-start.7 = ((bf16[4,3,32,256]{3,2,1,0:T(8,128)(2,1)}), bf16[4,3,32,256]{3,2,1,0:T(8,128)(2,1)S(1)}, u32[]{:S(2)}, u32[]{:S(2)}) async-start(bf16[4,3,32,256]{3,2,1,0:T(8,128)(2,1)} %pad_maximum_fusion), calls=%async_computation.7 | async-start | bytes 393216 | tf_op jit(solution)/shard_map/all_to_all | solution.py:38

commit v7 on v6

--- a/solution.py
+++ b/solution.py
@@ -16,7 +16,7 @@
 ]
 NEIGHBOURS = [(z, (z + 1 if z % 2 else z - 1) % LENGTH) for z in range(LENGTH)]
 SUM_GROUPS = [
-    [(STEP * k + first + (side if k < STEP // 2 else 1 - side)) % LENGTH for k in range(STEP)]
+    [(STEP * k + first + side) % LENGTH for k in range(STEP)]
     for first in (1, 3)
     for side in range(2)
 ]

time: 204 us -> 203 us (level)
  starting transfers between devices: 76.2 us -> 44.7 us
  blocking collectives: 74.6 us -> 99.8 us
  waiting for transfers between devices: 28.3 us -> 34.3 us
    all_to_all x5, blocking collectives: 74.6 us -> 99.8 us  [exchange(): return lax.all_to_all(x, axes, 0, 0, tiled=True, axis_index_groups=groups)]
    ppermute x6, starting transfers between devices: 44.5 us -> 22.1 us  [swap(): return lax.ppermute(x, axis, pairs)]
    all_to_all x3, starting transfers between devices: 31.7 us -> 22.6 us  [exchange(): return lax.all_to_all(x, axes, 0, 0, tiled=True, axis_index_groups=groups)]
    ppermute x6, waiting for transfers between devices: 24.2 us -> 29.8 us  [swap(): return lax.ppermute(x, axis, pairs)]
where the time goes in v7:
time: 203 us; the launch traced here: 202 us
  blocking collectives  99.8 us (49%)
  starting transfers between devices  44.7 us (22%)
  waiting for transfers between devices  34.3 us (17%)
  Pallas kernels  14.4 us (7%)
  local copies, waits for them, and re-layouts  5.45 us (3%)
  other arithmetic  2.21 us (1%)
    all_to_all x5, blocking collectives, exchange(): return lax.all_to_all(x, axes, 0, 0, tiled=True, axis_index_groups=groups)  99.8 us
    ppermute x6, waiting for transfers between devices, swap(): return lax.ppermute(x, axis, pairs)  29.8 us
    all_to_all x3, starting transfers between devices, exchange(): return lax.all_to_all(x, axes, 0, 0, tiled=True, axis_index_groups=groups)  22.6 us
    ppermute x6, starting transfers between devices, swap(): return lax.ppermute(x, axis, pairs)  22.1 us
    pallas_call x6, Pallas kernels, product(): pl.pallas_call(body, out_shape=jax.ShapeDtypeStruct((STEP, pair, 2, rows...  12.7 us
    all_to_all x3, waiting for transfers between devices, exchange(): return lax.all_to_all(x, axes, 0, 0, tiled=True, axis_index_groups=groups)  4.47 us
  transfers between devices with their start and end apart: 9, of which 6 were waited for; matrix products, arithmetic and copies ran while one was open for 1% of the time, Pallas kernels for 4%

profile of v7, /device:TPU:1, one launch (start us, length us, event | category | flops | bytes accessed | tf_op | source)
XLA Modules:
  0.0 201.7 jit_solution(13717068333343611877)
XLA Ops:
  2.8 10.1 %all-to-all-start = ((bf16[4,32,384]{2,1,0:T(8,128)(2,1)}), bf16[4,32,384]{2,1,0:T(8,128)(2,1)S(1)}, u32[]{:S(2)}, u32[]{:S(2)}) async-start(bf16[4,32,384]{2,1,0:T(8,128)(2,1)} %maximum_select_fusion), calls=%async_computation | async-start | bytes 196608 | tf_op jit(solution)/shard_map/all_to_all | solution.py:38
  15.8 3.3 %collective-permute-start = (bf16[512,1024]{1,0:T(8,128)(2,1)S(1)}, bf16[512,1024]{1,0:T(8,128)(2,1)S(1)}, u32[]{:S(2)}, u32[]{:S(2)}) collective-permute-start(bf16[512,1024]{1,0:T(8,128)(2,1)S(1)} %dense_panel.1.refs_2_), channel_id=1, source_target_pairs={{0,1},{1,0},{2,3},{3,2},{4,5},{5,4},{6,7},{7,6},{8,9},{9,8},{10,11... | collective-permute-start | bytes 3145736 | tf_op jit(solution)/shard_map/ppermute | solution.py:42
  20.5 4.3 %all-to-all-start.1 = ((bf16[16,128,256]{2,1,0:T(8,128)(2,1)}), bf16[16,128,256]{2,1,0:T(8,128)(2,1)}, u32[]{:S(2)}, u32[]{:S(2)}) async-start(bf16[16,128,256]{2,1,0:T(8,128)(2,1)} %broadcast_in_dim.12), calls=%async_computation.1 | async-start | bytes 2097152 | tf_op jit(solution)/shard_map/all_to_all | solution.py:38
  24.8 2.6 %collective-permute-start.1 = (bf16[512,1024]{1,0:T(8,128)(2,1)S(1)}, bf16[512,1024]{1,0:T(8,128)(2,1)S(1)}, u32[]{:S(2)}, u32[]{:S(2)}) collective-permute-start(bf16[512,1024]{1,0:T(8,128)(2,1)S(1)} %dense_panel.1.refs_2_), channel_id=1, source_target_pairs={{0,16},{16,0},{1,17},{17,1},{2,18},{18,2},{3,19},{19,3},{4,20},{20... | collective-permute-start | bytes 3145736 | tf_op jit(solution)/shard_map/ppermute | solution.py:42
  27.4 15.1 %collective-permute-done.refs_3_ = bf16[512,1024]{1,0:T(8,128)(2,1)S(1)} collective-permute-done((bf16[512,1024]{1,0:T(8,128)(2,1)S(1)}, bf16[512,1024]{1,0:T(8,128)(2,1)S(1)}, u32[]{:S(2)}, u32[]{:S(2)}) %collective-permute-start) | collective-permute-done | bytes 1048608 | tf_op jit(solution)/shard_map/ppermute | solution.py:42
  42.5 3.0 %collective-permute-start.2 = (bf16[512,1024]{1,0:T(8,128)(2,1)S(1)}, bf16[512,1024]{1,0:T(8,128)(2,1)}, u32[]{:S(2)}, u32[]{:S(2)}) collective-permute-start(bf16[512,1024]{1,0:T(8,128)(2,1)S(1)} %collective-permute-done.refs_3_), channel_id=1, source_target_pairs={{0,16},{16,0},{1,17},{17,1},{2,18},{18,2},{3,19},{19,3},{4,20},{20... | collective-permute-start | bytes 3145736 | tf_op jit(solution)/shard_map/ppermute | solution.py:42
  47.9 2.3 %go_product.3 = bf16[4,2,2,32,256]{4,3,2,1,0:T(8,128)(2,1)S(1)} custom-call(s32[10]{0:T(128)S(1)} %pad_add_fusion.refs_0_, bf16[16,2,64,256]{3,2,1,0:T(8,128)(2,1)} %bitcast.10.refs_1_, bf16[512,1024]{1,0:T(8,128)(2,1)S(1)} %dense_panel.1.refs_2_, bf16[512,1024]{1,0:T(8,128)(2,1)S(1)} %collective-permute-done.refs_3_, ...), custom_call_target="tpu_custom_call" | custom-call | tf_op jit(solution)/shard_map/go_product/pallas_call | solution.py:100
  50.2 7.7 %collective-permute-start.3 = (bf16[4,2,2,32,256]{4,3,2,1,0:T(8,128)(2,1)S(1)}, bf16[4,2,2,32,256]{4,3,2,1,0:T(8,128)(2,1)S(1)}, u32[]{:S(2)}, u32[]{:S(2)}) collective-permute-start(bf16[4,2,2,32,256]{4,3,2,1,0:T(8,128)(2,1)S(1)} %go_product.3), channel_id=1, source_target_pairs={{0,15},{1,2},{2,1},{3,4},{4,3},{5,6},{6,5},{7,8},{8,7},{9,10},{10,... | collective-permute-start | bytes 786440 | tf_op jit(solution)/shard_map/ppermute | solution.py:42
  57.9 2.3 %stay_product.3 = bf16[4,2,2,32,256]{4,3,2,1,0:T(8,128)(2,1)S(1)} custom-call(s32[10]{0:T(128)S(1)} %pad_add_fusion.refs_0_, bf16[16,2,64,256]{3,2,1,0:T(8,128)(2,1)} %bitcast.10.refs_1_, bf16[512,1024]{1,0:T(8,128)(2,1)S(1)} %dense_panel.1.refs_2_, bf16[512,1024]{1,0:T(8,128)(2,1)S(1)} %collective-permute-done.refs_3_, ...), custom_call_target="tpu_custom_call" | custom-call | tf_op jit(solution)/shard_map/stay_product/pallas_call | solution.py:100
  60.2 4.0 %collective-permute-done.3 = bf16[4,2,2,32,256]{4,3,2,1,0:T(8,128)(2,1)S(1)} collective-permute-done((bf16[4,2,2,32,256]{4,3,2,1,0:T(8,128)(2,1)S(1)}, bf16[4,2,2,32,256]{4,3,2,1,0:T(8,128)(2,1)S(1)}, u32[]{:S(2)}, u32[]{:S(2)}) %collective-permute-start.3) | collective-permute-done | bytes 262176 | tf_op jit(solution)/shard_map/ppermute | solution.py:42
  64.3 27.4 %all_to_all.40 = bf16[4,128,256]{2,1,0:T(8,128)(2,1)S(1)} all-to-all(bf16[4,128,256]{2,1,0:T(8,128)(2,1)S(1)} %bitcast.34), channel_id=1, replica_groups={{1,5,9,13},{2,6,10,14},{3,7,11,15},{4,8,12,0},{17,21,25,29},{18,22,26,3..., dimensions={0} | all-to-all | bytes 524288 | tf_op jit(solution)/shard_map/all_to_all | solution.py:38
  91.9 18.5 %all_to_all.41 = bf16[16,128,256]{2,1,0:T(8,128)(2,1)S(1)} all-to-all(bf16[16,128,256]{2,1,0:T(8,128)(2,1)S(1)} %broadcast_in_dim.13), channel_id=1, replica_groups=mesh['x'=4,'y'=4,'c'=2,'z'=16] {'x','y'}, dimensions={0} | all-to-all | bytes 2097152 | tf_op jit(solution)/shard_map/all_to_all | solution.py:38
  110.4 2.0 go_product.4
  114.4 2.0 %stay_product.4 = bf16[4,2,2,32,256]{4,3,2,1,0:T(8,128)(2,1)S(1)} custom-call(s32[10]{0:T(128)S(1)} %pad_add_fusion.refs_0_, bf16[16,2,64,256]{3,2,1,0:T(8,128)(2,1)S(1)} %bitcast.30, bf16[512,1024]{1,0:T(8,128)(2,1)S(1)} %dense_panel.1.refs_2_, bf16[512,1024]{1,0:T(8,128)(2,1)S(1)} %collective-permute-done.refs_3_, ...), custom_call_target="tpu_custom_call" | custom-call | tf_op jit(solution)/shard_map/stay_product/pallas_call | solution.py:100
  116.4 4.4 %collective-permute-done.4 = bf16[4,2,2,32,256]{4,3,2,1,0:T(8,128)(2,1)S(1)} collective-permute-done((bf16[4,2,2,32,256]{4,3,2,1,0:T(8,128)(2,1)S(1)}, bf16[4,2,2,32,256]{4,3,2,1,0:T(8,128)(2,1)S(1)}, u32[]{:S(2)}, u32[]{:S(2)}) %collective-permute-start.4) | collective-permute-done | bytes 262176 | tf_op jit(solution)/shard_map/ppermute | solution.py:42
  120.9 18.1 %all_to_all.42 = bf16[4,128,256]{2,1,0:T(8,128)(2,1)S(1)} all-to-all(bf16[4,128,256]{2,1,0:T(8,128)(2,1)S(1)} %bitcast.35), channel_id=1, replica_groups={{1,5,9,13},{2,6,10,14},{3,7,11,15},{4,8,12,0},{17,21,25,29},{18,22,26,3..., dimensions={0} | all-to-all | bytes 524288 | tf_op jit(solution)/shard_map/all_to_all | solution.py:38
  139.2 17.6 %all_to_all.43 = bf16[16,128,256]{2,1,0:T(8,128)(2,1)S(1)} all-to-all(bf16[16,128,256]{2,1,0:T(8,128)(2,1)S(1)} %broadcast_in_dim.14), channel_id=1, replica_groups=mesh['x'=4,'y'=4,'c'=2,'z'=16] {'x','y'}, dimensions={0} | all-to-all | bytes 2097152 | tf_op jit(solution)/shard_map/all_to_all | solution.py:38
  156.8 2.0 go_product.5
  158.8 3.7 %collective-permute-start.5 = (bf16[4,2,2,32,256]{4,3,2,1,0:T(8,128)(2,1)S(1)}, bf16[4,2,2,32,256]{4,3,2,1,0:T(8,128)(2,1)S(1)}, u32[]{:S(2)}, u32[]{:S(2)}) collective-permute-start(bf16[4,2,2,32,256]{4,3,2,1,0:T(8,128)(2,1)S(1)} %go_product.5), channel_id=1, source_target_pairs={{0,15},{1,2},{2,1},{3,4},{4,3},{5,6},{6,5},{7,8},{8,7},{9,10},{10,... | collective-permute-start | bytes 786440 | tf_op jit(solution)/shard_map/ppermute | solution.py:42
  162.5 2.0 %stay_product.5 = bf16[4,2,2,32,256]{4,3,2,1,0:T(8,128)(2,1)S(1)} custom-call(s32[10]{0:T(128)S(1)} %pad_add_fusion.refs_0_, bf16[16,2,64,256]{3,2,1,0:T(8,128)(2,1)S(1)} %bitcast.28, bf16[512,1024]{1,0:T(8,128)(2,1)S(1)} %dense_panel.1.refs_2_, bf16[512,1024]{1,0:T(8,128)(2,1)S(1)} %collective-permute-done.refs_3_, ...), custom_call_target="tpu_custom_call" | custom-call | tf_op jit(solution)/shard_map/stay_product/pallas_call | solution.py:100
  164.5 4.7 %collective-permute-done.5 = bf16[4,2,2,32,256]{4,3,2,1,0:T(8,128)(2,1)S(1)} collective-permute-done((bf16[4,2,2,32,256]{4,3,2,1,0:T(8,128)(2,1)S(1)}, bf16[4,2,2,32,256]{4,3,2,1,0:T(8,128)(2,1)S(1)}, u32[]{:S(2)}, u32[]{:S(2)}) %collective-permute-start.5) | collective-permute-done | bytes 262176 | tf_op jit(solution)/shard_map/ppermute | solution.py:42
  169.3 18.3 %all_to_all.44 = bf16[4,128,256]{2,1,0:T(8,128)(2,1)S(1)} all-to-all(bf16[4,128,256]{2,1,0:T(8,128)(2,1)S(1)} %bitcast.36), channel_id=1, replica_groups={{1,5,9,13},{2,6,10,14},{3,7,11,15},{4,8,12,0},{17,21,25,29},{18,22,26,3..., dimensions={0} | all-to-all | bytes 524288 | tf_op jit(solution)/shard_map/all_to_all | solution.py:38
  188.4 8.1 %all-to-all-start.7 = ((bf16[4,3,32,256]{3,2,1,0:T(8,128)(2,1)}), bf16[4,3,32,256]{3,2,1,0:T(8,128)(2,1)S(1)}, u32[]{:S(2)}, u32[]{:S(2)}) async-start(bf16[4,3,32,256]{3,2,1,0:T(8,128)(2,1)} %pad_maximum_fusion), calls=%async_computation.7 | async-start | bytes 393216 | tf_op jit(solution)/shard_map/all_to_all | solution.py:38
  196.5 4.5 %all-to-all-done.7.back = bf16[4,3,32,256]{3,2,1,0:T(8,128)(2,1)S(1)} async-done(((bf16[4,3,32,256]{3,2,1,0:T(8,128)(2,1)}), bf16[4,3,32,256]{3,2,1,0:T(8,128)(2,1)S(1)}, u32[]{:S(2)}, u32[]{:S(2)}) %all-to-all-start.7) | async-done | bytes 196640 | tf_op jit(solution)/shard_map/all_to_all | solution.py:38
  (38 shorter events, 12.8 us)
Async XLA Ops:
  0.6 0.7 copy-start.3
  2.8 16.3 %all-to-all-start = ((bf16[4,32,384]{2,1,0:T(8,128)(2,1)}), bf16[4,32,384]{2,1,0:T(8,128)(2,1)S(1)}, u32[]{:S(2)}, u32[]{:S(2)}) async-start(bf16[4,32,384]{2,1,0:T(8,128)(2,1)} %maximum_select_fusion), calls=%async_computation | async-start | bytes 196608 | tf_op jit(solution)/shard_map/all_to_all | solution.py:38
  13.0 0.7 copy-start.1
  13.0 0.7 copy-start.2
  13.7 1.2 copy-start
  15.8 26.6 %collective-permute-start = (bf16[512,1024]{1,0:T(8,128)(2,1)S(1)}, bf16[512,1024]{1,0:T(8,128)(2,1)S(1)}, u32[]{:S(2)}, u32[]{:S(2)}) collective-permute-start(bf16[512,1024]{1,0:T(8,128)(2,1)S(1)} %dense_panel.1.refs_2_), channel_id=1, source_target_pairs={{0,1},{1,0},{2,3},{3,2},{4,5},{5,4},{6,7},{7,6},{8,9},{9,8},{10,11... | collective-permute-start | bytes 3145736 | tf_op jit(solution)/shard_map/ppermute | solution.py:42
  20.5 22.0 %all-to-all-start.1 = ((bf16[16,128,256]{2,1,0:T(8,128)(2,1)}), bf16[16,128,256]{2,1,0:T(8,128)(2,1)}, u32[]{:S(2)}, u32[]{:S(2)}) async-start(bf16[16,128,256]{2,1,0:T(8,128)(2,1)} %broadcast_in_dim.12), calls=%async_computation.1 | async-start | bytes 2097152 | tf_op jit(solution)/shard_map/all_to_all | solution.py:38
  24.8 21.4 %collective-permute-start.1 = (bf16[512,1024]{1,0:T(8,128)(2,1)S(1)}, bf16[512,1024]{1,0:T(8,128)(2,1)S(1)}, u32[]{:S(2)}, u32[]{:S(2)}) collective-permute-start(bf16[512,1024]{1,0:T(8,128)(2,1)S(1)} %dense_panel.1.refs_2_), channel_id=1, source_target_pairs={{0,16},{16,0},{1,17},{17,1},{2,18},{18,2},{3,19},{19,3},{4,20},{20... | collective-permute-start | bytes 3145736 | tf_op jit(solution)/shard_map/ppermute | solution.py:42
  42.5 5.4 %collective-permute-start.2 = (bf16[512,1024]{1,0:T(8,128)(2,1)S(1)}, bf16[512,1024]{1,0:T(8,128)(2,1)}, u32[]{:S(2)}, u32[]{:S(2)}) collective-permute-start(bf16[512,1024]{1,0:T(8,128)(2,1)S(1)} %collective-permute-done.refs_3_), channel_id=1, source_target_pairs={{0,16},{16,0},{1,17},{17,1},{2,18},{18,2},{3,19},{19,3},{4,20},{20... | collective-permute-start | bytes 3145736 | tf_op jit(solution)/shard_map/ppermute | solution.py:42
  50.2 14.0 %collective-permute-start.3 = (bf16[4,2,2,32,256]{4,3,2,1,0:T(8,128)(2,1)S(1)}, bf16[4,2,2,32,256]{4,3,2,1,0:T(8,128)(2,1)S(1)}, u32[]{:S(2)}, u32[]{:S(2)}) collective-permute-start(bf16[4,2,2,32,256]{4,3,2,1,0:T(8,128)(2,1)S(1)} %go_product.3), channel_id=1, source_target_pairs={{0,15},{1,2},{2,1},{3,4},{4,3},{5,6},{6,5},{7,8},{8,7},{9,10},{10,... | collective-permute-start | bytes 786440 | tf_op jit(solution)/shard_map/ppermute | solution.py:42
  112.5 8.3 %collective-permute-start.4 = (bf16[4,2,2,32,256]{4,3,2,1,0:T(8,128)(2,1)S(1)}, bf16[4,2,2,32,256]{4,3,2,1,0:T(8,128)(2,1)S(1)}, u32[]{:S(2)}, u32[]{:S(2)}) collective-permute-start(bf16[4,2,2,32,256]{4,3,2,1,0:T(8,128)(2,1)S(1)} %go_product.4), channel_id=1, source_target_pairs={{0,15},{1,2},{2,1},{3,4},{4,3},{5,6},{6,5},{7,8},{8,7},{9,10},{10,... | collective-permute-start | bytes 786440 | tf_op jit(solution)/shard_map/ppermute | solution.py:42
  158.8 10.4 %collective-permute-start.5 = (bf16[4,2,2,32,256]{4,3,2,1,0:T(8,128)(2,1)S(1)}, bf16[4,2,2,32,256]{4,3,2,1,0:T(8,128)(2,1)S(1)}, u32[]{:S(2)}, u32[]{:S(2)}) collective-permute-start(bf16[4,2,2,32,256]{4,3,2,1,0:T(8,128)(2,1)S(1)} %go_product.5), channel_id=1, source_target_pairs={{0,15},{1,2},{2,1},{3,4},{4,3},{5,6},{6,5},{7,8},{8,7},{9,10},{10,... | collective-permute-start | bytes 786440 | tf_op jit(solution)/shard_map/ppermute | solution.py:42
  188.4 12.6 %all-to-all-start.7 = ((bf16[4,3,32,256]{3,2,1,0:T(8,128)(2,1)}), bf16[4,3,32,256]{3,2,1,0:T(8,128)(2,1)S(1)}, u32[]{:S(2)}, u32[]{:S(2)}) async-start(bf16[4,3,32,256]{3,2,1,0:T(8,128)(2,1)} %pad_maximum_fusion), calls=%async_computation.7 | async-start | bytes 393216 | tf_op jit(solution)/shard_map/all_to_all | solution.py:38

commit v8 on v7

--- a/solution.py
+++ b/solution.py
@@ -108,23 +108,26 @@
     )(place, whole, *panels)
 
 
-def collect_kernel(crossed, back, *outs):
-    _, _, _, width = back.shape
+def collect_kernel(crossed, early, late, *outs):
+    _, n_early, _, width = early.shape
     for q in range(4):
+        at = q ^ 2 * crossed[0]
         for k, out in enumerate(outs):
-            out[:, q * width : (q + 1) * width] = back[q ^ 2 * crossed[0], k]
-
-
-def collect(crossed, back):
-    _, hops, rows, width = back.shape
+            part = early[at, k] if k < n_early else late[at, k - n_early]
+            out[:, q * width : (q + 1) * width] = part
+
+
+def collect(crossed, early, late):
+    _, n_early, rows, width = early.shape
+    hops = n_early + late.shape[1]
     return pl.pallas_call(
         collect_kernel,
-        out_shape=(jax.ShapeDtypeStruct((rows, 4 * width), back.dtype),) * hops,
-        in_specs=[SMEM, VMEM],
+        out_shape=(jax.ShapeDtypeStruct((rows, 4 * width), early.dtype),) * hops,
+        in_specs=[SMEM, VMEM, VMEM],
         out_specs=(VMEM,) * hops,
         compiler_params=pltpu.CompilerParams(vmem_limit_bytes=8 << 20),
         name="collect_rows",
-    )(crossed, back)
+    )(crossed, early, late)
 
 
 def on_device(features, degree, blocks, block_cols, block_count):
@@ -165,16 +168,21 @@
             copies = jnp.broadcast_to(sent[None], (plane,) + sent.shape)
             whole = exchange(copies, PLANE)
         whole = whole.reshape(plane, 2, 2 * rows, width)
-        come = swap(product(STEP, place, whole, panels), "z", NEIGHBOURS)
+        go = product(STEP, place, whole, panels)
+        come = swap(go, "z", NEIGHBOURS)
+        if hop == HOPS - 1:
+            early = exchange(after(jnp.stack(hops, axis=1), go), ("c", "z"), TILE_GROUPS)
         stay = product(0, place, whole, panels)
+        if hop == HOPS - 1:
+            stay = after(stay, early)
         both = (stay.astype(f32) + come.astype(f32)).astype(bf16)
         parts = exchange(both.reshape(STEP, pooled, width), "z", SUM_GROUPS)
         total = jnp.sum(parts.astype(f32), axis=0)
         value = (scale * (total + sent.astype(f32))).astype(bf16)
         sent = (scale * value.astype(f32)).astype(bf16)
         hops.append(value.reshape(4, rows, width))
-    back = exchange(jnp.stack(hops, axis=1), ("c", "z"), TILE_GROUPS)
-    return collect(((z & 2) >> 1).astype(jnp.int32)[None], back)
+    late = exchange(hops[-1], ("c", "z"), TILE_GROUPS)[:, None]
+    return collect(((z & 2) >> 1).astype(jnp.int32)[None], early, late)
 
 
 def solution(mesh):

time: 203 us -> 218 us (1.074)
  waiting for transfers between devices: 34.3 us -> 45.5 us
  blocking collectives: 99.8 us -> 88.8 us
  starting transfers between devices: 44.7 us -> 55.1 us
    all_to_all x5 -> x4, blocking collectives: 99.8 us -> 88.8 us  [exchange(): return lax.all_to_all(x, axes, 0, 0, tiled=True, axis_index_groups=groups)]
    all_to_all x3 -> x5, starting transfers between devices: 22.6 us -> 33.4 us  [exchange(): return lax.all_to_all(x, axes, 0, 0, tiled=True, axis_index_groups=groups)]
    all_to_all x3 -> x5, waiting for transfers between devices: 4.47 us -> 14.8 us  [exchange(): return lax.all_to_all(x, axes, 0, 0, tiled=True, axis_index_groups=groups)]
  transfers between devices with their start and end apart: 9 -> 11, of which waited for: 6 -> 7; matrix products, arithmetic and copies ran while one was open for 1% -> 1% of each run, Pallas kernels for 4% -> 4%
where the time goes in v8:
time: 218 us; the launch traced here: 216 us
  blocking collectives  88.8 us (41%)
  starting transfers between devices  55.1 us (25%)
  waiting for transfers between devices  45.5 us (21%)
  Pallas kernels  15.7 us (7%)
  local copies, waits for them, and re-layouts  6.58 us (3%)
  other arithmetic  3.78 us (2%)
    all_to_all x4, blocking collectives, exchange(): return lax.all_to_all(x, axes, 0, 0, tiled=True, axis_index_groups=groups)  88.8 us
    all_to_all x5, starting transfers between devices, exchange(): return lax.all_to_all(x, axes, 0, 0, tiled=True, axis_index_groups=groups)  33.4 us
    ppermute x6, waiting for transfers between devices, swap(): return lax.ppermute(x, axis, pairs)  30.7 us
    ppermute x6, starting transfers between devices, swap(): return lax.ppermute(x, axis, pairs)  21.8 us
    all_to_all x5, waiting for transfers between devices, exchange(): return lax.all_to_all(x, axes, 0, 0, tiled=True, axis_index_groups=groups)  14.8 us
    pallas_call x6, Pallas kernels, product(): pl.pallas_call(body, out_shape=jax.ShapeDtypeStruct((STEP, pair, 2, rows...  14.1 us
  transfers between devices with their start and end apart: 11, of which 7 were waited for; matrix products, arithmetic and copies ran while one was open for 1% of the time, Pallas kernels for 4%

profile of v8, /device:TPU:1, one launch (start us, length us, event | category | flops | bytes accessed | tf_op | source)
XLA Modules:
  0.0 216.4 jit_solution(3818307049715538792)
XLA Ops:
  2.2 10.1 %all-to-all-start = ((bf16[4,32,384]{2,1,0:T(8,128)(2,1)}), bf16[4,32,384]{2,1,0:T(8,128)(2,1)S(1)}, u32[]{:S(2)}, u32[]{:S(2)}) async-start(bf16[4,32,384]{2,1,0:T(8,128)(2,1)} %maximum_select_fusion), calls=%async_computation | async-start | bytes 196608 | tf_op jit(solution)/shard_map/all_to_all | solution.py:38
  15.2 3.3 %collective-permute-start = (bf16[512,1024]{1,0:T(8,128)(2,1)S(1)}, bf16[512,1024]{1,0:T(8,128)(2,1)S(1)}, u32[]{:S(2)}, u32[]{:S(2)}) collective-permute-start(bf16[512,1024]{1,0:T(8,128)(2,1)S(1)} %dense_panel.1.refs_2_), channel_id=1, source_target_pairs={{0,1},{1,0},{2,3},{3,2},{4,5},{5,4},{6,7},{7,6},{8,9},{9,8},{10,11... | collective-permute-start | bytes 3145736 | tf_op jit(solution)/shard_map/ppermute | solution.py:42
  19.8 4.3 %all-to-all-start.1 = ((bf16[16,128,256]{2,1,0:T(8,128)(2,1)}), bf16[16,128,256]{2,1,0:T(8,128)(2,1)}, u32[]{:S(2)}, u32[]{:S(2)}) async-start(bf16[16,128,256]{2,1,0:T(8,128)(2,1)} %broadcast_in_dim.14), calls=%async_computation.1 | async-start | bytes 2097152 | tf_op jit(solution)/shard_map/all_to_all | solution.py:38
  24.2 2.6 %collective-permute-start.1 = (bf16[512,1024]{1,0:T(8,128)(2,1)S(1)}, bf16[512,1024]{1,0:T(8,128)(2,1)S(1)}, u32[]{:S(2)}, u32[]{:S(2)}) collective-permute-start(bf16[512,1024]{1,0:T(8,128)(2,1)S(1)} %dense_panel.1.refs_2_), channel_id=1, source_target_pairs={{0,16},{16,0},{1,17},{17,1},{2,18},{18,2},{3,19},{19,3},{4,20},{20... | collective-permute-start | bytes 3145736 | tf_op jit(solution)/shard_map/ppermute | solution.py:42
  26.7 15.1 %collective-permute-done.refs_3_ = bf16[512,1024]{1,0:T(8,128)(2,1)S(1)} collective-permute-done((bf16[512,1024]{1,0:T(8,128)(2,1)S(1)}, bf16[512,1024]{1,0:T(8,128)(2,1)S(1)}, u32[]{:S(2)}, u32[]{:S(2)}) %collective-permute-start) | collective-permute-done | bytes 1048608 | tf_op jit(solution)/shard_map/ppermute | solution.py:42
  41.9 3.0 %collective-permute-start.2 = (bf16[512,1024]{1,0:T(8,128)(2,1)S(1)}, bf16[512,1024]{1,0:T(8,128)(2,1)}, u32[]{:S(2)}, u32[]{:S(2)}) collective-permute-start(bf16[512,1024]{1,0:T(8,128)(2,1)S(1)} %collective-permute-done.refs_3_), channel_id=1, source_target_pairs={{0,16},{16,0},{1,17},{17,1},{2,18},{18,2},{3,19},{19,3},{4,20},{20... | collective-permute-start | bytes 3145736 | tf_op jit(solution)/shard_map/ppermute | solution.py:42
  47.2 2.3 %go_product.3 = bf16[4,2,2,32,256]{4,3,2,1,0:T(8,128)(2,1)S(1)} custom-call(s32[10]{0:T(128)S(1)} %pad_add_fusion.refs_0_, bf16[16,2,64,256]{3,2,1,0:T(8,128)(2,1)} %bitcast.10.refs_1_, bf16[512,1024]{1,0:T(8,128)(2,1)S(1)} %dense_panel.1.refs_2_, bf16[512,1024]{1,0:T(8,128)(2,1)S(1)} %collective-permute-done.refs_3_, ...), custom_call_target="tpu_custom_call" | custom-call | tf_op jit(solution)/shard_map/go_product/pallas_call | solution.py:100
  49.6 7.6 %collective-permute-start.3 = (bf16[4,2,2,32,256]{4,3,2,1,0:T(8,128)(2,1)S(1)}, bf16[4,2,2,32,256]{4,3,2,1,0:T(8,128)(2,1)S(1)}, u32[]{:S(2)}, u32[]{:S(2)}) collective-permute-start(bf16[4,2,2,32,256]{4,3,2,1,0:T(8,128)(2,1)S(1)} %go_product.3), channel_id=1, source_target_pairs={{0,15},{1,2},{2,1},{3,4},{4,3},{5,6},{6,5},{7,8},{8,7},{9,10},{10,... | collective-permute-start | bytes 786440 | tf_op jit(solution)/shard_map/ppermute | solution.py:42
  57.2 2.3 %stay_product.3 = bf16[4,2,2,32,256]{4,3,2,1,0:T(8,128)(2,1)S(1)} custom-call(s32[10]{0:T(128)S(1)} %pad_add_fusion.refs_0_, bf16[16,2,64,256]{3,2,1,0:T(8,128)(2,1)} %bitcast.10.refs_1_, bf16[512,1024]{1,0:T(8,128)(2,1)S(1)} %dense_panel.1.refs_2_, bf16[512,1024]{1,0:T(8,128)(2,1)S(1)} %collective-permute-done.refs_3_, ...), custom_call_target="tpu_custom_call" | custom-call | tf_op jit(solution)/shard_map/stay_product/pallas_call | solution.py:100
  59.6 4.0 %collective-permute-done.3 = bf16[4,2,2,32,256]{4,3,2,1,0:T(8,128)(2,1)S(1)} collective-permute-done((bf16[4,2,2,32,256]{4,3,2,1,0:T(8,128)(2,1)S(1)}, bf16[4,2,2,32,256]{4,3,2,1,0:T(8,128)(2,1)S(1)}, u32[]{:S(2)}, u32[]{:S(2)}) %collective-permute-start.3) | collective-permute-done | bytes 262176 | tf_op jit(solution)/shard_map/ppermute | solution.py:42
  63.7 27.3 %all_to_all.45 = bf16[4,128,256]{2,1,0:T(8,128)(2,1)S(1)} all-to-all(bf16[4,128,256]{2,1,0:T(8,128)(2,1)S(1)} %bitcast.34), channel_id=1, replica_groups={{1,5,9,13},{2,6,10,14},{3,7,11,15},{4,8,12,0},{17,21,25,29},{18,22,26,3..., dimensions={0} | all-to-all | bytes 524288 | tf_op jit(solution)/shard_map/all_to_all | solution.py:38
  91.2 18.5 %all_to_all.46 = bf16[16,128,256]{2,1,0:T(8,128)(2,1)S(1)} all-to-all(bf16[16,128,256]{2,1,0:T(8,128)(2,1)S(1)} %broadcast_in_dim.15), channel_id=1, replica_groups=mesh['x'=4,'y'=4,'c'=2,'z'=16] {'x','y'}, dimensions={0} | all-to-all | bytes 2097152 | tf_op jit(solution)/shard_map/all_to_all | solution.py:38
  115.7 4.4 %collective-permute-done.4 = bf16[4,2,2,32,256]{4,3,2,1,0:T(8,128)(2,1)S(1)} collective-permute-done((bf16[4,2,2,32,256]{4,3,2,1,0:T(8,128)(2,1)S(1)}, bf16[4,2,2,32,256]{4,3,2,1,0:T(8,128)(2,1)S(1)}, u32[]{:S(2)}, u32[]{:S(2)}) %collective-permute-start.4) | collective-permute-done | bytes 262176 | tf_op jit(solution)/shard_map/ppermute | solution.py:42
  120.2 19.1 %all_to_all.47 = bf16[4,128,256]{2,1,0:T(8,128)(2,1)S(1)} all-to-all(bf16[4,128,256]{2,1,0:T(8,128)(2,1)S(1)} %bitcast.35), channel_id=1, replica_groups={{1,5,9,13},{2,6,10,14},{3,7,11,15},{4,8,12,0},{17,21,25,29},{18,22,26,3..., dimensions={0} | all-to-all | bytes 524288 | tf_op jit(solution)/shard_map/all_to_all | solution.py:38
  140.5 4.3 %all-to-all-start.5 = ((bf16[16,128,256]{2,1,0:T(8,128)(2,1)}), bf16[16,128,256]{2,1,0:T(8,128)(2,1)}, u32[]{:S(2)}, u32[]{:S(2)}) async-start(bf16[16,128,256]{2,1,0:T(8,128)(2,1)} %broadcast_in_dim.16), calls=%async_computation.5 | async-start | bytes 2097152 | tf_op jit(solution)/shard_map/all_to_all | solution.py:38
  145.5 11.6 %all-to-all-done.5 = bf16[16,128,256]{2,1,0:T(8,128)(2,1)} async-done(((bf16[16,128,256]{2,1,0:T(8,128)(2,1)}), bf16[16,128,256]{2,1,0:T(8,128)(2,1)}, u32[]{:S(2)}, u32[]{:S(2)}) %all-to-all-start.5) | async-done | bytes 1048608 | tf_op jit(solution)/shard_map/all_to_all | solution.py:38
  157.1 3.0 %go_product.5 = bf16[4,2,2,32,256]{4,3,2,1,0:T(8,128)(2,1)} custom-call(s32[10]{0:T(128)S(1)} %pad_add_fusion.refs_0_, bf16[16,2,64,256]{3,2,1,0:T(8,128)(2,1)} %bitcast.19.refs_1_, bf16[512,1024]{1,0:T(8,128)(2,1)S(1)} %dense_panel.1.refs_2_, bf16[512,1024]{1,0:T(8,128)(2,1)S(1)} %collective-permute-done.refs_3_, ...), custom_call_target="tpu_custom_call" | custom-call | tf_op jit(solution)/shard_map/go_product/pallas_call | solution.py:100
  160.1 9.1 %all-to-all-start.6 = ((bf16[4,2,32,256]{3,2,1,0:T(8,128)(2,1)}), bf16[4,2,32,256]{3,2,1,0:T(8,128)(2,1)S(1)}, u32[]{:S(2)}, u32[]{:S(2)}) async-start(bf16[4,2,32,256]{3,2,1,0:T(8,128)(2,1)} %pad_maximum_fusion), calls=%async_computation.6 | async-start | bytes 262144 | tf_op jit(solution)/shard_map/all_to_all | solution.py:38
  169.2 3.4 %collective-permute-start.5 = (bf16[4,2,2,32,256]{4,3,2,1,0:T(8,128)(2,1)}, bf16[4,2,2,32,256]{4,3,2,1,0:T(8,128)(2,1)}, u32[]{:S(2)}, u32[]{:S(2)}) collective-permute-start(bf16[4,2,2,32,256]{4,3,2,1,0:T(8,128)(2,1)} %go_product.5), channel_id=1, source_target_pairs={{0,15},{1,2},{2,1},{3,4},{4,3},{5,6},{6,5},{7,8},{8,7},{9,10},{10,... | collective-permute-start | bytes 786440 | tf_op jit(solution)/shard_map/ppermute | solution.py:42
  172.6 2.3 %stay_product.5 = bf16[4,2,2,32,256]{4,3,2,1,0:T(8,128)(2,1)S(1)} custom-call(s32[10]{0:T(128)S(1)} %pad_add_fusion.refs_0_, bf16[16,2,64,256]{3,2,1,0:T(8,128)(2,1)} %bitcast.19.refs_1_, bf16[512,1024]{1,0:T(8,128)(2,1)S(1)} %dense_panel.1.refs_2_, bf16[512,1024]{1,0:T(8,128)(2,1)S(1)} %collective-permute-done.refs_3_, ...), custom_call_target="tpu_custom_call" | custom-call | tf_op jit(solution)/shard_map/stay_product/pallas_call | solution.py:100
  175.0 5.5 %collective-permute-done.5 = bf16[4,2,2,32,256]{4,3,2,1,0:T(8,128)(2,1)} collective-permute-done((bf16[4,2,2,32,256]{4,3,2,1,0:T(8,128)(2,1)}, bf16[4,2,2,32,256]{4,3,2,1,0:T(8,128)(2,1)}, u32[]{:S(2)}, u32[]{:S(2)}) %collective-permute-start.5) | collective-permute-done | bytes 262176 | tf_op jit(solution)/shard_map/ppermute | solution.py:42
  181.5 23.9 %all_to_all.48 = bf16[4,128,256]{2,1,0:T(8,128)(2,1)S(1)} all-to-all(bf16[4,128,256]{2,1,0:T(8,128)(2,1)S(1)} %bitcast.36), channel_id=1, replica_groups={{1,5,9,13},{2,6,10,14},{3,7,11,15},{4,8,12,0},{17,21,25,29},{18,22,26,3..., dimensions={0} | all-to-all | bytes 524288 | tf_op jit(solution)/shard_map/all_to_all | solution.py:38
  207.0 5.4 %all-to-all-start.8 = ((bf16[4,32,256]{2,1,0:T(8,128)(2,1)}), bf16[4,32,256]{2,1,0:T(8,128)(2,1)S(1)}, u32[]{:S(2)}, u32[]{:S(2)}) async-start(bf16[4,32,256]{2,1,0:T(8,128)(2,1)} %bitcast.21), calls=%async_computation.8 | async-start | bytes 131072 | tf_op jit(solution)/shard_map/all_to_all | solution.py:38
  212.4 3.3 %all-to-all-done.8 = bf16[4,32,256]{2,1,0:T(8,128)(2,1)S(1)} async-done(((bf16[4,32,256]{2,1,0:T(8,128)(2,1)}), bf16[4,32,256]{2,1,0:T(8,128)(2,1)S(1)}, u32[]{:S(2)}, u32[]{:S(2)}) %all-to-all-start.8) | async-done | bytes 65568 | tf_op jit(solution)/shard_map/all_to_all | solution.py:38
  (45 shorter events, 19.6 us)
Async XLA Ops:
  0.6 0.8 copy-start.5
  2.2 16.3 %all-to-all-start = ((bf16[4,32,384]{2,1,0:T(8,128)(2,1)}), bf16[4,32,384]{2,1,0:T(8,128)(2,1)S(1)}, u32[]{:S(2)}, u32[]{:S(2)}) async-start(bf16[4,32,384]{2,1,0:T(8,128)(2,1)} %maximum_select_fusion), calls=%async_computation | async-start | bytes 196608 | tf_op jit(solution)/shard_map/all_to_all | solution.py:38
  12.4 0.7 copy-start.1
  12.4 0.7 copy-start.2
  13.0 1.2 copy-start
  15.2 26.6 %collective-permute-start = (bf16[512,1024]{1,0:T(8,128)(2,1)S(1)}, bf16[512,1024]{1,0:T(8,128)(2,1)S(1)}, u32[]{:S(2)}, u32[]{:S(2)}) collective-permute-start(bf16[512,1024]{1,0:T(8,128)(2,1)S(1)} %dense_panel.1.refs_2_), channel_id=1, source_target_pairs={{0,1},{1,0},{2,3},{3,2},{4,5},{5,4},{6,7},{7,6},{8,9},{9,8},{10,11... | collective-permute-start | bytes 3145736 | tf_op jit(solution)/shard_map/ppermute | solution.py:42
  19.8 22.0 %all-to-all-start.1 = ((bf16[16,128,256]{2,1,0:T(8,128)(2,1)}), bf16[16,128,256]{2,1,0:T(8,128)(2,1)}, u32[]{:S(2)}, u32[]{:S(2)}) async-start(bf16[16,128,256]{2,1,0:T(8,128)(2,1)} %broadcast_in_dim.14), calls=%async_computation.1 | async-start | bytes 2097152 | tf_op jit(solution)/shard_map/all_to_all | solution.py:38
  24.2 21.4 %collective-permute-start.1 = (bf16[512,1024]{1,0:T(8,128)(2,1)S(1)}, bf16[512,1024]{1,0:T(8,128)(2,1)S(1)}, u32[]{:S(2)}, u32[]{:S(2)}) collective-permute-start(bf16[512,1024]{1,0:T(8,128)(2,1)S(1)} %dense_panel.1.refs_2_), channel_id=1, source_target_pairs={{0,16},{16,0},{1,17},{17,1},{2,18},{18,2},{3,19},{19,3},{4,20},{20... | collective-permute-start | bytes 3145736 | tf_op jit(solution)/shard_map/ppermute | solution.py:42
  41.9 5.4 %collective-permute-start.2 = (bf16[512,1024]{1,0:T(8,128)(2,1)S(1)}, bf16[512,1024]{1,0:T(8,128)(2,1)}, u32[]{:S(2)}, u32[]{:S(2)}) collective-permute-start(bf16[512,1024]{1,0:T(8,128)(2,1)S(1)} %collective-permute-done.refs_3_), channel_id=1, source_target_pairs={{0,16},{16,0},{1,17},{17,1},{2,18},{18,2},{3,19},{19,3},{4,20},{20... | collective-permute-start | bytes 3145736 | tf_op jit(solution)/shard_map/ppermute | solution.py:42
  49.6 14.0 %collective-permute-start.3 = (bf16[4,2,2,32,256]{4,3,2,1,0:T(8,128)(2,1)S(1)}, bf16[4,2,2,32,256]{4,3,2,1,0:T(8,128)(2,1)S(1)}, u32[]{:S(2)}, u32[]{:S(2)}) collective-permute-start(bf16[4,2,2,32,256]{4,3,2,1,0:T(8,128)(2,1)S(1)} %go_product.3), channel_id=1, source_target_pairs={{0,15},{1,2},{2,1},{3,4},{4,3},{5,6},{6,5},{7,8},{8,7},{9,10},{10,... | collective-permute-start | bytes 786440 | tf_op jit(solution)/shard_map/ppermute | solution.py:42
  111.8 8.3 %collective-permute-start.4 = (bf16[4,2,2,32,256]{4,3,2,1,0:T(8,128)(2,1)S(1)}, bf16[4,2,2,32,256]{4,3,2,1,0:T(8,128)(2,1)S(1)}, u32[]{:S(2)}, u32[]{:S(2)}) collective-permute-start(bf16[4,2,2,32,256]{4,3,2,1,0:T(8,128)(2,1)S(1)} %go_product.4), channel_id=1, source_target_pairs={{0,15},{1,2},{2,1},{3,4},{4,3},{5,6},{6,5},{7,8},{8,7},{9,10},{10,... | collective-permute-start | bytes 786440 | tf_op jit(solution)/shard_map/ppermute | solution.py:42
  139.4 5.4 %copy-start.3 = (bf16[128,256]{1,0:T(8,128)(2,1)}, bf16[128,256]{1,0:T(8,128)(2,1)S(1)}, u32[]{:S(2)}) copy-start(bf16[128,256]{1,0:T(8,128)(2,1)S(1)} %get-tuple-element.14) | copy-start | bytes 196612
  140.5 16.6 %all-to-all-start.5 = ((bf16[16,128,256]{2,1,0:T(8,128)(2,1)}), bf16[16,128,256]{2,1,0:T(8,128)(2,1)}, u32[]{:S(2)}, u32[]{:S(2)}) async-start(bf16[16,128,256]{2,1,0:T(8,128)(2,1)} %broadcast_in_dim.16), calls=%async_computation.5 | async-start | bytes 2097152 | tf_op jit(solution)/shard_map/all_to_all | solution.py:38
  160.1 14.8 %all-to-all-start.6 = ((bf16[4,2,32,256]{3,2,1,0:T(8,128)(2,1)}), bf16[4,2,32,256]{3,2,1,0:T(8,128)(2,1)S(1)}, u32[]{:S(2)}, u32[]{:S(2)}) async-start(bf16[4,2,32,256]{3,2,1,0:T(8,128)(2,1)} %pad_maximum_fusion), calls=%async_computation.6 | async-start | bytes 262144 | tf_op jit(solution)/shard_map/all_to_all | solution.py:38
  169.2 11.3 %collective-permute-start.5 = (bf16[4,2,2,32,256]{4,3,2,1,0:T(8,128)(2,1)}, bf16[4,2,2,32,256]{4,3,2,1,0:T(8,128)(2,1)}, u32[]{:S(2)}, u32[]{:S(2)}) collective-permute-start(bf16[4,2,2,32,256]{4,3,2,1,0:T(8,128)(2,1)} %go_product.5), channel_id=1, source_target_pairs={{0,15},{1,2},{2,1},{3,4},{4,3},{5,6},{6,5},{7,8},{8,7},{9,10},{10,... | collective-permute-start | bytes 786440 | tf_op jit(solution)/shard_map/ppermute | solution.py:42
  205.4 0.8 copy-start.4
  207.0 8.7 %all-to-all-start.8 = ((bf16[4,32,256]{2,1,0:T(8,128)(2,1)}), bf16[4,32,256]{2,1,0:T(8,128)(2,1)S(1)}, u32[]{:S(2)}, u32[]{:S(2)}) async-start(bf16[4,32,256]{2,1,0:T(8,128)(2,1)} %bitcast.21), calls=%async_computation.8 | async-start | bytes 131072 | tf_op jit(solution)/shard_map/all_to_all | solution.py:38

commit v9 on v7

--- a/solution.py
+++ b/solution.py
@@ -15,16 +15,26 @@
     [core * LENGTH + 2 * k + level for level in range(2) for core in range(2)] for k in range(TILES)
 ]
 NEIGHBOURS = [(z, (z + 1 if z % 2 else z - 1) % LENGTH) for z in range(LENGTH)]
+SIDES = ((0, 0, 1, 1), (0, 1, 1, 0))
 SUM_GROUPS = [
-    [(STEP * k + first + side) % LENGTH for k in range(STEP)]
+    [core * LENGTH + (STEP * k + first + (side ^ SIDES[core][k])) % LENGTH for k in range(STEP)]
+    for core in range(2)
     for first in (1, 3)
     for side in range(2)
 ]
 
 
 def tile_order():
-    group_of = {z: group for group in SUM_GROUPS for z in group}
-    return [[z // 2 for z in group_of[me] + group_of[other]] for me, other in NEIGHBOURS]
+    group_of = {device: group for group in SUM_GROUPS for device in group}
+    return [
+        [
+            device % LENGTH // 2
+            for z in (me, other)
+            for device in group_of[core * LENGTH + z]
+        ]
+        for core in range(2)
+        for me, other in NEIGHBOURS
+    ]
 
 
 LANES = 128
@@ -135,7 +145,7 @@
     plane = SIZES["x"] * SIZES["y"]
     z = lax.axis_index("z")
     here = jnp.stack([lax.axis_index("c"), z & 1]).astype(jnp.int32)
-    place = jnp.concatenate([here, jnp.asarray(tile_order(), jnp.int32)[z]])
+    place = jnp.concatenate([here, jnp.asarray(tile_order(), jnp.int32)[lax.axis_index("c") * LENGTH + z]])
     crossed = (z & 2) != 0
 
     counts = jnp.broadcast_to(degree.astype(bf16)[:, None], (rows, LANES))
@@ -168,7 +178,7 @@
         come = swap(product(STEP, place, whole, panels), "z", NEIGHBOURS)
         stay = product(0, place, whole, panels)
         both = (stay.astype(f32) + come.astype(f32)).astype(bf16)
-        parts = exchange(both.reshape(STEP, pooled, width), "z", SUM_GROUPS)
+        parts = exchange(both.reshape(STEP, pooled, width), ("c", "z"), SUM_GROUPS)
         total = jnp.sum(parts.astype(f32), axis=0)
         value = (scale * (total + sent.astype(f32))).astype(bf16)
         sent = (scale * value.astype(f32)).astype(bf16)

time: 203 us -> 203 us (level)
  starting transfers between devices: 44.7 us -> 57.2 us
  blocking collectives: 99.8 us -> 92.6 us
  waiting for transfers between devices: 34.3 us -> 28.7 us
    ppermute x6, starting transfers between devices: 22.1 us -> 33.9 us  [swap(): return lax.ppermute(x, axis, pairs)]
    all_to_all x5, blocking collectives: 99.8 us -> 92.6 us  [exchange(): return lax.all_to_all(x, axes, 0, 0, tiled=True, axis_index_groups=groups)]
    ppermute x6, waiting for transfers between devices: 29.8 us -> 24.2 us  [swap(): return lax.ppermute(x, axis, pairs)]
where the time goes in v9:
time: 203 us; the launch traced here: 201 us
  blocking collectives  92.6 us (46%)
  starting transfers between devices  57.2 us (28%)
  waiting for transfers between devices  28.7 us (14%)
  Pallas kernels  14.4 us (7%)
  local copies, waits for them, and re-layouts  5.45 us (3%)
  other arithmetic  2.21 us (1%)
    all_to_all x5, blocking collectives, exchange(): return lax.all_to_all(x, axes, 0, 0, tiled=True, axis_index_groups=groups)  92.6 us
    ppermute x6, starting transfers between devices, swap(): return lax.ppermute(x, axis, pairs)  33.9 us
    ppermute x6, waiting for transfers between devices, swap(): return lax.ppermute(x, axis, pairs)  24.2 us
    all_to_all x3, starting transfers between devices, exchange(): return lax.all_to_all(x, axes, 0, 0, tiled=True, axis_index_groups=groups)  23.3 us
    pallas_call x6, Pallas kernels, product(): pl.pallas_call(body, out_shape=jax.ShapeDtypeStruct((STEP, pair, 2, rows...  12.7 us
    all_to_all x3, waiting for transfers between devices, exchange(): return lax.all_to_all(x, axes, 0, 0, tiled=True, axis_index_groups=groups)  4.47 us
  transfers between devices with their start and end apart: 9, of which 6 were waited for; matrix products, arithmetic and copies ran while one was open for 1% of the time, Pallas kernels for 4%

profile of v9, /device:TPU:1, one launch (start us, length us, event | category | flops | bytes accessed | tf_op | source)
XLA Modules:
  0.0 201.4 jit_solution(18295842463222672200)
XLA Ops:
  2.8 10.1 %all-to-all-start = ((bf16[4,32,384]{2,1,0:T(8,128)(2,1)}), bf16[4,32,384]{2,1,0:T(8,128)(2,1)S(1)}, u32[]{:S(2)}, u32[]{:S(2)}) async-start(bf16[4,32,384]{2,1,0:T(8,128)(2,1)} %maximum_select_fusion), calls=%async_computation | async-start | bytes 196608 | tf_op jit(solution)/shard_map/all_to_all | solution.py:48
  15.9 3.3 %collective-permute-start = (bf16[512,1024]{1,0:T(8,128)(2,1)S(1)}, bf16[512,1024]{1,0:T(8,128)(2,1)S(1)}, u32[]{:S(2)}, u32[]{:S(2)}) collective-permute-start(bf16[512,1024]{1,0:T(8,128)(2,1)S(1)} %dense_panel.1.refs_2_), channel_id=1, source_target_pairs={{0,1},{1,0},{2,3},{3,2},{4,5},{5,4},{6,7},{7,6},{8,9},{9,8},{10,11... | collective-permute-start | bytes 3145736 | tf_op jit(solution)/shard_map/ppermute | solution.py:52
  20.5 4.3 %all-to-all-start.1 = ((bf16[16,128,256]{2,1,0:T(8,128)(2,1)}), bf16[16,128,256]{2,1,0:T(8,128)(2,1)}, u32[]{:S(2)}, u32[]{:S(2)}) async-start(bf16[16,128,256]{2,1,0:T(8,128)(2,1)} %broadcast_in_dim.12), calls=%async_computation.1 | async-start | bytes 2097152 | tf_op jit(solution)/shard_map/all_to_all | solution.py:48
  24.8 2.5 %collective-permute-start.1 = (bf16[512,1024]{1,0:T(8,128)(2,1)S(1)}, bf16[512,1024]{1,0:T(8,128)(2,1)S(1)}, u32[]{:S(2)}, u32[]{:S(2)}) collective-permute-start(bf16[512,1024]{1,0:T(8,128)(2,1)S(1)} %dense_panel.1.refs_2_), channel_id=1, source_target_pairs={{0,16},{16,0},{1,17},{17,1},{2,18},{18,2},{3,19},{19,3},{4,20},{20... | collective-permute-start | bytes 3145736 | tf_op jit(solution)/shard_map/ppermute | solution.py:52
  27.4 15.1 %collective-permute-done.refs_3_ = bf16[512,1024]{1,0:T(8,128)(2,1)S(1)} collective-permute-done((bf16[512,1024]{1,0:T(8,128)(2,1)S(1)}, bf16[512,1024]{1,0:T(8,128)(2,1)S(1)}, u32[]{:S(2)}, u32[]{:S(2)}) %collective-permute-start) | collective-permute-done | bytes 1048608 | tf_op jit(solution)/shard_map/ppermute | solution.py:52
  42.5 3.0 %collective-permute-start.2 = (bf16[512,1024]{1,0:T(8,128)(2,1)S(1)}, bf16[512,1024]{1,0:T(8,128)(2,1)}, u32[]{:S(2)}, u32[]{:S(2)}) collective-permute-start(bf16[512,1024]{1,0:T(8,128)(2,1)S(1)} %collective-permute-done.refs_3_), channel_id=1, source_target_pairs={{0,16},{16,0},{1,17},{17,1},{2,18},{18,2},{3,19},{19,3},{4,20},{20... | collective-permute-start | bytes 3145736 | tf_op jit(solution)/shard_map/ppermute | solution.py:52
  47.9 2.3 %go_product.3 = bf16[4,2,2,32,256]{4,3,2,1,0:T(8,128)(2,1)S(1)} custom-call(s32[10]{0:T(128)S(1)} %pad_add_fusion.refs_0_, bf16[16,2,64,256]{3,2,1,0:T(8,128)(2,1)} %bitcast.10.refs_1_, bf16[512,1024]{1,0:T(8,128)(2,1)S(1)} %dense_panel.1.refs_2_, bf16[512,1024]{1,0:T(8,128)(2,1)S(1)} %collective-permute-done.refs_3_, ...), custom_call_target="tpu_custom_call" | custom-call | tf_op jit(solution)/shard_map/go_product/pallas_call | solution.py:110
  50.2 7.6 %collective-permute-start.3 = (bf16[4,2,2,32,256]{4,3,2,1,0:T(8,128)(2,1)S(1)}, bf16[4,2,2,32,256]{4,3,2,1,0:T(8,128)(2,1)S(1)}, u32[]{:S(2)}, u32[]{:S(2)}) collective-permute-start(bf16[4,2,2,32,256]{4,3,2,1,0:T(8,128)(2,1)S(1)} %go_product.3), channel_id=1, source_target_pairs={{0,15},{1,2},{2,1},{3,4},{4,3},{5,6},{6,5},{7,8},{8,7},{9,10},{10,... | collective-permute-start | bytes 786440 | tf_op jit(solution)/shard_map/ppermute | solution.py:52
  57.8 2.3 %stay_product.3 = bf16[4,2,2,32,256]{4,3,2,1,0:T(8,128)(2,1)S(1)} custom-call(s32[10]{0:T(128)S(1)} %pad_add_fusion.refs_0_, bf16[16,2,64,256]{3,2,1,0:T(8,128)(2,1)} %bitcast.10.refs_1_, bf16[512,1024]{1,0:T(8,128)(2,1)S(1)} %dense_panel.1.refs_2_, bf16[512,1024]{1,0:T(8,128)(2,1)S(1)} %collective-permute-done.refs_3_, ...), custom_call_target="tpu_custom_call" | custom-call | tf_op jit(solution)/shard_map/stay_product/pallas_call | solution.py:110
  60.2 4.0 %collective-permute-done.3 = bf16[4,2,2,32,256]{4,3,2,1,0:T(8,128)(2,1)S(1)} collective-permute-done((bf16[4,2,2,32,256]{4,3,2,1,0:T(8,128)(2,1)S(1)}, bf16[4,2,2,32,256]{4,3,2,1,0:T(8,128)(2,1)S(1)}, u32[]{:S(2)}, u32[]{:S(2)}) %collective-permute-start.3) | collective-permute-done | bytes 262176 | tf_op jit(solution)/shard_map/ppermute | solution.py:52
  64.3 16.7 %all_to_all.40 = bf16[4,128,256]{2,1,0:T(8,128)(2,1)S(1)} all-to-all(bf16[4,128,256]{2,1,0:T(8,128)(2,1)S(1)} %bitcast.34), channel_id=1, replica_groups={{1,5,10,14},{2,6,9,13},{3,7,12,0},{4,8,11,15},{17,22,26,29},{18,21,25,3..., dimensions={0} | all-to-all | bytes 524288 | tf_op jit(solution)/shard_map/all_to_all | solution.py:48
  81.2 26.9 %all_to_all.41 = bf16[16,128,256]{2,1,0:T(8,128)(2,1)S(1)} all-to-all(bf16[16,128,256]{2,1,0:T(8,128)(2,1)S(1)} %broadcast_in_dim.13), channel_id=1, replica_groups=mesh['x'=4,'y'=4,'c'=2,'z'=16] {'x','y'}, dimensions={0} | all-to-all | bytes 2097152 | tf_op jit(solution)/shard_map/all_to_all | solution.py:48
  108.1 2.0 %go_product.4 = bf16[4,2,2,32,256]{4,3,2,1,0:T(8,128)(2,1)S(1)} custom-call(s32[10]{0:T(128)S(1)} %pad_add_fusion.refs_0_, bf16[16,2,64,256]{3,2,1,0:T(8,128)(2,1)S(1)} %bitcast.29, bf16[512,1024]{1,0:T(8,128)(2,1)S(1)} %dense_panel.1.refs_2_, bf16[512,1024]{1,0:T(8,128)(2,1)S(1)} %collective-permute-done.refs_3_, ...), custom_call_target="tpu_custom_call" | custom-call | tf_op jit(solution)/shard_map/go_product/pallas_call | solution.py:110
  110.1 4.8 %collective-permute-start.4 = (bf16[4,2,2,32,256]{4,3,2,1,0:T(8,128)(2,1)S(1)}, bf16[4,2,2,32,256]{4,3,2,1,0:T(8,128)(2,1)S(1)}, u32[]{:S(2)}, u32[]{:S(2)}) collective-permute-start(bf16[4,2,2,32,256]{4,3,2,1,0:T(8,128)(2,1)S(1)} %go_product.4), channel_id=1, source_target_pairs={{0,15},{1,2},{2,1},{3,4},{4,3},{5,6},{6,5},{7,8},{8,7},{9,10},{10,... | collective-permute-start | bytes 786440 | tf_op jit(solution)/shard_map/ppermute | solution.py:52
  115.0 2.0 %stay_product.4 = bf16[4,2,2,32,256]{4,3,2,1,0:T(8,128)(2,1)S(1)} custom-call(s32[10]{0:T(128)S(1)} %pad_add_fusion.refs_0_, bf16[16,2,64,256]{3,2,1,0:T(8,128)(2,1)S(1)} %bitcast.30, bf16[512,1024]{1,0:T(8,128)(2,1)S(1)} %dense_panel.1.refs_2_, bf16[512,1024]{1,0:T(8,128)(2,1)S(1)} %collective-permute-done.refs_3_, ...), custom_call_target="tpu_custom_call" | custom-call | tf_op jit(solution)/shard_map/stay_product/pallas_call | solution.py:110
  118.8 17.5 %all_to_all.42 = bf16[4,128,256]{2,1,0:T(8,128)(2,1)S(1)} all-to-all(bf16[4,128,256]{2,1,0:T(8,128)(2,1)S(1)} %bitcast.35), channel_id=1, replica_groups={{1,5,10,14},{2,6,9,13},{3,7,12,0},{4,8,11,15},{17,22,26,29},{18,21,25,3..., dimensions={0} | all-to-all | bytes 524288 | tf_op jit(solution)/shard_map/all_to_all | solution.py:48
  136.5 15.7 %all_to_all.43 = bf16[16,128,256]{2,1,0:T(8,128)(2,1)S(1)} all-to-all(bf16[16,128,256]{2,1,0:T(8,128)(2,1)S(1)} %broadcast_in_dim.14), channel_id=1, replica_groups=mesh['x'=4,'y'=4,'c'=2,'z'=16] {'x','y'}, dimensions={0} | all-to-all | bytes 2097152 | tf_op jit(solution)/shard_map/all_to_all | solution.py:48
  152.2 2.0 %go_product.5 = bf16[4,2,2,32,256]{4,3,2,1,0:T(8,128)(2,1)S(1)} custom-call(s32[10]{0:T(128)S(1)} %pad_add_fusion.refs_0_, bf16[16,2,64,256]{3,2,1,0:T(8,128)(2,1)S(1)} %bitcast.27, bf16[512,1024]{1,0:T(8,128)(2,1)S(1)} %dense_panel.1.refs_2_, bf16[512,1024]{1,0:T(8,128)(2,1)S(1)} %collective-permute-done.refs_3_, ...), custom_call_target="tpu_custom_call" | custom-call | tf_op jit(solution)/shard_map/go_product/pallas_call | solution.py:110
  154.3 12.7 %collective-permute-start.5 = (bf16[4,2,2,32,256]{4,3,2,1,0:T(8,128)(2,1)S(1)}, bf16[4,2,2,32,256]{4,3,2,1,0:T(8,128)(2,1)S(1)}, u32[]{:S(2)}, u32[]{:S(2)}) collective-permute-start(bf16[4,2,2,32,256]{4,3,2,1,0:T(8,128)(2,1)S(1)} %go_product.5), channel_id=1, source_target_pairs={{0,15},{1,2},{2,1},{3,4},{4,3},{5,6},{6,5},{7,8},{8,7},{9,10},{10,... | collective-permute-start | bytes 786440 | tf_op jit(solution)/shard_map/ppermute | solution.py:52
  167.0 2.0 %stay_product.5 = bf16[4,2,2,32,256]{4,3,2,1,0:T(8,128)(2,1)S(1)} custom-call(s32[10]{0:T(128)S(1)} %pad_add_fusion.refs_0_, bf16[16,2,64,256]{3,2,1,0:T(8,128)(2,1)S(1)} %bitcast.28, bf16[512,1024]{1,0:T(8,128)(2,1)S(1)} %dense_panel.1.refs_2_, bf16[512,1024]{1,0:T(8,128)(2,1)S(1)} %collective-permute-done.refs_3_, ...), custom_call_target="tpu_custom_call" | custom-call | tf_op jit(solution)/shard_map/stay_product/pallas_call | solution.py:110
  169.0 1.7 collective-permute-done.5
  170.8 15.8 %all_to_all.44 = bf16[4,128,256]{2,1,0:T(8,128)(2,1)S(1)} all-to-all(bf16[4,128,256]{2,1,0:T(8,128)(2,1)S(1)} %bitcast.36), channel_id=1, replica_groups={{1,5,10,14},{2,6,9,13},{3,7,12,0},{4,8,11,15},{17,22,26,29},{18,21,25,3..., dimensions={0} | all-to-all | bytes 524288 | tf_op jit(solution)/shard_map/all_to_all | solution.py:48
  187.5 8.8 %all-to-all-start.7 = ((bf16[4,3,32,256]{3,2,1,0:T(8,128)(2,1)}), bf16[4,3,32,256]{3,2,1,0:T(8,128)(2,1)S(1)}, u32[]{:S(2)}, u32[]{:S(2)}) async-start(bf16[4,3,32,256]{3,2,1,0:T(8,128)(2,1)} %pad_maximum_fusion), calls=%async_computation.7 | async-start | bytes 393216 | tf_op jit(solution)/shard_map/all_to_all | solution.py:48
  196.3 4.5 %all-to-all-done.7.back = bf16[4,3,32,256]{3,2,1,0:T(8,128)(2,1)S(1)} async-done(((bf16[4,3,32,256]{3,2,1,0:T(8,128)(2,1)}), bf16[4,3,32,256]{3,2,1,0:T(8,128)(2,1)S(1)}, u32[]{:S(2)}, u32[]{:S(2)}) %all-to-all-start.7) | async-done | bytes 196640 | tf_op jit(solution)/shard_map/all_to_all | solution.py:48
  (38 shorter events, 12.6 us)
Async XLA Ops:
  0.6 0.7 copy-start.3
  2.8 16.4 %all-to-all-start = ((bf16[4,32,384]{2,1,0:T(8,128)(2,1)}), bf16[4,32,384]{2,1,0:T(8,128)(2,1)S(1)}, u32[]{:S(2)}, u32[]{:S(2)}) async-start(bf16[4,32,384]{2,1,0:T(8,128)(2,1)} %maximum_select_fusion), calls=%async_computation | async-start | bytes 196608 | tf_op jit(solution)/shard_map/all_to_all | solution.py:48
  13.0 0.7 copy-start.1
  13.0 0.7 copy-start.2
  13.7 1.2 copy-start
  15.9 26.7 %collective-permute-start = (bf16[512,1024]{1,0:T(8,128)(2,1)S(1)}, bf16[512,1024]{1,0:T(8,128)(2,1)S(1)}, u32[]{:S(2)}, u32[]{:S(2)}) collective-permute-start(bf16[512,1024]{1,0:T(8,128)(2,1)S(1)} %dense_panel.1.refs_2_), channel_id=1, source_target_pairs={{0,1},{1,0},{2,3},{3,2},{4,5},{5,4},{6,7},{7,6},{8,9},{9,8},{10,11... | collective-permute-start | bytes 3145736 | tf_op jit(solution)/shard_map/ppermute | solution.py:52
  20.5 22.0 %all-to-all-start.1 = ((bf16[16,128,256]{2,1,0:T(8,128)(2,1)}), bf16[16,128,256]{2,1,0:T(8,128)(2,1)}, u32[]{:S(2)}, u32[]{:S(2)}) async-start(bf16[16,128,256]{2,1,0:T(8,128)(2,1)} %broadcast_in_dim.12), calls=%async_computation.1 | async-start | bytes 2097152 | tf_op jit(solution)/shard_map/all_to_all | solution.py:48
  24.8 21.4 %collective-permute-start.1 = (bf16[512,1024]{1,0:T(8,128)(2,1)S(1)}, bf16[512,1024]{1,0:T(8,128)(2,1)S(1)}, u32[]{:S(2)}, u32[]{:S(2)}) collective-permute-start(bf16[512,1024]{1,0:T(8,128)(2,1)S(1)} %dense_panel.1.refs_2_), channel_id=1, source_target_pairs={{0,16},{16,0},{1,17},{17,1},{2,18},{18,2},{3,19},{19,3},{4,20},{20... | collective-permute-start | bytes 3145736 | tf_op jit(solution)/shard_map/ppermute | solution.py:52
  42.5 5.4 %collective-permute-start.2 = (bf16[512,1024]{1,0:T(8,128)(2,1)S(1)}, bf16[512,1024]{1,0:T(8,128)(2,1)}, u32[]{:S(2)}, u32[]{:S(2)}) collective-permute-start(bf16[512,1024]{1,0:T(8,128)(2,1)S(1)} %collective-permute-done.refs_3_), channel_id=1, source_target_pairs={{0,16},{16,0},{1,17},{17,1},{2,18},{18,2},{3,19},{19,3},{4,20},{20... | collective-permute-start | bytes 3145736 | tf_op jit(solution)/shard_map/ppermute | solution.py:52
  50.2 13.9 %collective-permute-start.3 = (bf16[4,2,2,32,256]{4,3,2,1,0:T(8,128)(2,1)S(1)}, bf16[4,2,2,32,256]{4,3,2,1,0:T(8,128)(2,1)S(1)}, u32[]{:S(2)}, u32[]{:S(2)}) collective-permute-start(bf16[4,2,2,32,256]{4,3,2,1,0:T(8,128)(2,1)S(1)} %go_product.3), channel_id=1, source_target_pairs={{0,15},{1,2},{2,1},{3,4},{4,3},{5,6},{6,5},{7,8},{8,7},{9,10},{10,... | collective-permute-start | bytes 786440 | tf_op jit(solution)/shard_map/ppermute | solution.py:52
  110.1 8.6 %collective-permute-start.4 = (bf16[4,2,2,32,256]{4,3,2,1,0:T(8,128)(2,1)S(1)}, bf16[4,2,2,32,256]{4,3,2,1,0:T(8,128)(2,1)S(1)}, u32[]{:S(2)}, u32[]{:S(2)}) collective-permute-start(bf16[4,2,2,32,256]{4,3,2,1,0:T(8,128)(2,1)S(1)} %go_product.4), channel_id=1, source_target_pairs={{0,15},{1,2},{2,1},{3,4},{4,3},{5,6},{6,5},{7,8},{8,7},{9,10},{10,... | collective-permute-start | bytes 786440 | tf_op jit(solution)/shard_map/ppermute | solution.py:52
  154.3 16.5 %collective-permute-start.5 = (bf16[4,2,2,32,256]{4,3,2,1,0:T(8,128)(2,1)S(1)}, bf16[4,2,2,32,256]{4,3,2,1,0:T(8,128)(2,1)S(1)}, u32[]{:S(2)}, u32[]{:S(2)}) collective-permute-start(bf16[4,2,2,32,256]{4,3,2,1,0:T(8,128)(2,1)S(1)} %go_product.5), channel_id=1, source_target_pairs={{0,15},{1,2},{2,1},{3,4},{4,3},{5,6},{6,5},{7,8},{8,7},{9,10},{10,... | collective-permute-start | bytes 786440 | tf_op jit(solution)/shard_map/ppermute | solution.py:52
  187.5 13.3 %all-to-all-start.7 = ((bf16[4,3,32,256]{3,2,1,0:T(8,128)(2,1)}), bf16[4,3,32,256]{3,2,1,0:T(8,128)(2,1)S(1)}, u32[]{:S(2)}, u32[]{:S(2)}) async-start(bf16[4,3,32,256]{3,2,1,0:T(8,128)(2,1)} %pad_maximum_fusion), calls=%async_computation.7 | async-start | bytes 393216 | tf_op jit(solution)/shard_map/all_to_all | solution.py:48
